TPU v7x, 256 devices: a whole 4x4x8 slice. The times are simulated.
256 devices in a mesh: ctx: 32 (over y, x, core), tp: 8 (over z).
Axes of the slice: x: 4, y: 4, z: 8, core: 2. Of those that a mesh axis runs over, the one named last changes fastest.
Arguments:
- hyena_gate: bfloat16 [4096, 4096], P('ctx', 'tp'), may hold values from -6 to 6
- hyena_key: bfloat16 [4096, 4096], P('ctx', 'tp'), may hold values from -6 to 6
- hyena_value: bfloat16 [4096, 4096], P('ctx', 'tp'), may hold values from -6 to 6
- filter_taps: bfloat16 [4096, 4096], P(None, 'tp'), may hold values from -0.25 to 0.25
- skip_weight: float32 [4096], P('tp'), may hold values from -4 to 4
- queries: bfloat16 [4096, 4096], P('ctx', 'tp'), may hold values from -100 to 100
- attn_keys: bfloat16 [4096, 4096], P('ctx', 'tp'), may hold values from -4.5 to 4.5
- valid_length: int32 [1], replicated, may hold values from 3585 to 4096
Outputs:
- hyena_out: bfloat16 [4096, 4096], P('ctx', 'tp')
- attn_out: bfloat16 [4096, 4096], P('ctx', 'tp')
All inputs are finite; a program needn't handle non-finite values.
Results may differ from a plain program's by a relative error of at most 0.015.
Values may be sent and summed in bfloat16 or wider, within the bound.
No kernel may reach another device: no remote copies, remote signals or barrier semaphores. Data moves between devices by JAX's collectives and lax.ppermute only.
A program may use at most 64 MiB of HBM per device.

v0:
```python
import math

import jax
import jax.numpy as jnp
from jax import lax
from jax.sharding import PartitionSpec as P

HD = 128
DW = 4096


def tables(group_rows):
    doubled = 2 * group_rows
    freq = jnp.arange(doubled, dtype=jnp.int32)[:, None]
    place = jnp.arange(group_rows, dtype=jnp.int32)[None, :]
    phase = (freq * place % doubled).astype(jnp.float32) * (2.0 * math.pi / doubled)
    parity = (1 - 2 * (jnp.arange(doubled, dtype=jnp.int32) % 2)).astype(jnp.float32)[:, None]
    cosine = jnp.cos(phase)
    sine = jnp.sin(phase)
    cos_high = cosine.astype(jnp.bfloat16)
    cos_low = (cosine - cos_high.astype(jnp.float32)).astype(jnp.bfloat16)
    sin_high = sine.astype(jnp.bfloat16)
    sin_low = (sine - sin_high.astype(jnp.float32)).astype(jnp.bfloat16)
    return ((cos_high, cos_low, sin_high, sin_low, cosine, sine), parity)


def split_dot(high, low, block):
    return jnp.dot(high, block, preferred_element_type=jnp.float32) + jnp.dot(
        low, block, preferred_element_type=jnp.float32
    )


def forward(tabs, block):
    return (split_dot(tabs[0], tabs[1], block), -split_dot(tabs[2], tabs[3], block))


def inverse(tabs, real_part, imag_part):
    cosine, sine = (tabs[4], tabs[5])
    scale = 1.0 / cosine.shape[0]
    first = jnp.dot(
        cosine.T, real_part, precision=lax.Precision.HIGH, preferred_element_type=jnp.float32
    )
    second = jnp.dot(
        sine.T, imag_part, precision=lax.Precision.HIGH, preferred_element_type=jnp.float32
    )
    return (first - second) * scale


def complex_mul(left_real, left_imag, right_real, right_imag):
    return (
        left_real * right_real - left_imag * right_imag,
        left_real * right_imag + left_imag * right_real,
    )


def taps_spectrum(filter_taps, lag, tabs):
    group_rows = tabs[0].shape[1]
    blocks = filter_taps.shape[0] // group_rows
    first = jnp.clip(lag, 0, blocks - 1) * group_rows
    block = lax.dynamic_slice_in_dim(filter_taps, first, group_rows, 0)
    keep = (lag >= 0).astype(jnp.float32)
    real_part, imag_part = forward(tabs, block)
    return (real_part * keep, imag_part * keep)


def shards(
    hyena_gate, hyena_key, hyena_value, filter_taps, skip_weight, queries, attn_keys, valid_length
):
    group_rows = hyena_gate.shape[0]
    own_index = lax.axis_index("ctx")
    tabs, parity = tables(group_rows)
    mixed = (hyena_key.astype(jnp.float32) * hyena_value.astype(jnp.float32)).astype(jnp.bfloat16)
    mixed_float = mixed.astype(jnp.float32)
    input_real, input_imag = forward(tabs, mixed)
    base = jnp.int32(0) // group_rows - own_index
    first_prior = taps_spectrum(filter_taps, base - 1, tabs)

    def one_block(prior, offset):
        lag = base + offset
        this_real, this_imag = taps_spectrum(filter_taps, lag, tabs)
        lag_real = this_real + parity * prior[0]
        lag_imag = this_imag + parity * prior[1]
        out_real, out_imag = complex_mul(lag_real, lag_imag, input_real, input_imag)
        result = inverse(tabs, out_real, out_imag)
        return ((this_real, this_imag), jnp.where(lag >= 0, result, 0.0))

    last, blocks = lax.scan(
        one_block,
        first_prior,
        jnp.arange(lax.axis_size("ctx") * group_rows // group_rows, dtype=jnp.int32),
    )
    convolved = lax.psum_scatter(
        blocks.reshape(lax.axis_size("ctx") * group_rows, blocks.shape[2]).astype(jnp.bfloat16),
        "ctx",
        scatter_dimension=0,
        tiled=True,
    ).astype(jnp.float32)
    positions = own_index * group_rows + jnp.arange(group_rows, dtype=jnp.int32)
    valid_rows = (positions < valid_length[0])[:, None]
    gated = hyena_gate.astype(jnp.float32) * (convolved + skip_weight[None, :] * mixed_float)
    hyena_out = jnp.where(valid_rows, gated, 0.0).astype(jnp.bfloat16)
    heads_here = queries.shape[1] // HD
    scale = 1.0 / math.sqrt(HD)
    query_heads = queries.reshape(group_rows, heads_here, HD)
    start_max = jnp.full((heads_here, group_rows), -1e30, jnp.float32)
    key_piece = lax.all_gather(attn_keys, "ctx", axis=0, tiled=True)
    value_piece = lax.all_gather(hyena_out, "ctx", axis=0, tiled=True)
    width = key_piece.shape[0]
    key_heads = key_piece.reshape(width, heads_here, HD)
    value_heads = value_piece.reshape(width, heads_here, HD)
    scores = (
        jnp.einsum("qhd,khd->hqk", query_heads, key_heads, preferred_element_type=jnp.float32)
        * scale
    )
    key_places = jnp.arange(width, dtype=jnp.int32)
    allowed = (key_places[None, :] <= positions[:, None]) & (key_places < valid_length[0])[None, :]
    scores = jnp.where(allowed[None], scores, -1e30)
    new_max = jnp.maximum(start_max, jnp.max(scores, axis=2))
    weights = jnp.where(allowed[None], jnp.exp(scores - new_max[:, :, None]), 0.0)
    totals = jnp.sum(weights, axis=2)
    update = jnp.einsum(
        "hqk,khd->hqd",
        weights.astype(jnp.bfloat16),
        value_heads,
        preferred_element_type=jnp.float32,
    )
    result = (new_max, totals, update)
    attended = (
        (result[2] / result[1][:, :, None]).transpose(1, 0, 2).reshape(group_rows, heads_here * HD)
    )
    squares = jnp.sum(attended * attended, axis=1)
    total_squares = lax.psum(squares, "tp")
    scaled = attended / jnp.sqrt(total_squares / DW + 1e-06)[:, None]
    attn_out = jnp.where(valid_rows, scaled, 0.0).astype(jnp.bfloat16)
    return (hyena_out, attn_out)


def solution(mesh):
    in_specs = (
        P("ctx", "tp"),
        P("ctx", "tp"),
        P("ctx", "tp"),
        P(None, "tp"),
        P("tp"),
        P("ctx", "tp"),
        P("ctx", "tp"),
        P(),
    )
    out_specs = (P("ctx", "tp"), P("ctx", "tp"))
    return jax.shard_map(shards, mesh=mesh, in_specs=in_specs, out_specs=out_specs, check_vma=False)
```

profile of v0, /device:TPU:1, one launch (start us, length us, event | category | flops | bytes accessed | tf_op | source)
XLA Modules:
  0.0 591.7 jit_solution(15059241128906599720)
XLA Ops:
  17.7 328.5 %while.16 = (s32[]{:T(128)}, f32[256,512]{0,1:T(8,128)S(1)}, f32[256,512]{0,1:T(8,128)S(1)}, bf16[32,128,512]{1,2,0:T(8,128)(2,1)}, s32[32]{0:T(128)S(1)}, /*ind...) while((s32[]{:T(128)}, f32[256,512]{0,1:T(8,128)S(1)}, ...), condition=%wide.region_1.2_spmd.clone.clone, body=%wide.region_0.1_spmd.clone.clone.sunk | while | flops 341313792 | bytes 12848406 | solution.py:87
  20.5 1.6 fusion.195
  23.8 1.6 fusion.193
  30.8 1.6 fusion.195
  34.0 1.6 fusion.193
  41.0 1.6 fusion.195
  44.3 1.6 fusion.193
  51.3 1.6 fusion.195
  54.6 1.6 fusion.193
  61.6 1.6 fusion.195
  64.8 1.6 fusion.193
  71.8 1.6 fusion.195
  75.1 1.6 fusion.193
  85.3 1.6 fusion.193
  92.4 1.6 fusion.195
  95.6 1.6 fusion.193
  102.6 1.6 fusion.195
  105.9 1.6 fusion.193
  116.1 1.6 fusion.193
  123.1 1.6 fusion.195
  126.4 1.6 fusion.193
  133.4 1.6 fusion.195
  136.7 1.6 fusion.193
  143.7 1.6 fusion.195
  146.9 1.6 fusion.193
  153.9 1.6 fusion.195
  157.2 1.6 fusion.193
  167.4 1.6 fusion.193
  177.7 1.6 fusion.193
  188.0 1.6 fusion.193
  195.0 1.6 fusion.195
  198.2 1.6 fusion.193
  205.3 1.6 fusion.195
  208.5 1.6 fusion.193
  215.5 1.6 fusion.195
  218.8 1.6 fusion.193
  229.0 1.6 fusion.193
  239.3 1.6 fusion.193
  249.6 1.6 fusion.193
  259.8 1.6 fusion.193
  266.9 1.6 fusion.195
  270.1 1.6 fusion.193
  277.1 1.6 fusion.195
  280.4 1.6 fusion.193
  287.4 1.6 fusion.195
  290.6 1.6 fusion.193
  300.9 1.6 fusion.193
  311.1 1.6 fusion.193
  321.4 1.6 fusion.193
  328.4 1.6 fusion.195
  331.7 1.6 fusion.193
  338.7 1.6 fusion.195
  342.0 1.6 fusion.193
  346.2 6.6 %copy.22 = bf16[32,128,512]{2,1,0:T(8,128)(2,1)} copy(bf16[32,128,512]{1,2,0:T(8,128)(2,1)} %get-tuple-element.87) | data formatting | bytes 8388608 | tf_op jit(solution)/shard_map/convert_element_type | solution.py:93
  355.3 89.6 %reduce-scatter.2.cloned.1.call-done = bf16[128,512]{1,0:T(8,128)(2,1)} async-done(((bf16[4096,512]{1,0:T(8,128)(2,1)}), bf16[128,512]{1,0:T(8,128)(2,1)}) %reduce-scatter.2.cloned.1.call-update) | async-done | bytes 131088 | tf_op jit(solution)/shard_map/reduce_scatter | solution.py:92
  445.0 1.6 select_convert_fusion.1
  447.1 56.1 %all-gather.3.cloned.1.call-done = bf16[4096,512]{0,1:T(8,128)(2,1)} async-done(((bf16[128,512]{0,1:T(8,128)(2,1)}), bf16[4096,512]{0,1:T(8,128)(2,1)}) %all-gather.3.cloned.1.call-update) | async-done | bytes 4194320 | tf_op jit(solution)/shard_map/all_gather | solution.py:106
  503.2 4.3 fusion.81
  507.6 3.2 copy-done.1
  510.8 2.5 fusion.82
  513.3 43.7 %all-gather.5.cloned.1.call-done = bf16[4096,512]{1,0:T(8,128)(2,1)} async-done(((bf16[128,512]{1,0:T(8,128)(2,1)}), bf16[4096,512]{1,0:T(8,128)(2,1)}) %all-gather.5.cloned.1.call-update) | async-done | bytes 4194320 | tf_op jit(solution)/shard_map/all_gather | solution.py:107
  557.0 6.4 %copy.26 = bf16[4096,512]{0,1:T(8,128)(2,1)} copy(bf16[4096,512]{1,0:T(8,128)(2,1)} %all-gather.5.cloned.1.call-done) | data formatting | bytes 8388608 | tf_op jit(solution)/shard_map/all_gather | solution.py:107
  563.4 7.0 %multiply_reduce_fusion = (f32[128]{0:T(128)S(1)}, f32[128,4,128]{0,2,1:T(8,128)S(1)}) fusion(f32[128,4]{0,1:T(4,128)S(1)} %bitcast.55, bf16[4096,4,128]{0,2,1:T(8,128)(2,1)} %bitcast.51, f32[4,128,4096]{2,1,0:T(8,128)} %copy-done.1, f32[4,128]{1,0:T(4,128)S(1)} %broadcast_maximum_fusion, pred[128,4096]{1,0:T(8,128)(4,1)S(1)} %fusion.87), kind=kOutput, calls=%fused_computation.97 | convolution fusion | flops 547553152 | bytes 13373952 | tf_op jit(solution)/shard_map/hqk,khd->hqd/dot_general | solution.py:121
  570.4 13.9 %psum.7 = f32[128]{0:T(128)S(1)} all-reduce(f32[128]{0:T(128)S(1)} %get-tuple-element.188), channel_id=1, replica_groups=mesh['ctx'=32,'tp'=8] {'tp'}, use_global_device_ids=true, to_apply=%region_6.7 | all-reduce | flops 128 | bytes 1024 | tf_op jit(solution)/shard_map/psum | solution.py:132
  (307 shorter events, 237.3 us)
Async XLA Ops:
  7.2 496.0 %copy-start = (bf16[128,512]{1,0:T(8,128)(2,1)S(1)}, bf16[128,512]{1,0:T(8,128)(2,1)}, u32[]{:S(2)}) copy-start(bf16[128,512]{1,0:T(8,128)(2,1)} %param.15) | copy-start | bytes 393220
  7.2 437.8 %reduce-scatter.2.cloned.1.call-start = ((), (), s32[]{:S(2)}) async-start(), calls=%async_computation.1 | async-start | bytes 4325376 | tf_op jit(solution)/shard_map/reduce_scatter | solution.py:92
  352.7 0.9 copy-start.3
  352.8 92.2 %copy-start.2 = (bf16[128,512]{1,0:T(8,128)(2,1)S(1)}, bf16[128,512]{1,0:T(8,128)(2,1)}, u32[]{:S(2)}) copy-start(bf16[128,512]{1,0:T(8,128)(2,1)} %param.10) | copy-start | bytes 393220
  352.8 92.2 %copy-start.4 = (f32[512]{0:T(512)S(1)}, f32[512]{0:T(512)}, u32[]{:S(2)}) copy-start(f32[512]{0:T(512)} %param.14) | copy-start | bytes 6148
  352.8 150.4 %all-gather.3.cloned.1.call-start = ((), (), s32[]{:S(2)}) async-start(), calls=%async_computation.2 | async-start | bytes 4325376 | tf_op jit(solution)/shard_map/all_gather | solution.py:106
  354.4 202.5 %all-gather.5.cloned.1.call-start = ((), (), s32[]{:S(2)}) async-start(), calls=%async_computation.3 | async-start | bytes 4325376 | tf_op jit(solution)/shard_map/all_gather | solution.py:107
  507.5 3.2 copy-start.1
Sparse Core Ops, SparseCore 0:
  352.9 92.0 reduce-scatter.1
  448.0 55.1 all-gather.2
  506.3 50.5 all-gather.4
where the time goes:
time: 597 us; the launch traced here: 592 us
  matrix products  307 us (51%)
  waiting for transfers between devices  189 us (32%)
  local copies, waits for them, and re-layouts  39.5 us (7%)
  loops' own time  20.7 us (3%)
  between operations  14.5 us (2%)
  blocking collectives  13.9 us (2%)
  other arithmetic  6.63 us (1%)
    dot_general x68, matrix products, split_dot(): jnp.dot(low, block, preferred_element_type=jnp.float32)  108 us
    dot_general x68, matrix products, split_dot(): jnp.dot(high, block, preferred_element_type=jnp.float32)  107 us
    reduce_scatter x1, waiting for transfers between devices, shards(): lax.psum_scatter(blocks.reshape(lax.axis_size('ctx') * group_rows, blocks...  89.6 us
    all_gather x1, waiting for transfers between devices, shards(): key_piece = lax.all_gather(attn_keys, 'ctx', axis=0, tiled=True)  56.1 us
    dot_general x32, matrix products, inverse(): jnp.dot(sine.T, imag_part, precision=lax.Precision.HIGH, preferred_elemen...  51 us
    all_gather x1, waiting for transfers between devices, shards(): value_piece = lax.all_gather(hyena_out, 'ctx', axis=0, tiled=True)  43.7 us
    dot_general x32, matrix products, inverse(): jnp.dot(cosine.T, real_part, precision=lax.Precision.HIGH, preferred_elem...  29.6 us
    another operation x1, loops' own time, shards(): lax.scan(one_block, first_prior, jnp.arange(lax.axis_size('ctx') * group_...  20.7 us
  transfers between devices with their start and end apart: 3, of which 3 were waited for; matrix products, arithmetic and copies ran while one was open for 2% of the time, Pallas kernels for 0%

commit v1 on v0

v1 whole, which is shorter than its diff:
```python
import functools
import math

import jax
import jax.numpy as jnp
import numpy as np
from jax import lax
from jax.experimental import pallas as pl
from jax.experimental.pallas import tpu as pltpu
from jax.sharding import PartitionSpec as P

HD = 128
DW = 4096
SEQ = 4096
G = 128
NB = SEQ // G
CH = 16
DELTA = 0.25

COLS = [[8 * y + 2 * x + e for y in range(4) for e in range(2)] for x in range(4)]
ROWS = [[8 * y + 2 * k + e for k in range(4)] for y in range(4) for e in range(2)]
COLS_TP = [[i * 8 + t for i in col for t in range(8)] for col in COLS]
CORES = [(i, i ^ 1) for i in range(32)]

BF = jnp.bfloat16
F32 = jnp.float32
NT = (((1,), (1,)), ((), ()))


def tables():
    b = np.arange(G)
    ang = 2.0 * np.pi * np.outer(b, b) / G
    c, s = np.cos(ang), np.sin(ang)
    fwd = np.block([[c, -s], [s, c]]).astype(np.float32)
    high = fwd.astype(jnp.bfloat16)
    low = (fwd - high.astype(np.float32)).astype(jnp.bfloat16)
    phase = 2.0 * np.pi * np.outer(np.arange(NB) + DELTA, b) / SEQ
    twiddle = np.stack([np.cos(phase), np.sin(phase)]).astype(np.float32)
    return high, low, high.T.copy(), low.T.copy(), twiddle


def cmul_const(z, ang):
    re, im = z
    c, s = math.cos(ang), math.sin(ang)
    if im is None:
        return (re * c, re * s) if abs(s) > 1e-12 else (re, jnp.zeros_like(re))
    if abs(s) < 1e-12:
        return (re, im) if c > 0 else (-re, -im)
    if abs(c) < 1e-12:
        return (-im, re) if s > 0 else (im, -re)
    return (re * c - im * s, re * s + im * c)


def fft(z, sign):
    n = len(z)
    if n == 1:
        return z
    half = n // 2
    up, down = [], []
    for j in range(half):
        (ar, ai), (br, bi) = z[j], z[j + half]
        up.append((ar + br, ai + bi))
        down.append(cmul_const((ar - br, ai - bi), sign * 2.0 * math.pi * j / n))
    even, odd = fft(up, sign), fft(down, sign)
    out = []
    for e, o in zip(even, odd):
        out += [e, o]
    return out


def split(x):
    high = x.astype(BF)
    return high, (x - high.astype(F32)).astype(BF)


def dot3(x, m_high, m_low):
    high, low = split(x)
    return (
        jnp.dot(high, m_high, preferred_element_type=F32)
        + jnp.dot(low, m_high, preferred_element_type=F32)
        + jnp.dot(high, m_low, preferred_element_type=F32)
    )


def spectrum(blocks, tw_ref, mh_ref, ml_ref, buf):
    z = [cmul_const((x, None), -2.0 * math.pi * DELTA * i / NB) for i, x in enumerate(blocks)]
    z = fft(z, -1.0)
    for p, (re, im) in enumerate(z):
        c, s = tw_ref[0, p : p + 1, :], tw_ref[1, p : p + 1, :]
        buf[p * CH : (p + 1) * CH, :G] = re * c + im * s
        buf[p * CH : (p + 1) * CH, G:] = im * c - re * s
    return dot3(buf[...], mh_ref[...], ml_ref[...])


def pre_kernel(key_ref, value_ref, gate_ref, attn_ref, query_ref, msg_ref, qmsg_ref):
    for h in range(4):
        cols = slice(h * HD, (h + 1) * HD)
        mixed = (key_ref[:, cols].astype(F32) * value_ref[:, cols].astype(F32)).T.astype(BF)
        gate = gate_ref[:, cols].astype(F32).T.astype(BF)
        for c in range(2):
            for k in range(4):
                e = 8 * h + 2 * k + c
                rows = slice(c * 64 + k * CH, c * 64 + (k + 1) * CH)
                msg_ref[e, 0:64, :] = attn_ref[c * 64 : (c + 1) * 64, cols]
                msg_ref[e, 64:80, :] = mixed[rows]
                msg_ref[e, 80:96, :] = gate[rows]
            qmsg_ref[2 * h + c] = query_ref[:, cols]


def taps_kernel(idx_ref, taps_ref, tw_ref, mh_ref, ml_ref, out_ref, buf):
    first = idx_ref[1]
    row = lax.broadcasted_iota(jnp.int32, (CH, G), 0)
    lane = lax.broadcasted_iota(jnp.int32, (CH, G), 1)
    pick = jnp.where(lane == row + first, 1.0, 0.0).astype(BF)
    blocks = [
        lax.dot_general(pick, taps_ref[i * G : (i + 1) * G, :], NT, preferred_element_type=F32)
        for i in range(NB)
    ]
    out_ref[...] = spectrum(blocks, tw_ref, mh_ref, ml_ref, buf)


def conv_kernel(
    idx_ref, in_ref, spec_ref, skip_ref, tw_ref, mh_ref, ml_ref, nh_ref, nl_ref, out_ref, buf
):
    valid = idx_ref[2]
    blocks = [in_ref[i, 0:CH, :].astype(F32) for i in range(NB)]
    x = spectrum(blocks, tw_ref, mh_ref, ml_ref, buf)
    xr, xi, hr, hi = x[:, :G], x[:, G:], spec_ref[:, :G], spec_ref[:, G:]
    buf[:, :G] = xr * hr - xi * hi
    buf[:, G:] = xr * hi + xi * hr
    buf[...] = dot3(buf[...], nh_ref[...], nl_ref[...])
    z = []
    for p in range(NB):
        re, im = buf[p * CH : (p + 1) * CH, :G], buf[p * CH : (p + 1) * CH, G:]
        c, s = tw_ref[0, p : p + 1, :], tw_ref[1, p : p + 1, :]
        z.append((re * c - im * s, im * c + re * s))
    z = fft(z, 1.0)
    skip = skip_ref[...]
    lane = lax.broadcasted_iota(jnp.int32, (CH, G), 1)
    for i, (re, im) in enumerate(z):
        ang = 2.0 * math.pi * DELTA * i / NB
        y = (re * math.cos(ang) - im * math.sin(ang)) * (1.0 / SEQ)
        y = in_ref[i, CH : 2 * CH, :].astype(F32) * (y + skip * in_ref[i, 0:CH, :].astype(F32))
        y = jnp.where(lane + i * G < valid, y, 0.0).astype(BF)
        for k in range(4):
            out_ref[k, i] = y


def weights_kernel(idx_ref, q_ref, own_ref, other_ref, w_ref, total_ref, keys, scores):
    k, core, valid = idx_ref[3], idx_ref[4], idx_ref[2]
    flip = core == 1
    for s in range(NB):
        own, other = own_ref[s], other_ref[s]
        keys[s * G : s * G + 64] = jnp.where(flip, other, own)
        keys[s * G + 64 : (s + 1) * G] = jnp.where(flip, own, other)
    factor = math.log2(math.e) / math.sqrt(HD)
    row = lax.broadcasted_iota(jnp.int32, (2 * G, G), 0)
    lane = lax.broadcasted_iota(jnp.int32, (2 * G, G), 1)
    for t in range(4):
        q = q_ref[2 * t : 2 * t + 2].reshape(2 * G, HD)
        limit = jnp.minimum(row + (8 * t + 2 * k) * G, valid - 1)
        top = None
        for m in range(4 * t + 4):
            s = lax.dot_general(
                q, keys[m * 2 * G : (m + 1) * 2 * G], NT, preferred_element_type=F32
            )
            for u in range(2):
                n = 2 * m + u
                part = s[:, u * G : (u + 1) * G]
                if n >= 8 * t:
                    part = jnp.where(lane + n * G <= limit, part, -1e30)
                scores[:, n * G : (n + 1) * G] = part
                top = part if top is None else jnp.maximum(top, part)
        top = jnp.max(top, axis=1, keepdims=True)
        total = None
        for n in range(8 * t + 8):
            part = jnp.exp2((scores[:, n * G : (n + 1) * G] - top) * factor)
            w_ref[2 * t * G : (2 * t + 2) * G, n * G : (n + 1) * G] = part.astype(BF)
            total = part if total is None else total + part
        total = jnp.sum(total, axis=1, keepdims=True)
        total_ref[2 * t * G : (2 * t + 2) * G, :] = jnp.broadcast_to(total, (2 * G, G))


def values_kernel(idx_ref, w_ref, total_ref, v_ref, msg_ref, sum_ref, vals):
    k, core = idx_ref[3], idx_ref[4]
    for s in range(NB):
        block = v_ref[:, s].reshape(64, G)
        vals[0:64, s * G : (s + 1) * G] = block
        vals[64:128, s * G : (s + 1) * G] = block
    lane = lax.broadcasted_iota(jnp.int32, (64, G), 1)
    mine = (lane < 64) != (core == 1)
    ones = jnp.where(lax.broadcasted_iota(jnp.int32, (8, G), 1) < 64, 1.0, 0.0).astype(BF)
    for t in range(4):
        n = (8 * t + 8) * G
        rows = slice(2 * t * G, (2 * t + 2) * G)
        out = lax.dot_general(w_ref[rows, 0:n], vals[:, 0:n], NT, preferred_element_type=F32)
        out = out / total_ref[rows, :]
        high, low = split(out * out)
        sums = lax.dot_general(ones, high, NT, preferred_element_type=F32) + lax.dot_general(
            ones, low, NT, preferred_element_type=F32
        )
        for c in range(2):
            j = 2 * t + c
            a = out[c * G : c * G + 64]
            b = out[c * G + 64 : (c + 1) * G]
            msg_ref[j, 0:64, :] = jnp.where(mine, a, b).astype(BF)
            msg_ref[j, 64:128, :] = v_ref[:, 8 * t + 2 * k + c].reshape(64, G)
            sum_ref[8 * j : 8 * j + 8, :] = sums[:, c * G : (c + 1) * G]


def final_kernel(idx_ref, msg_ref, sum_ref, hyena_ref, attn_ref):
    valid, own = idx_ref[2], idx_ref[5]
    total = jnp.sum(sum_ref[...], axis=0, keepdims=True)
    norm = jnp.sqrt(total * (1.0 / DW) + 1e-06)
    inv = jnp.broadcast_to(1.0 / norm, (G, G)).T
    row = lax.broadcasted_iota(jnp.int32, (G, G), 0)
    inv = jnp.where(row + own * G < valid, inv, 0.0)
    left = lax.broadcasted_iota(jnp.int32, (64, G), 1) < 64
    for h in range(4):
        cols = slice(h * HD, (h + 1) * HD)
        p0 = msg_ref[2 * h, 0:64, :].astype(F32)
        p1 = msg_ref[2 * h + 1, 0:64, :].astype(F32)
        low = jnp.where(left, p0, p1)
        high = pltpu.roll(jnp.where(left, p1, p0), 64, 1)
        attn_ref[0:64, cols] = (low * inv[0:64]).astype(BF)
        attn_ref[64:128, cols] = (high * inv[64:128]).astype(BF)
        hy = msg_ref[2 * h : 2 * h + 2, 64:128, :].reshape(G, G).astype(F32)
        hyena_ref[:, cols] = hy.T.astype(BF)


def sds(shape, dtype):
    return jax.ShapeDtypeStruct(shape, dtype)


def full(*shape):
    return pl.BlockSpec(shape, lambda *_: (0,) * len(shape))


def call(kernel, out_shape, in_specs, scratch=(), cost=(1e7, 1 << 20), vmem=24):
    outs = out_shape if isinstance(out_shape, (tuple, list)) else (out_shape,)
    specs = [full(*o.shape) for o in outs]
    return pl.pallas_call(
        kernel,
        out_shape=out_shape,
        grid_spec=pltpu.PrefetchScalarGridSpec(
            num_scalar_prefetch=1,
            grid=(1,),
            in_specs=in_specs,
            out_specs=specs if isinstance(out_shape, (tuple, list)) else specs[0],
            scratch_shapes=list(scratch),
        ),
        compiler_params=pltpu.CompilerParams(vmem_limit_bytes=vmem << 20),
        cost_estimate=pl.CostEstimate(
            flops=int(cost[0]), bytes_accessed=int(cost[1]), transcendentals=0
        ),
    )


def shards(
    hyena_gate, hyena_key, hyena_value, filter_taps, skip_weight, queries, attn_keys, valid_length
):
    own = lax.axis_index("ctx").astype(jnp.int32)
    h, k, core = own // 8, (own // 2) % 4, own % 2
    first = core * 64 + k * CH
    idx = jnp.stack([h, first, valid_length[0], k, core, own])
    high, low, high_t, low_t, twiddle = (jnp.asarray(t) for t in tables())
    skip = lax.dynamic_slice_in_dim(skip_weight, h * HD + first, CH, 0)
    skip = jnp.broadcast_to(skip[:, None], (CH, G))
    a2a = functools.partial(lax.all_to_all, split_axis=0, concat_axis=0, tiled=True)

    block = full(G, 4 * HD)
    msg, qmsg = pl.pallas_call(
        pre_kernel,
        out_shape=(sds((NB, 96, G), BF), sds((8, G, HD), BF)),
        compiler_params=pltpu.CompilerParams(vmem_limit_bytes=16 << 20),
        cost_estimate=pl.CostEstimate(flops=1000000, bytes_accessed=2 << 20, transcendentals=0),
    )(hyena_key, hyena_value, hyena_gate, attn_keys, queries)
    got = a2a(msg, "ctx")
    got_q = a2a(qmsg, "ctx", axis_index_groups=COLS)

    spec = call(
        taps_kernel,
        sds((NB * CH, 2 * G), F32),
        [
            pl.BlockSpec((SEQ, G), lambda i, idx: (0, idx[0])),
            full(2, NB, G),
            full(2 * G, 2 * G),
            full(2 * G, 2 * G),
        ],
        [pltpu.VMEM((NB * CH, 2 * G), F32)],
        cost=(2e9, 4 << 20),
    )(idx, filter_taps, twiddle, high, low)

    got_other = lax.ppermute(got, "ctx", CORES)
    values = call(
        conv_kernel,
        sds((4, NB, CH, G), BF),
        [
            pl.BlockSpec((NB, 2 * CH, G), lambda i, idx: (0, 2, 0)),
            full(NB * CH, 2 * G),
            full(CH, G),
            full(2, NB, G),
            full(2 * G, 2 * G),
            full(2 * G, 2 * G),
            full(2 * G, 2 * G),
            full(2 * G, 2 * G),
        ],
        [pltpu.VMEM((NB * CH, 2 * G), F32)],
        cost=(2e9, 4 << 20),
    )(idx, got, spec, skip, twiddle, high, low, high_t, low_t)
    got_v = a2a(values, "ctx", axis_index_groups=ROWS)

    weights, totals = call(
        weights_kernel,
        (sds((8 * G, SEQ), BF), sds((8 * G, G), F32)),
        [
            full(8, G, HD),
            pl.BlockSpec((NB, 64, G), lambda i, idx: (0, 0, 0)),
            pl.BlockSpec((NB, 64, G), lambda i, idx: (0, 0, 0)),
        ],
        [pltpu.VMEM((SEQ, HD), BF), pltpu.VMEM((2 * G, SEQ), F32)],
        cost=(4e9, 16 << 20),
    )(idx, got_q, got, got_other)

    back, sums = call(
        values_kernel,
        (sds((8, G, G), BF), sds((64, G), F32)),
        [full(8 * G, SEQ), full(8 * G, G), full(4, NB, CH, G)],
        [pltpu.VMEM((G, SEQ), BF)],
        cost=(2e9, 8 << 20),
        vmem=32,
    )(idx, weights, totals, got_v)
    got_back = a2a(back, "ctx", axis_index_groups=COLS)
    got_sums = a2a(sums, ("ctx", "tp"), axis_index_groups=COLS_TP)

    return call(
        final_kernel,
        (sds((G, 4 * HD), BF), sds((G, 4 * HD), BF)),
        [full(8, G, G), full(64, G)],
        cost=(1e6, 1 << 20),
    )(idx, got_back, got_sums)


def solution(mesh):
    in_specs = (
        P("ctx", "tp"),
        P("ctx", "tp"),
        P("ctx", "tp"),
        P(None, "tp"),
        P("tp"),
        P("ctx", "tp"),
        P("ctx", "tp"),
        P(),
    )
    out_specs = (P("ctx", "tp"), P("ctx", "tp"))
    return jax.shard_map(shards, mesh=mesh, in_specs=in_specs, out_specs=out_specs, check_vma=False)
```

time: 597 us -> 96.9 us (0.16)
  matrix products: 307 us -> 0 us
  waiting for transfers between devices: 189 us -> 2.2 us
  blocking collectives: 13.9 us -> 53.9 us
  local copies, waits for them, and re-layouts: 39.5 us -> 16.8 us
  loops' own time: 20.7 us -> 0 us
  Pallas kernels: 0 us -> 14.5 us
  between operations: 14.5 us -> 1.42 us
  starting transfers between devices: 0.3 us -> 7.35 us
  other arithmetic: 6.63 us -> 0 us
    dot_general x202 -> x0, matrix products: 307 us -> none  [the longest x68 108 us: split_dot(): jnp.dot(low, block, preferred_element_type=jnp.float32)]
    all_gather x2 -> x0, waiting for transfers between devices: 99.8 us -> none  [the longest x1 56.1 us: shards(): key_piece = lax.all_gather(attn_keys, 'ctx', axis=0, tiled=True)]
    reduce_scatter x1 -> x0, waiting for transfers between devices: 89.6 us -> none  [shards(): lax.psum_scatter(blocks.reshape(lax.axis_size('ctx') * group_rows, blocks...]
    all_to_all x0 -> x3, blocking collectives: none -> 53.9 us  [the longest x1 22.6 us: shards(): got = a2a(msg, 'ctx')]
    another operation x1 -> x0, loops' own time: 20.7 us -> none  [shards(): lax.scan(one_block, first_prior, jnp.arange(lax.axis_size('ctx') * group_...]
    dynamic_slice x32 -> x1, local copies, waits for them, and re-layouts: 18.5 us -> 0.76 us  [shards(): skip = lax.dynamic_slice_in_dim(skip_weight, h * HD + first, CH, 0)]
    pallas_call x0 -> x6, Pallas kernels: none -> 14.5 us  [the longest x1 4.03 us: shards(): call(weights_kernel, (sds((8 * G, SEQ), BF), sds((8 * G, G), F32)), [full...]
    psum x1 -> x0, blocking collectives: 13.9 us -> none  [shards(): total_squares = lax.psum(squares, 'tp')]
  transfers between devices with their start and end apart: 3 -> 3, of which waited for: 3 -> 1; matrix products, arithmetic and copies ran while one was open for 2% -> 1% of each run, Pallas kernels for 0% -> 9%
where the time goes in v1:
time: 96.9 us; the launch traced here: 96.2 us
  blocking collectives  53.9 us (56%)
  local copies, waits for them, and re-layouts  16.8 us (17%)
  Pallas kernels  14.5 us (15%)
  starting transfers between devices  7.35 us (8%)
  waiting for transfers between devices  2.2 us (2%)
  between operations  1.42 us (1%)
    all_to_all x1, blocking collectives, shards(): got = a2a(msg, 'ctx')  22.6 us
    all_to_all x1, blocking collectives, shards(): got_sums = a2a(sums, ('ctx', 'tp'), axis_index_groups=COLS_TP)  21.5 us
    unnamed x32, local copies, waits for them, and re-layouts  15.9 us
    all_to_all x1, blocking collectives, shards(): got_back = a2a(back, 'ctx', axis_index_groups=COLS)  9.76 us
    pallas_call x1, Pallas kernels, shards(): call(weights_kernel, (sds((8 * G, SEQ), BF), sds((8 * G, G), F32)), [full...  4.03 us
    pallas_call x1, Pallas kernels, shards(): call(values_kernel, (sds((8, G, G), BF), sds((64, G), F32)), [full(8 * G,...  3.94 us
    all_to_all x1, starting transfers between devices, shards(): got_v = a2a(values, 'ctx', axis_index_groups=ROWS)  3.47 us
    all_to_all x1, starting transfers between devices, shards(): got_q = a2a(qmsg, 'ctx', axis_index_groups=COLS)  3.36 us
  transfers between devices with their start and end apart: 3, of which 1 were waited for; matrix products, arithmetic and copies ran while one was open for 1% of the time, Pallas kernels for 9%

profile of v1, /device:TPU:1, one launch (start us, length us, event | category | flops | bytes accessed | tf_op | source)
XLA Modules:
  0.0 96.2 jit_solution(4125487235376559633)
XLA Ops:
  0.6 0.0 copy-start.2
  0.6 0.9 copy-done.2
  1.5 0.0 copy-start.3
  1.5 0.9 copy-done.3
  2.4 0.0 copy-start.4
  2.4 0.9 copy-done.4
  3.3 0.0 copy-start.5
  3.3 0.9 copy-done.5
  4.3 0.0 copy-start.6
  4.3 0.9 copy-done.6
  5.2 0.0 copy-start.9
  5.2 0.0 copy-start.11
  5.2 0.0 copy-start.12
  5.2 0.0 copy-start.13
  5.2 0.0 copy-start.15
  5.2 0.8 shard_map.140
  6.0 22.6 %all_to_all.31.own_ref.in_ref = bf16[32,96,128]{2,1,0:T(8,128)(2,1)S(1)} all-to-all(bf16[32,96,128]{2,1,0:T(8,128)(2,1)S(1)} %get-tuple-element.9), channel_id=1, replica_groups=mesh['ctx'=32,'tp'=8] {'ctx'}, dimensions={0} | all-to-all | bytes 1572864 | tf_op jit(solution)/shard_map/all_to_all | solution.py:278
  28.6 0.5 collective-permute-start
  29.2 3.4 %all-to-all-start = ((bf16[8,128,128]{2,1,0:T(8,128)(2,1)}), bf16[8,128,128]{2,1,0:T(8,128)(2,1)S(1)}, u32[]{:S(2)}, u32[]{:S(2)}) async-start(bf16[8,128,128]{2,1,0:T(8,128)(2,1)} %get-tuple-element.8), calls=%async_computation | async-start | bytes 524288 | tf_op jit(solution)/shard_map/all_to_all | solution.py:279
  33.2 0.1 stack.23.idx_ref
  33.3 0.0 copy-start.7
  33.3 2.2 %copy-done.7 = bf16[4096,512]{1,0:T(8,128)(2,1)S(1)} copy-done((bf16[4096,512]{1,0:T(8,128)(2,1)S(1)}, bf16[4096,512]{1,0:T(8,128)(2,1)}, u32[]{:S(2)}) %copy-start.7) | copy-done | bytes 4194328
  35.5 0.0 copy-start.8
  35.5 0.9 copy-done.8
  36.4 0.0 copy-start.10
  36.4 0.9 copy-done.10
  37.3 0.0 copy-start.14
  37.3 0.8 copy-done.14
  38.1 1.6 %shard_map.142.spec_ref = f32[512,256]{1,0:T(8,128)S(1)} custom-call(s32[6]{0:T(128)S(1)} %stack.23.idx_ref, bf16[4096,512]{1,0:T(8,128)(2,1)S(1)} %copy-done.7, f32[2,32,128]{2,1,0:T(8,128)S(1)} %copy-done.14, bf16[256,256]{1,0:T(8,128)(2,1)S(1)} %copy-done.8, bf16[256,256]{1,0:T(8,128)(2,1)S(1)} %copy-done.10), custom_call_target="tpu_custom_call" | custom-call | flops 2000000000 | bytes 4194304 | tf_op jit(solution)/shard_map/pallas_call | solution.py:281
  39.7 0.8 dynamic_slice.3
  40.4 0.1 broadcast_in_dim.2.skip_ref
  40.5 0.0 copy-done.9
  40.5 0.0 copy-done.11
  40.5 0.0 copy-done.12
  40.5 0.0 copy-done.13
  40.5 0.0 copy-done.15
  40.6 2.7 %shard_map.143 = bf16[4,32,16,128]{3,2,1,0:T(8,128)(2,1)} custom-call(s32[6]{0:T(128)S(1)} %stack.23.idx_ref, bf16[32,96,128]{2,1,0:T(8,128)(2,1)S(1)} %all_to_all.31.own_ref.in_ref, f32[512,256]{1,0:T(8,128)S(1)} %shard_map.142.spec_ref, f32[16,128]{1,0:T(8,128)S(1)} %broadcast_in_dim.2.skip_ref, f32[2,32,128]{2,1,0:T(8,128)S(1)} %copy-done.15, ...), custom_call_target="tpu_custom_call" | custom-call | flops 2000000000 | bytes 4194304 | tf_op jit(solution)/shard_map/pallas_call | solution.py:295
  43.3 0.0 all-to-all-done.q_ref
  43.3 3.5 %all-to-all-start.2 = ((bf16[4,32,16,128]{3,2,1,0:T(8,128)(2,1)}), bf16[4,32,16,128]{3,2,1,0:T(8,128)(2,1)S(1)}, u32[]{:S(2)}, u32[]{:S(2)}) async-start(bf16[4,32,16,128]{3,2,1,0:T(8,128)(2,1)} %shard_map.143), calls=%async_computation.2 | async-start | bytes 1048576 | tf_op jit(solution)/shard_map/all_to_all | solution.py:311
  46.8 0.0 collective-permute-done.other_ref
  46.8 4.0 %shard_map.141 = (bf16[1024,4096]{1,0:T(8,128)(2,1)S(1)}, f32[1024,128]{1,0:T(8,128)S(1)}) custom-call(s32[6]{0:T(128)S(1)} %stack.23.idx_ref, bf16[8,128,128]{2,1,0:T(8,128)(2,1)S(1)} %all-to-all-done.q_ref, bf16[32,96,128]{2,1,0:T(8,128)(2,1)S(1)} %all_to_all.31.own_ref.in_ref, bf16[32,96,128]{2,1,0:T(8,128)(2,1)S(1)} %collective-permute-done.other_ref), custom_call_target="tpu_custom_call" | custom-call | flops 4000000000 | bytes 16777216 | tf_op jit(solution)/shard_map/pallas_call | solution.py:313
  50.8 0.0 copy-start
  50.8 3.3 %copy-done = bf16[1024,4096]{1,0:T(8,128)(2,1)} copy-done((bf16[1024,4096]{1,0:T(8,128)(2,1)}, bf16[1024,4096]{1,0:T(8,128)(2,1)S(1)}, u32[]{:S(2)}) %copy-start) | copy-done | bytes 8388632
  54.1 2.2 %all-to-all-done.2.v_ref = bf16[4,32,16,128]{3,2,1,0:T(8,128)(2,1)S(1)} async-done(((bf16[4,32,16,128]{3,2,1,0:T(8,128)(2,1)}), bf16[4,32,16,128]{3,2,1,0:T(8,128)(2,1)S(1)}, u32[]{:S(2)}, u32[]{:S(2)}) %all-to-all-start.2) | async-done | bytes 524320 | tf_op jit(solution)/shard_map/all_to_all | solution.py:311
  56.3 0.0 copy-start.1
  56.3 3.4 %copy-done.1 = bf16[1024,4096]{1,0:T(8,128)(2,1)S(1)} copy-done((bf16[1024,4096]{1,0:T(8,128)(2,1)S(1)}, bf16[1024,4096]{1,0:T(8,128)(2,1)}, u32[]{:S(2)}) %copy-start.1) | copy-done | bytes 8388632
  59.6 3.9 %shard_map.144 = (bf16[8,128,128]{2,1,0:T(8,128)(2,1)S(1)}, f32[64,128]{1,0:T(8,128)S(1)}) custom-call(s32[6]{0:T(128)S(1)} %stack.23.idx_ref, bf16[1024,4096]{1,0:T(8,128)(2,1)S(1)} %copy-done.1, f32[1024,128]{1,0:T(8,128)S(1)} %get-tuple-element.11.total_ref, bf16[4,32,16,128]{3,2,1,0:T(8,128)(2,1)S(1)} %all-to-all-done.2.v_ref), custom_call_target="tpu_custom_call" | custom-call | flops 2000000000 | bytes 8388608 | tf_op jit(solution)/shard_map/pallas_call | solution.py:325
  63.6 21.5 %all_to_all.32 = f32[64,1,128]{2,1,0:T(1,128)S(1)} all-to-all(f32[64,1,128]{2,1,0:T(1,128)S(1)} %bitcast.10), channel_id=1, replica_groups={{0,1,2,3,4,5,6,7,8,9,10,11,12,13,14,15,64,65,66,67,68,69,70,71,72,73,74..., dimensions={0} | all-to-all | bytes 65536 | tf_op jit(solution)/shard_map/all_to_all | solution.py:334
  85.1 9.8 %all_to_all.33.msg_ref = bf16[8,128,128]{2,1,0:T(8,128)(2,1)S(1)} all-to-all(bf16[8,128,128]{2,1,0:T(8,128)(2,1)S(1)} %get-tuple-element.12), channel_id=1, replica_groups={{0,8,64,72,128,136,192,200},{16,24,80,88,144,152,208,216},{32,40,96,104..., dimensions={0} | all-to-all | bytes 524288 | tf_op jit(solution)/shard_map/all_to_all | solution.py:333
  94.8 1.4 %shard_map.145 = (bf16[128,512]{1,0:T(8,128)(2,1)}, bf16[128,512]{1,0:T(8,128)(2,1)}) custom-call(s32[6]{0:T(128)S(1)} %stack.23.idx_ref, bf16[8,128,128]{2,1,0:T(8,128)(2,1)S(1)} %all_to_all.33.msg_ref, f32[64,128]{1,0:T(8,128)S(1)} %bitcast.9), custom_call_target="tpu_custom_call" | custom-call | flops 1000000 | bytes 1048576 | tf_op jit(solution)/shard_map/pallas_call | solution.py:336
Async XLA Ops:
  0.6 0.9 copy-start.2
  1.5 0.9 copy-start.3
  2.4 0.9 copy-start.4
  3.3 0.9 copy-start.5
  4.3 0.9 copy-start.6
  5.2 35.4 %copy-start.9 = (bf16[256,256]{1,0:T(8,128)(2,1)S(1)}, bf16[256,256]{1,0:T(8,128)(2,1)}, u32[]{:S(2)}) copy-start(bf16[256,256]{1,0:T(8,128)(2,1)} %constant.69.clone.mh_ref) | copy-start | bytes 393220
  5.2 35.4 %copy-start.11 = (bf16[256,256]{1,0:T(8,128)(2,1)S(1)}, bf16[256,256]{1,0:T(8,128)(2,1)}, u32[]{:S(2)}) copy-start(bf16[256,256]{1,0:T(8,128)(2,1)} %constant.70.clone.ml_ref) | copy-start | bytes 393220
  5.2 35.4 %copy-start.12 = (bf16[256,256]{1,0:T(8,128)(2,1)S(1)}, bf16[256,256]{1,0:T(8,128)(2,1)}, u32[]{:S(2)}) copy-start(bf16[256,256]{1,0:T(8,128)(2,1)} %constant.71.clone.nh_ref) | copy-start | bytes 393220
  5.2 35.4 %copy-start.13 = (bf16[256,256]{1,0:T(8,128)(2,1)S(1)}, bf16[256,256]{1,0:T(8,128)(2,1)}, u32[]{:S(2)}) copy-start(bf16[256,256]{1,0:T(8,128)(2,1)} %constant.72.clone.nl_ref) | copy-start | bytes 393220
  5.2 35.4 %copy-start.15 = (f32[2,32,128]{2,1,0:T(8,128)S(1)}, f32[2,32,128]{2,1,0:T(8,128)}, u32[]{:S(2)}) copy-start(f32[2,32,128]{2,1,0:T(8,128)} %constant.73.clone.tw_ref) | copy-start | bytes 98308
  28.6 18.1 %collective-permute-start = (bf16[32,96,128]{2,1,0:T(8,128)(2,1)S(1)}, bf16[32,96,128]{2,1,0:T(8,128)(2,1)S(1)}, u32[]{:S(2)}, u32[]{:S(2)}) collective-permute-start(bf16[32,96,128]{2,1,0:T(8,128)(2,1)S(1)} %all_to_all.31.own_ref.in_ref), channel_id=1, source_target_pairs={{0,8},{8,0},{16,24},{24,16},{32,40},{40,32},{48,56},{56,48},{64,72... | collective-permute-start | bytes 2359304 | tf_op jit(solution)/shard_map/ppermute | solution.py:294
  29.2 14.1 %all-to-all-start = ((bf16[8,128,128]{2,1,0:T(8,128)(2,1)}), bf16[8,128,128]{2,1,0:T(8,128)(2,1)S(1)}, u32[]{:S(2)}, u32[]{:S(2)}) async-start(bf16[8,128,128]{2,1,0:T(8,128)(2,1)} %get-tuple-element.8), calls=%async_computation | async-start | bytes 524288 | tf_op jit(solution)/shard_map/all_to_all | solution.py:279
  33.3 2.2 %copy-start.7 = (bf16[4096,512]{1,0:T(8,128)(2,1)S(1)}, bf16[4096,512]{1,0:T(8,128)(2,1)}, u32[]{:S(2)}) copy-start(bf16[4096,512]{1,0:T(8,128)(2,1)} %taps_ref.1) | copy-start | bytes 12582916
  35.5 0.9 copy-start.8
  36.4 0.9 copy-start.10
  37.3 0.8 copy-start.14
  43.3 13.0 %all-to-all-start.2 = ((bf16[4,32,16,128]{3,2,1,0:T(8,128)(2,1)}), bf16[4,32,16,128]{3,2,1,0:T(8,128)(2,1)S(1)}, u32[]{:S(2)}, u32[]{:S(2)}) async-start(bf16[4,32,16,128]{3,2,1,0:T(8,128)(2,1)} %shard_map.143), calls=%async_computation.2 | async-start | bytes 1048576 | tf_op jit(solution)/shard_map/all_to_all | solution.py:311
  50.8 3.3 %copy-start = (bf16[1024,4096]{1,0:T(8,128)(2,1)}, bf16[1024,4096]{1,0:T(8,128)(2,1)S(1)}, u32[]{:S(2)}) copy-start(bf16[1024,4096]{1,0:T(8,128)(2,1)S(1)} %get-tuple-element.10.w_ref) | copy-start | bytes 25165828
  56.3 3.4 %copy-start.1 = (bf16[1024,4096]{1,0:T(8,128)(2,1)S(1)}, bf16[1024,4096]{1,0:T(8,128)(2,1)}, u32[]{:S(2)}) copy-start(bf16[1024,4096]{1,0:T(8,128)(2,1)} %copy-done) | copy-start | bytes 25165828

commit v2 on v1

v2 whole, which is shorter than its diff:
```python
import math

import jax
import jax.numpy as jnp
import numpy as np
from jax import lax
from jax.experimental import pallas as pl
from jax.experimental.pallas import tpu as pltpu
from jax.sharding import PartitionSpec as P


HD = 128
DW = 4096
SEQ = 4096
G = 128
NB = SEQ // G
CH = 16
DELTA = 0.25

COLS = [[8 * y + 2 * x + e for y in range(4) for e in range(2)] for x in range(4)]
CORES = [(i, i ^ 1) for i in range(32)]


def along_y(d):
    return [(i, (i + 8 * d) % 32) for i in range(32)]


def along_x(d):
    return [(i, 8 * (i // 8) + (i + 2 * d) % 8) for i in range(32)]


BF = jnp.bfloat16
F32 = jnp.float32
NT = (((1,), (1,)), ((), ()))


def tables():
    b = np.arange(G)
    ang = 2.0 * np.pi * np.outer(b, b) / G
    c, s = np.cos(ang), np.sin(ang)
    fwd = np.block([[c, -s], [s, c]]).astype(np.float32)
    high = fwd.astype(jnp.bfloat16)
    low = (fwd - high.astype(np.float32)).astype(jnp.bfloat16)
    phase = 2.0 * np.pi * np.outer(np.arange(NB) + DELTA, b) / SEQ
    twiddle = np.stack([np.cos(phase), np.sin(phase)]).astype(np.float32)
    return high, low, high.T.copy(), low.T.copy(), twiddle


def cmul_const(z, ang):
    re, im = z
    c, s = math.cos(ang), math.sin(ang)
    if im is None:
        return (re * c, re * s) if abs(s) > 1e-12 else (re, jnp.zeros_like(re))
    if abs(s) < 1e-12:
        return (re, im) if c > 0 else (-re, -im)
    if abs(c) < 1e-12:
        return (-im, re) if s > 0 else (im, -re)
    return (re * c - im * s, re * s + im * c)


def fft(z, sign):
    n = len(z)
    if n == 1:
        return z
    half = n // 2
    up, down = [], []
    for j in range(half):
        (ar, ai), (br, bi) = z[j], z[j + half]
        up.append((ar + br, ai + bi))
        down.append(cmul_const((ar - br, ai - bi), sign * 2.0 * math.pi * j / n))
    even, odd = fft(up, sign), fft(down, sign)
    out = []
    for e, o in zip(even, odd):
        out += [e, o]
    return out


def split(x):
    high = x.astype(BF)
    return high, (x - high.astype(F32)).astype(BF)


def dot3(x, m_high, m_low):
    high, low = split(x)
    return (
        jnp.dot(high, m_high, preferred_element_type=F32)
        + jnp.dot(low, m_high, preferred_element_type=F32)
        + jnp.dot(high, m_low, preferred_element_type=F32)
    )


def spectrum(blocks, tw_ref, mh_ref, ml_ref, buf):
    z = [cmul_const((x, None), -2.0 * math.pi * DELTA * i / NB) for i, x in enumerate(blocks)]
    z = fft(z, -1.0)
    for p, (re, im) in enumerate(z):
        c, s = tw_ref[0, p : p + 1, :], tw_ref[1, p : p + 1, :]
        buf[p * CH : (p + 1) * CH, :G] = re * c + im * s
        buf[p * CH : (p + 1) * CH, G:] = im * c - re * s
    return dot3(buf[...], mh_ref[...], ml_ref[...])


def load(pairs, sems):
    copies = [pltpu.make_async_copy(a, b, sems.at[n]) for n, (a, b) in enumerate(pairs)]
    for copy in copies:
        copy.start()
    return copies


def pre_kernel(idx_ref, key_hbm, value_hbm, gate_hbm, attn_hbm, query_hbm, *refs):
    msg_ref, q_refs, (key_ref, value_ref, gate_ref, attn_ref, query_ref, sems) = (
        refs[0],
        refs[1:5],
        refs[5:],
    )
    copies = load(
        [
            (key_hbm, key_ref),
            (value_hbm, value_ref),
            (gate_hbm, gate_ref),
            (attn_hbm, attn_ref),
            (query_hbm, query_ref),
        ],
        sems,
    )
    copies[0].wait()
    copies[1].wait()
    for h in range(4):
        cols = slice(h * HD, (h + 1) * HD)
        mixed = (key_ref[:, cols].astype(F32) * value_ref[:, cols].astype(F32)).T.astype(BF)
        for c in range(2):
            for k in range(4):
                rows = slice(c * 64 + k * CH, c * 64 + (k + 1) * CH)
                msg_ref[8 * h + 2 * k + c, 64:80, :] = mixed[rows]
    copies[2].wait()
    for h in range(4):
        gate = gate_ref[:, h * HD : (h + 1) * HD].astype(F32).T.astype(BF)
        for c in range(2):
            for k in range(4):
                rows = slice(c * 64 + k * CH, c * 64 + (k + 1) * CH)
                msg_ref[8 * h + 2 * k + c, 80:96, :] = gate[rows]
    copies[3].wait()
    for h in range(4):
        for c in range(2):
            for k in range(4):
                msg_ref[8 * h + 2 * k + c, 0:64, :] = attn_ref[
                    c * 64 : (c + 1) * 64, h * HD : (h + 1) * HD
                ]
    copies[4].wait()
    for d in range(4):
        col = pl.multiple_of(lax.rem(idx_ref[0] + d, 4) * HD, HD)
        q_refs[d][...] = query_ref[:, pl.ds(col, HD)]


def taps_kernel(idx_ref, taps_hbm, tw_hbm, mh_hbm, ml_hbm, *refs):
    out_ref, taps_ref, buf, tw_ref, mh_ref, ml_ref, sems = refs[-7:]
    col = pl.multiple_of(idx_ref[0] * HD, HD)
    parts = 4
    size = SEQ // parts
    copies = load(
        [
            (
                taps_hbm.at[pl.ds(n * size, size), pl.ds(col, HD)],
                taps_ref.at[pl.ds(n * size, size), :],
            )
            for n in range(parts)
        ]
        + [(tw_hbm, tw_ref), (mh_hbm, mh_ref), (ml_hbm, ml_ref)],
        sems,
    )
    first = idx_ref[1]
    row = lax.broadcasted_iota(jnp.int32, (CH, G), 0)
    lane = lax.broadcasted_iota(jnp.int32, (CH, G), 1)
    pick = jnp.where(lane == row + first, 1.0, 0.0).astype(BF)
    for copy in copies:
        copy.wait()
    blocks = [
        lax.dot_general(pick, taps_ref[i * G : (i + 1) * G, :], NT, preferred_element_type=F32)
        for i in range(NB)
    ]
    out_ref[...] = spectrum(blocks, tw_ref, mh_ref, ml_ref, buf)


def conv_kernel(
    idx_ref, in_ref, spec_ref, skip_ref, tw_ref, mh_ref, ml_ref, nh_ref, nl_ref, out_ref, buf
):
    valid = idx_ref[2]
    blocks = [in_ref[i, 64:80, :].astype(F32) for i in range(NB)]
    x = spectrum(blocks, tw_ref, mh_ref, ml_ref, buf)
    xr, xi, hr, hi = x[:, :G], x[:, G:], spec_ref[:, :G], spec_ref[:, G:]
    buf[:, :G] = xr * hr - xi * hi
    buf[:, G:] = xr * hi + xi * hr
    buf[...] = dot3(buf[...], nh_ref[...], nl_ref[...])
    z = []
    for p in range(NB):
        re, im = buf[p * CH : (p + 1) * CH, :G], buf[p * CH : (p + 1) * CH, G:]
        c, s = tw_ref[0, p : p + 1, :], tw_ref[1, p : p + 1, :]
        z.append((re * c - im * s, im * c + re * s))
    z = fft(z, 1.0)
    row = lax.broadcasted_iota(jnp.int32, (CH, G), 0)
    lane = lax.broadcasted_iota(jnp.int32, (CH, G), 1)
    skip = jnp.zeros((CH, G), F32)
    for r in range(CH):
        skip = jnp.where(row == r, skip_ref[idx_ref[0] * HD + idx_ref[1] + r], skip)
    for i, (re, im) in enumerate(z):
        ang = 2.0 * math.pi * DELTA * i / NB
        y = (re * math.cos(ang) - im * math.sin(ang)) * (1.0 / SEQ)
        y = in_ref[i, 80:96, :].astype(F32) * (y + skip * in_ref[i, 64:80, :].astype(F32))
        out_ref[i] = jnp.where(lane + i * G < valid, y, 0.0).astype(BF)


def weights_kernel(idx_ref, *refs):
    q_refs, own_ref, other_ref, w_ref, total_ref = refs[:8], refs[8], refs[9], refs[10], refs[11]
    qs, keys, scores = refs[12:]
    head, k, core, valid = idx_ref[0], idx_ref[3], idx_ref[4], idx_ref[2]
    flip = core == 1
    for d in range(4):
        own, other = q_refs[d][...], q_refs[4 + d][...]
        qs[d, 0:G] = jnp.where(flip, other, own)
        qs[d, G : 2 * G] = jnp.where(flip, own, other)
    for s in range(NB):
        own, other = own_ref[s, 0:64], other_ref[s, 0:64]
        keys[s * G : s * G + 64] = jnp.where(flip, other, own)
        keys[s * G + 64 : (s + 1) * G] = jnp.where(flip, own, other)
    factor = math.log2(math.e) / math.sqrt(HD)
    row = lax.broadcasted_iota(jnp.int32, (2 * G, G), 0)
    lane = lax.broadcasted_iota(jnp.int32, (2 * G, G), 1)
    for t in range(4):
        q = qs[lax.rem(head + 4 - t, 4)]
        limit = jnp.minimum(row + (8 * t + 2 * k) * G, valid - 1)
        top = None
        for m in range(4 * t + 4):
            s = lax.dot_general(
                q, keys[m * 2 * G : (m + 1) * 2 * G], NT, preferred_element_type=F32
            )
            for u in range(2):
                n = 2 * m + u
                part = s[:, u * G : (u + 1) * G]
                if n >= 8 * t:
                    part = jnp.where(lane + n * G <= limit, part, -1e30)
                scores[:, n * G : (n + 1) * G] = part
                top = part if top is None else jnp.maximum(top, part)
        top = jnp.max(top, axis=1, keepdims=True)
        total = None
        for n in range(8 * t + 8):
            part = jnp.exp2((scores[:, n * G : (n + 1) * G] - top) * factor)
            w_ref[2 * t * G : (2 * t + 2) * G, n * G : (n + 1) * G] = part.astype(BF)
            total = part if total is None else total + part
        total = jnp.sum(total, axis=1, keepdims=True)
        total_ref[2 * t * G : (2 * t + 2) * G, :] = jnp.broadcast_to(total, (2 * G, G))


def values_kernel(idx_ref, w_ref, total_ref, v0, v1, v2, v3, msg_ref, vals):
    k, core = idx_ref[3], idx_ref[4]
    for d, v_ref in enumerate((v0, v1, v2, v3)):
        row = pl.multiple_of(lax.rem(k + 4 - d, 4) * CH, CH)
        for s in range(NB):
            block = v_ref[s]
            vals[pl.ds(row, CH), s * G : (s + 1) * G] = block
            vals[pl.ds(row + 64, CH), s * G : (s + 1) * G] = block
    lane = lax.broadcasted_iota(jnp.int32, (64, G), 1)
    mine = (lane < 64) != (core == 1)
    for t in range(4):
        n = (8 * t + 8) * G
        rows = slice(2 * t * G, (2 * t + 2) * G)
        out = lax.dot_general(w_ref[rows, 0:n], vals[:, 0:n], NT, preferred_element_type=F32)
        out = out / total_ref[rows, :]
        for c in range(2):
            j = 2 * t + c
            a = out[c * G : c * G + 64]
            b = out[c * G + 64 : (c + 1) * G]
            msg_ref[j, 0:64, :] = jnp.where(mine, a, b).astype(BF)
            col = pl.multiple_of((8 * t + 2 * k + c) * G, G)
            msg_ref[j, 64:128, :] = vals[0:64, pl.ds(col, G)]


def gather_kernel(msg_ref, attended_ref, sum_ref):
    left = lax.broadcasted_iota(jnp.int32, (64, G), 1) < 64
    ones = jnp.ones((8, G), BF)
    sums = jnp.zeros((8, G), F32)
    for h in range(4):
        cols = slice(h * HD, (h + 1) * HD)
        p0 = msg_ref[2 * h, 0:64, :].astype(F32)
        p1 = msg_ref[2 * h + 1, 0:64, :].astype(F32)
        low = jnp.where(left, p0, p1)
        high = pltpu.roll(jnp.where(left, p1, p0), 64, 1)
        both = jnp.concatenate([low, high], axis=0)
        attended_ref[:, cols] = both.astype(BF)
        for part in split(both * both):
            sums += lax.dot_general(ones, part, NT, preferred_element_type=F32)
    sum_ref[...] = sums


def hyena_kernel(msg_ref, hyena_ref):
    for h in range(4):
        block = msg_ref[2 * h : 2 * h + 2, 64:128, :].reshape(G, G).astype(F32)
        hyena_ref[:, h * HD : (h + 1) * HD] = block.T.astype(BF)


def final_kernel(idx_ref, attended_ref, sum_ref, attn_ref):
    valid, own = idx_ref[2], idx_ref[5]
    total = jnp.sum(sum_ref[...], axis=0, keepdims=True)
    norm = jnp.sqrt(total * (1.0 / DW) + 1e-06)
    inv = jnp.broadcast_to(1.0 / norm, (G, G)).T
    row = lax.broadcasted_iota(jnp.int32, (G, G), 0)
    inv = jnp.where(row + own * G < valid, inv, 0.0)
    for h in range(4):
        cols = slice(h * HD, (h + 1) * HD)
        attn_ref[:, cols] = (attended_ref[:, cols].astype(F32) * inv).astype(BF)


def sds(shape, dtype):
    return jax.ShapeDtypeStruct(shape, dtype)


VM = pl.BlockSpec(memory_space=pltpu.MemorySpace.VMEM)
SM = pl.BlockSpec(memory_space=pltpu.MemorySpace.SMEM)
AN = pl.BlockSpec(memory_space=pl.ANY)
HB = pl.BlockSpec(memory_space=pltpu.MemorySpace.HBM)


def call(kernel, out_shape, in_specs, scratch=(), out_specs=None, us=1, vmem=16):
    many = isinstance(out_shape, (tuple, list))
    return pl.pallas_call(
        kernel,
        out_shape=out_shape,
        in_specs=in_specs,
        out_specs=out_specs or ([VM] * len(out_shape) if many else VM),
        scratch_shapes=list(scratch),
        compiler_params=pltpu.CompilerParams(vmem_limit_bytes=vmem << 20),
        cost_estimate=pl.CostEstimate(
            flops=int(us * 10**9), bytes_accessed=int(us * 2 * 10**6), transcendentals=0
        ),
    )


def dma(n):
    return pltpu.SemaphoreType.DMA((n,))


def shards(
    hyena_gate, hyena_key, hyena_value, filter_taps, skip_weight, queries, attn_keys, valid_length
):
    own = lax.axis_index("ctx").astype(jnp.int32)
    head = lax.shift_right_logical(own, 3)
    k = lax.bitwise_and(lax.shift_right_logical(own, 1), 3)
    core = lax.bitwise_and(own, 1)
    idx = jnp.stack([head, core * 64 + k * CH, valid_length[0], k, core, own])
    high, low, high_t, low_t, twiddle = (jnp.asarray(t) for t in tables())

    block = pltpu.VMEM((G, 4 * HD), BF)
    msg, *q = call(
        pre_kernel,
        (sds((NB, 96, G), BF),) + (sds((G, HD), BF),) * 4,
        [SM] + [HB] * 5,
        [block] * 5 + [dma(5)],
        vmem=60,
    )(idx, hyena_key, hyena_value, hyena_gate, attn_keys, queries)
    got = lax.all_to_all(msg, "ctx", 0, 0, tiled=True)
    q = [q[0]] + [lax.ppermute(q[d], "ctx", along_y(d)) for d in (1, 2, 3)]
    q += [lax.ppermute(x, "ctx", CORES) for x in q]
    spec = call(
        taps_kernel,
        sds((NB * CH, 2 * G), F32),
        [SM, HB] + [AN] * 10,
        [
            pltpu.VMEM((SEQ, HD), BF),
            pltpu.VMEM((NB * CH, 2 * G), F32),
            pltpu.VMEM((2, NB, G), F32),
            pltpu.VMEM((2 * G, 2 * G), BF),
            pltpu.VMEM((2 * G, 2 * G), BF),
            dma(7),
        ],
        us=2,
        vmem=50,
    )(idx, filter_taps, twiddle, high, low, *q[1:])
    got_other = lax.ppermute(got, "ctx", CORES)
    values = call(
        conv_kernel,
        sds((NB, CH, G), BF),
        [SM, VM, VM, SM] + [VM] * 5,
        [pltpu.VMEM((NB * CH, 2 * G), F32)],
        us=3,
    )(idx, got, spec, skip_weight, twiddle, high, low, high_t, low_t)
    v = [values] + [lax.ppermute(values, "ctx", along_x(d)) for d in (1, 2, 3)]
    weights, totals = call(
        weights_kernel,
        (sds((8 * G, SEQ), BF), sds((8 * G, G), F32)),
        [SM] + [VM] * 8 + [VM] * 2,
        [pltpu.VMEM((4, 2 * G, HD), BF), pltpu.VMEM((SEQ, HD), BF), pltpu.VMEM((2 * G, SEQ), F32)],
        us=4,
    )(idx, *q, got, got_other)
    back = call(
        values_kernel,
        sds((8, G, G), BF),
        [SM] + [VM] * 6,
        [pltpu.VMEM((G, SEQ), BF)],
        us=4,
    )(idx, weights, totals, *v)
    got_back = lax.all_to_all(back, "ctx", 0, 0, tiled=True, axis_index_groups=COLS)
    attended, sums = call(gather_kernel, (sds((G, 4 * HD), BF), sds((8, G), F32)), [VM])(got_back)
    sums = lax.all_to_all(sums, "tp", 0, 0, tiled=True)
    hyena_out = call(hyena_kernel, sds((G, 4 * HD), BF), [VM])(got_back)
    attn_out = call(final_kernel, sds((G, 4 * HD), BF), [SM, VM, VM])(idx, attended, sums)
    return hyena_out, attn_out


def solution(mesh):
    in_specs = (
        P("ctx", "tp"),
        P("ctx", "tp"),
        P("ctx", "tp"),
        P(None, "tp"),
        P("tp"),
        P("ctx", "tp"),
        P("ctx", "tp"),
        P(),
    )
    out_specs = (P("ctx", "tp"), P("ctx", "tp"))
    return jax.shard_map(shards, mesh=mesh, in_specs=in_specs, out_specs=out_specs, check_vma=False)
```

time: 96.9 us -> 84.8 us (0.88)
  blocking collectives: 53.9 us -> 34.1 us
  local copies, waits for them, and re-layouts: 16.8 us -> 3.79 us
  starting transfers between devices: 7.35 us -> 18.1 us
  waiting for transfers between devices: 2.2 us -> 10.1 us
  Pallas kernels: 14.5 us -> 16.8 us
    all_to_all x3 -> x2, blocking collectives: 53.9 us -> 34.1 us  [the longest x1 22.8 us: shards(): got = lax.all_to_all(msg, 'ctx', 0, 0, tiled=True)]
    unnamed x32 -> x20, local copies, waits for them, and re-layouts: 15.9 us -> 3.19 us
    ppermute x0 -> x10, starting transfers between devices: none -> 9.38 us  [the longest x4 3.69 us: shards(): q += [lax.ppermute(x, 'ctx', CORES) for x in q]]
    ppermute x0 -> x10, waiting for transfers between devices: none -> 4.33 us  [the longest x3 3.37 us: shards(): v = [values] + [lax.ppermute(values, 'ctx', along_x(d)) for d in (1, 2, 3)]]
    all_to_all x2 -> x1, waiting for transfers between devices: 2.19 us -> 5.72 us  [shards(): sums = lax.all_to_all(sums, 'tp', 0, 0, tiled=True)]
    pallas_call x6 -> x8, Pallas kernels: 14.5 us -> 16.8 us  [the longest x1 4.04 us: shards(): call(weights_kernel, (sds((8 * G, SEQ), BF), sds((8 * G, G), F32)), [SM]...]
    all_to_all x2 -> x1, starting transfers between devices: 6.83 us -> 8.19 us  [shards(): sums = lax.all_to_all(sums, 'tp', 0, 0, tiled=True)]
  transfers between devices with their start and end apart: 3 -> 12, of which waited for: 1 -> 6; matrix products, arithmetic and copies ran while one was open for 1% -> 0% of each run, Pallas kernels for 9% -> 11%
where the time goes in v2:
time: 84.8 us; the launch traced here: 84.3 us
  blocking collectives  34.1 us (40%)
  starting transfers between devices  18.1 us (21%)
  Pallas kernels  16.8 us (20%)
  waiting for transfers between devices  10.1 us (12%)
  local copies, waits for them, and re-layouts  3.79 us (4%)
  between operations  1.45 us (2%)
    all_to_all x1, blocking collectives, shards(): got = lax.all_to_all(msg, 'ctx', 0, 0, tiled=True)  22.8 us
    all_to_all x1, blocking collectives, shards(): lax.all_to_all(back, 'ctx', 0, 0, tiled=True, axis_index_groups=COLS)  11.2 us
    all_to_all x1, starting transfers between devices, shards(): sums = lax.all_to_all(sums, 'tp', 0, 0, tiled=True)  8.19 us
    all_to_all x1, waiting for transfers between devices, shards(): sums = lax.all_to_all(sums, 'tp', 0, 0, tiled=True)  5.72 us
    pallas_call x1, Pallas kernels, shards(): call(weights_kernel, (sds((8 * G, SEQ), BF), sds((8 * G, G), F32)), [SM]...  4.04 us
    ppermute x4, starting transfers between devices, shards(): q += [lax.ppermute(x, 'ctx', CORES) for x in q]  3.69 us
    ppermute x3, waiting for transfers between devices, shards(): v = [values] + [lax.ppermute(values, 'ctx', along_x(d)) for d in (1, 2, 3)]  3.37 us
    unnamed x20, local copies, waits for them, and re-layouts  3.19 us
  transfers between devices with their start and end apart: 12, of which 6 were waited for; matrix products, arithmetic and copies ran while one was open for 0% of the time, Pallas kernels for 11%

profile of v2, /device:TPU:1, one launch (start us, length us, event | category | flops | bytes accessed | tf_op | source)
XLA Modules:
  0.0 84.3 jit_solution(3570743848032184423)
XLA Ops:
  0.6 0.0 copy-start.9
  0.6 0.0 copy-start.6
  0.7 0.0 copy-start.7
  0.7 0.0 copy-start.3
  1.4 0.6 stack.23.idx_ref
  2.0 2.9 %shard_map.140 = (bf16[32,96,128]{2,1,0:T(8,128)(2,1)}, bf16[128,128]{1,0:T(8,128)(2,1)}, bf16[128,128]{1,0:T(8,128)(2,1)}, bf16[128,128]{1,0:T(8,128)(2,1)}, bf16[128,128]{1,0:T(8,128)(2,1)}) custom-call(s32[6]{0:T(128)} %stack.23.idx_ref, bf16[128,512]{1,0:T(8,128)(2,1)} %key_hbm.1, bf16[128,512]{1,0:T(8,128)(2,1)} %value_hbm.1, ...), custom_call_target="tpu_custom_call" | custom-call | flops 1000000000 | bytes 2000000 | tf_op jit(solution)/shard_map/pallas_call | solution.py:351
  4.9 0.0 copy-start.2
  4.9 22.8 %all_to_all.21.refs_8_.in_ref = bf16[32,96,128]{2,1,0:T(8,128)(2,1)S(1)} all-to-all(bf16[32,96,128]{2,1,0:T(8,128)(2,1)} %get-tuple-element.15), channel_id=1, replica_groups=mesh['ctx'=32,'tp'=8] {'ctx'}, dimensions={0} | all-to-all | bytes 1572864 | tf_op jit(solution)/shard_map/all_to_all | solution.py:358
  27.7 0.5 collective-permute-start.7
  28.2 0.0 collective-permute-start
  28.2 1.6 %collective-permute-start.1 = (bf16[128,128]{1,0:T(8,128)(2,1)}, bf16[128,128]{1,0:T(8,128)(2,1)S(1)}, u32[]{:S(2)}, u32[]{:S(2)}) collective-permute-start(bf16[128,128]{1,0:T(8,128)(2,1)} %get-tuple-element.13), channel_id=1, source_target_pairs={{0,128},{8,136},{16,144},{24,152},{32,160},{40,168},{48,176},{56,1... | collective-permute-start | bytes 98312 | tf_op jit(solution)/shard_map/ppermute | solution.py:359
  29.8 1.2 %collective-permute-start.2 = (bf16[128,128]{1,0:T(8,128)(2,1)}, bf16[128,128]{1,0:T(8,128)(2,1)S(1)}, u32[]{:S(2)}, u32[]{:S(2)}) collective-permute-start(bf16[128,128]{1,0:T(8,128)(2,1)} %get-tuple-element.14), channel_id=1, source_target_pairs={{0,192},{8,200},{16,208},{24,216},{32,224},{40,232},{48,240},{56,2... | collective-permute-start | bytes 98312 | tf_op jit(solution)/shard_map/ppermute | solution.py:359
  31.0 1.3 %collective-permute-start.3 = (bf16[128,128]{1,0:T(8,128)(2,1)}, bf16[128,128]{1,0:T(8,128)(2,1)S(1)}, u32[]{:S(2)}, u32[]{:S(2)}) collective-permute-start(bf16[128,128]{1,0:T(8,128)(2,1)} %get-tuple-element.11.refs_0_), channel_id=1, source_target_pairs={{0,8},{8,0},{16,24},{24,16},{32,40},{40,32},{48,56},{56,48},{64,72... | collective-permute-start | bytes 98312 | tf_op jit(solution)/shard_map/ppermute | solution.py:360
  32.3 0.1 collective-permute-done.refs_1_.refs_0_
  32.4 1.7 %collective-permute-start.4 = (bf16[128,128]{1,0:T(8,128)(2,1)S(1)}, bf16[128,128]{1,0:T(8,128)(2,1)S(1)}, u32[]{:S(2)}, u32[]{:S(2)}) collective-permute-start(bf16[128,128]{1,0:T(8,128)(2,1)S(1)} %collective-permute-done.refs_1_.refs_0_), channel_id=1, source_target_pairs={{0,8},{8,0},{16,24},{24,16},{32,40},{40,32},{48,56},{56,48},{64,72... | collective-permute-start | bytes 98312 | tf_op jit(solution)/shard_map/ppermute | solution.py:360
  34.2 0.0 collective-permute-done.1.refs_2_.refs_1_
  34.2 0.0 collective-permute-start.5
  34.2 0.0 collective-permute-done.2.refs_3_.refs_2_
  34.2 0.6 collective-permute-start.6
  34.8 0.0 collective-permute-done.3.refs_4_.refs_3_
  34.8 0.2 collective-permute-done.4.refs_5_.refs_4_
  35.0 0.4 collective-permute-done.5.refs_6_.refs_5_
  35.4 0.3 collective-permute-done.6.refs_7_.refs_6_
  35.6 0.0 copy-start
  35.6 0.6 copy-done
  36.2 0.0 copy-start.4
  36.2 0.9 %copy-done.4 = bf16[256,256]{1,0:T(8,128)(2,1)S(1)} copy-done((bf16[256,256]{1,0:T(8,128)(2,1)S(1)}, bf16[256,256]{1,0:T(8,128)(2,1)}, u32[]{:S(2)}) %copy-start.4) | copy-done | bytes 131096
  37.1 0.0 copy-start.5
  37.1 0.9 %copy-done.5 = bf16[256,256]{1,0:T(8,128)(2,1)S(1)} copy-done((bf16[256,256]{1,0:T(8,128)(2,1)S(1)}, bf16[256,256]{1,0:T(8,128)(2,1)}, u32[]{:S(2)}) %copy-start.5) | copy-done | bytes 131096
  38.0 0.0 copy-start.8
  38.0 0.8 copy-done.8
  38.8 2.9 %shard_map.142.spec_ref = f32[512,256]{1,0:T(8,128)S(1)} custom-call(s32[6]{0:T(128)S(1)} %copy-done, bf16[4096,512]{1,0:T(8,128)(2,1)} %taps_hbm.1, f32[2,32,128]{2,1,0:T(8,128)S(1)} %copy-done.8, bf16[256,256]{1,0:T(8,128)(2,1)S(1)} %copy-done.4, bf16[256,256]{1,0:T(8,128)(2,1)S(1)} %copy-done.5, ...), custom_call_target="tpu_custom_call" | custom-call | flops 2000000000 | bytes 4000000 | tf_op jit(solution)/shard_map/pallas_call | solution.py:361
  41.7 0.0 copy-done.9
  41.7 0.0 copy-done.6
  41.7 0.0 copy-done.7
  41.7 0.0 copy-done.3
  41.7 1.9 %shard_map.143.v0 = bf16[32,16,128]{2,1,0:T(8,128)(2,1)S(1)} custom-call(s32[6]{0:T(128)S(1)} %copy-done, bf16[32,96,128]{2,1,0:T(8,128)(2,1)S(1)} %all_to_all.21.refs_8_.in_ref, f32[512,256]{1,0:T(8,128)S(1)} %shard_map.142.spec_ref, f32[512]{0:T(512)S(1)} %copy-done.3, f32[2,32,128]{2,1,0:T(8,128)S(1)} %copy-done.9, bf16[256,256]{1,0:T(8,128)(2,1)S(1)} %copy-done.4, ...), custom_call_target="tpu_custom_call" | custom-call | flops 3000000000 | bytes 6000000 | tf_op jit(solution)/shard_map/pallas_call | solution.py:377
  43.6 1.7 %collective-permute-start.10 = (bf16[32,16,128]{2,1,0:T(8,128)(2,1)S(1)}, bf16[32,16,128]{2,1,0:T(8,128)(2,1)S(1)}, u32[]{:S(2)}, u32[]{:S(2)}) collective-permute-start(bf16[32,16,128]{2,1,0:T(8,128)(2,1)S(1)} %shard_map.143.v0), channel_id=1, source_target_pairs={{0,48},{8,56},{16,0},{24,8},{32,16},{40,24},{48,32},{56,40},{64,11... | collective-permute-start | bytes 393224 | tf_op jit(solution)/shard_map/ppermute | solution.py:384
  45.3 0.0 collective-permute-start.8
  45.3 1.3 %collective-permute-start.9 = (bf16[32,16,128]{2,1,0:T(8,128)(2,1)S(1)}, bf16[32,16,128]{2,1,0:T(8,128)(2,1)S(1)}, u32[]{:S(2)}, u32[]{:S(2)}) collective-permute-start(bf16[32,16,128]{2,1,0:T(8,128)(2,1)S(1)} %shard_map.143.v0), channel_id=1, source_target_pairs={{0,32},{8,40},{16,48},{24,56},{32,0},{40,8},{48,16},{56,24},{64,96... | collective-permute-start | bytes 393224 | tf_op jit(solution)/shard_map/ppermute | solution.py:384
  46.6 0.0 collective-permute-done.7.refs_9_
  46.6 0.0 copy-done.2
  46.6 4.0 %shard_map.141 = (bf16[1024,4096]{1,0:T(8,128)(2,1)S(1)}, f32[1024,128]{1,0:T(8,128)S(1)}) custom-call(s32[6]{0:T(128)S(1)} %copy-done, bf16[128,128]{1,0:T(8,128)(2,1)S(1)} %copy-done.2, bf16[128,128]{1,0:T(8,128)(2,1)S(1)} %collective-permute-done.refs_1_.refs_0_, bf16[128,128]{1,0:T(8,128)(2,1)S(1)} %collective-permute-done.1.refs_2_.refs_1_, ...), custom_call_target="tpu_custom_call" | custom-call | flops 4000000000 | bytes 8000000 | tf_op jit(solution)/shard_map/pallas_call | solution.py:385
  50.6 0.0 collective-permute-done.10.v3
  50.6 3.4 %collective-permute-done.8.v1 = bf16[32,16,128]{2,1,0:T(8,128)(2,1)S(1)} collective-permute-done((bf16[32,16,128]{2,1,0:T(8,128)(2,1)S(1)}, bf16[32,16,128]{2,1,0:T(8,128)(2,1)S(1)}, u32[]{:S(2)}, u32[]{:S(2)}) %collective-permute-start.8) | collective-permute-done | bytes 131104 | tf_op jit(solution)/shard_map/ppermute | solution.py:384
  54.0 0.0 collective-permute-done.9.v2
  54.0 0.0 copy-start.1
  54.0 2.1 %shard_map.144 = bf16[8,128,128]{2,1,0:T(8,128)(2,1)S(1)} custom-call(s32[6]{0:T(128)S(1)} %copy-done, bf16[1024,4096]{1,0:T(8,128)(2,1)S(1)} %get-tuple-element.16.w_ref, f32[1024,128]{1,0:T(8,128)S(1)} %get-tuple-element.17.total_ref, bf16[32,16,128]{2,1,0:T(8,128)(2,1)S(1)} %shard_map.143.v0, bf16[32,16,128]{2,1,0:T(8,128)(2,1)S(1)} %collective-permute-done.8.v1, ...), custom_call_target="tpu_custom_call" | custom-call | flops 4000000000 | bytes 8000000 | tf_op jit(solution)/shard_map/pallas_call | solution.py:392
  56.1 11.2 %all_to_all.22.msg_ref = bf16[8,128,128]{2,1,0:T(8,128)(2,1)S(1)} all-to-all(bf16[8,128,128]{2,1,0:T(8,128)(2,1)S(1)} %shard_map.144), channel_id=1, replica_groups={{0,8,64,72,128,136,192,200},{16,24,80,88,144,152,208,216},{32,40,96,104..., dimensions={0} | all-to-all | bytes 524288 | tf_op jit(solution)/shard_map/all_to_all | solution.py:399
  67.4 0.9 %shard_map.146 = (bf16[128,512]{1,0:T(8,128)(2,1)S(1)}, f32[8,128]{1,0:T(8,128)}) custom-call(bf16[8,128,128]{2,1,0:T(8,128)(2,1)S(1)} %all_to_all.22.msg_ref), custom_call_target="tpu_custom_call" | custom-call | flops 1000000000 | bytes 2000000 | tf_op jit(solution)/shard_map/pallas_call | solution.py:400
  68.3 8.2 %all-to-all-start.2 = ((f32[8,1,128]{2,1,0:T(1,128)}), f32[8,1,128]{2,1,0:T(1,128)S(1)}, u32[]{:S(2)}, u32[]{:S(2)}) async-start(f32[8,1,128]{2,1,0:T(1,128)} %bitcast.6), calls=%async_computation.2 | async-start | bytes 8192 | tf_op jit(solution)/shard_map/all_to_all | solution.py:401
  76.5 0.8 shard_map.145
  77.2 5.7 %all-to-all-done.2 = f32[8,1,128]{2,1,0:T(1,128)S(1)} async-done(((f32[8,1,128]{2,1,0:T(1,128)}), f32[8,1,128]{2,1,0:T(1,128)S(1)}, u32[]{:S(2)}, u32[]{:S(2)}) %all-to-all-start.2) | async-done | bytes 4128 | tf_op jit(solution)/shard_map/all_to_all | solution.py:401
  83.0 0.0 copy-done.1
  83.0 1.3 %shard_map.147 = bf16[128,512]{1,0:T(8,128)(2,1)} custom-call(s32[6]{0:T(128)S(1)} %copy-done.1, bf16[128,512]{1,0:T(8,128)(2,1)S(1)} %get-tuple-element.18.attended_ref, f32[8,128]{1,0:T(8,128)S(1)} %bitcast.9), custom_call_target="tpu_custom_call" | custom-call | flops 1000000000 | bytes 2000000 | tf_op jit(solution)/shard_map/pallas_call | solution.py:403
Async XLA Ops:
  0.6 41.1 %copy-start.9 = (f32[2,32,128]{2,1,0:T(8,128)S(1)}, f32[2,32,128]{2,1,0:T(8,128)}, u32[]{:S(2)}) copy-start(f32[2,32,128]{2,1,0:T(8,128)} %constant.28.clone.tw_hbm.tw_ref) | copy-start | bytes 98308
  0.6 41.1 %copy-start.6 = (bf16[256,256]{1,0:T(8,128)(2,1)S(1)}, bf16[256,256]{1,0:T(8,128)(2,1)}, u32[]{:S(2)}) copy-start(bf16[256,256]{1,0:T(8,128)(2,1)} %constant.26.clone.nh_ref) | copy-start | bytes 393220
  0.7 41.0 %copy-start.7 = (bf16[256,256]{1,0:T(8,128)(2,1)S(1)}, bf16[256,256]{1,0:T(8,128)(2,1)}, u32[]{:S(2)}) copy-start(bf16[256,256]{1,0:T(8,128)(2,1)} %constant.27.clone.nl_ref) | copy-start | bytes 393220
  0.7 41.0 %copy-start.3 = (f32[512]{0:T(512)S(1)}, f32[512]{0:T(512)}, u32[]{:S(2)}) copy-start(f32[512]{0:T(512)} %skip_ref.1) | copy-start | bytes 6148
  4.9 41.7 %copy-start.2 = (bf16[128,128]{1,0:T(8,128)(2,1)S(1)}, bf16[128,128]{1,0:T(8,128)(2,1)}, u32[]{:S(2)}) copy-start(bf16[128,128]{1,0:T(8,128)(2,1)} %get-tuple-element.11.refs_0_) | copy-start | bytes 98308
  27.7 18.9 %collective-permute-start.7 = (bf16[32,96,128]{2,1,0:T(8,128)(2,1)S(1)}, bf16[32,96,128]{2,1,0:T(8,128)(2,1)S(1)}, u32[]{:S(2)}, u32[]{:S(2)}) collective-permute-start(bf16[32,96,128]{2,1,0:T(8,128)(2,1)S(1)} %all_to_all.21.refs_8_.in_ref), channel_id=1, source_target_pairs={{0,8},{8,0},{16,24},{24,16},{32,40},{40,32},{48,56},{56,48},{64,72... | collective-permute-start | bytes 2359304 | tf_op jit(solution)/shard_map/ppermute | solution.py:376
  28.2 4.2 %collective-permute-start = (bf16[128,128]{1,0:T(8,128)(2,1)}, bf16[128,128]{1,0:T(8,128)(2,1)S(1)}, u32[]{:S(2)}, u32[]{:S(2)}) collective-permute-start(bf16[128,128]{1,0:T(8,128)(2,1)} %get-tuple-element.12), channel_id=1, source_target_pairs={{0,64},{8,72},{16,80},{24,88},{32,96},{40,104},{48,112},{56,120},{... | collective-permute-start | bytes 98312 | tf_op jit(solution)/shard_map/ppermute | solution.py:359
  28.2 5.9 %collective-permute-start.1 = (bf16[128,128]{1,0:T(8,128)(2,1)}, bf16[128,128]{1,0:T(8,128)(2,1)S(1)}, u32[]{:S(2)}, u32[]{:S(2)}) collective-permute-start(bf16[128,128]{1,0:T(8,128)(2,1)} %get-tuple-element.13), channel_id=1, source_target_pairs={{0,128},{8,136},{16,144},{24,152},{32,160},{40,168},{48,176},{56,1... | collective-permute-start | bytes 98312 | tf_op jit(solution)/shard_map/ppermute | solution.py:359
  29.8 4.4 %collective-permute-start.2 = (bf16[128,128]{1,0:T(8,128)(2,1)}, bf16[128,128]{1,0:T(8,128)(2,1)S(1)}, u32[]{:S(2)}, u32[]{:S(2)}) collective-permute-start(bf16[128,128]{1,0:T(8,128)(2,1)} %get-tuple-element.14), channel_id=1, source_target_pairs={{0,192},{8,200},{16,208},{24,216},{32,224},{40,232},{48,240},{56,2... | collective-permute-start | bytes 98312 | tf_op jit(solution)/shard_map/ppermute | solution.py:359
  31.0 3.8 %collective-permute-start.3 = (bf16[128,128]{1,0:T(8,128)(2,1)}, bf16[128,128]{1,0:T(8,128)(2,1)S(1)}, u32[]{:S(2)}, u32[]{:S(2)}) collective-permute-start(bf16[128,128]{1,0:T(8,128)(2,1)} %get-tuple-element.11.refs_0_), channel_id=1, source_target_pairs={{0,8},{8,0},{16,24},{24,16},{32,40},{40,32},{48,56},{56,48},{64,72... | collective-permute-start | bytes 98312 | tf_op jit(solution)/shard_map/ppermute | solution.py:360
  32.4 2.6 %collective-permute-start.4 = (bf16[128,128]{1,0:T(8,128)(2,1)S(1)}, bf16[128,128]{1,0:T(8,128)(2,1)S(1)}, u32[]{:S(2)}, u32[]{:S(2)}) collective-permute-start(bf16[128,128]{1,0:T(8,128)(2,1)S(1)} %collective-permute-done.refs_1_.refs_0_), channel_id=1, source_target_pairs={{0,8},{8,0},{16,24},{24,16},{32,40},{40,32},{48,56},{56,48},{64,72... | collective-permute-start | bytes 98312 | tf_op jit(solution)/shard_map/ppermute | solution.py:360
  34.2 1.2 %collective-permute-start.5 = (bf16[128,128]{1,0:T(8,128)(2,1)S(1)}, bf16[128,128]{1,0:T(8,128)(2,1)S(1)}, u32[]{:S(2)}, u32[]{:S(2)}) collective-permute-start(bf16[128,128]{1,0:T(8,128)(2,1)S(1)} %collective-permute-done.1.refs_2_.refs_1_), channel_id=1, source_target_pairs={{0,8},{8,0},{16,24},{24,16},{32,40},{40,32},{48,56},{56,48},{64,72... | collective-permute-start | bytes 98312 | tf_op jit(solution)/shard_map/ppermute | solution.py:360
  34.2 1.5 %collective-permute-start.6 = (bf16[128,128]{1,0:T(8,128)(2,1)S(1)}, bf16[128,128]{1,0:T(8,128)(2,1)S(1)}, u32[]{:S(2)}, u32[]{:S(2)}) collective-permute-start(bf16[128,128]{1,0:T(8,128)(2,1)S(1)} %collective-permute-done.2.refs_3_.refs_2_), channel_id=1, source_target_pairs={{0,8},{8,0},{16,24},{24,16},{32,40},{40,32},{48,56},{56,48},{64,72... | collective-permute-start | bytes 98312 | tf_op jit(solution)/shard_map/ppermute | solution.py:360
  35.6 0.6 copy-start
  36.2 0.9 %copy-start.4 = (bf16[256,256]{1,0:T(8,128)(2,1)S(1)}, bf16[256,256]{1,0:T(8,128)(2,1)}, u32[]{:S(2)}) copy-start(bf16[256,256]{1,0:T(8,128)(2,1)} %constant.24.clone.mh_hbm.mh_ref) | copy-start | bytes 393220
  37.1 0.9 %copy-start.5 = (bf16[256,256]{1,0:T(8,128)(2,1)S(1)}, bf16[256,256]{1,0:T(8,128)(2,1)}, u32[]{:S(2)}) copy-start(bf16[256,256]{1,0:T(8,128)(2,1)} %constant.25.clone.ml_hbm.ml_ref) | copy-start | bytes 393220
  38.0 0.8 copy-start.8
  43.6 7.0 %collective-permute-start.10 = (bf16[32,16,128]{2,1,0:T(8,128)(2,1)S(1)}, bf16[32,16,128]{2,1,0:T(8,128)(2,1)S(1)}, u32[]{:S(2)}, u32[]{:S(2)}) collective-permute-start(bf16[32,16,128]{2,1,0:T(8,128)(2,1)S(1)} %shard_map.143.v0), channel_id=1, source_target_pairs={{0,48},{8,56},{16,0},{24,8},{32,16},{40,24},{48,32},{56,40},{64,11... | collective-permute-start | bytes 393224 | tf_op jit(solution)/shard_map/ppermute | solution.py:384
  45.3 8.7 %collective-permute-start.8 = (bf16[32,16,128]{2,1,0:T(8,128)(2,1)S(1)}, bf16[32,16,128]{2,1,0:T(8,128)(2,1)S(1)}, u32[]{:S(2)}, u32[]{:S(2)}) collective-permute-start(bf16[32,16,128]{2,1,0:T(8,128)(2,1)S(1)} %shard_map.143.v0), channel_id=1, source_target_pairs={{0,16},{8,24},{16,32},{24,40},{32,48},{40,56},{48,0},{56,8},{64,80... | collective-permute-start | bytes 393224 | tf_op jit(solution)/shard_map/ppermute | solution.py:384
  45.3 8.7 %collective-permute-start.9 = (bf16[32,16,128]{2,1,0:T(8,128)(2,1)S(1)}, bf16[32,16,128]{2,1,0:T(8,128)(2,1)S(1)}, u32[]{:S(2)}, u32[]{:S(2)}) collective-permute-start(bf16[32,16,128]{2,1,0:T(8,128)(2,1)S(1)} %shard_map.143.v0), channel_id=1, source_target_pairs={{0,32},{8,40},{16,48},{24,56},{32,0},{40,8},{48,16},{56,24},{64,96... | collective-permute-start | bytes 393224 | tf_op jit(solution)/shard_map/ppermute | solution.py:384
  54.0 29.0 %copy-start.1 = (s32[6]{0:T(128)S(1)}, s32[6]{0:T(128)}, u32[]{:S(2)}) copy-start(s32[6]{0:T(128)} %stack.23.idx_ref) | copy-start | bytes 76
  68.3 14.7 %all-to-all-start.2 = ((f32[8,1,128]{2,1,0:T(1,128)}), f32[8,1,128]{2,1,0:T(1,128)S(1)}, u32[]{:S(2)}, u32[]{:S(2)}) async-start(f32[8,1,128]{2,1,0:T(1,128)} %bitcast.6), calls=%async_computation.2 | async-start | bytes 8192 | tf_op jit(solution)/shard_map/all_to_all | solution.py:401

commit v3 on v2

--- a/solution.py
+++ b/solution.py
@@ -99,6 +99,12 @@
     return dot3(buf[...], mh_ref[...], ml_ref[...])
 
 
+def place():
+    own = lax.axis_index("ctx").astype(jnp.int32)
+    k = lax.bitwise_and(lax.shift_right_logical(own, 1), 3)
+    return own, lax.shift_right_logical(own, 3), k, lax.bitwise_and(own, 1)
+
+
 def load(pairs, sems):
     copies = [pltpu.make_async_copy(a, b, sems.at[n]) for n, (a, b) in enumerate(pairs)]
     for copy in copies:
@@ -106,7 +112,7 @@
     return copies
 
 
-def pre_kernel(idx_ref, key_hbm, value_hbm, gate_hbm, attn_hbm, query_hbm, *refs):
+def pre_kernel(key_hbm, value_hbm, gate_hbm, attn_hbm, query_hbm, *refs):
     msg_ref, q_refs, (key_ref, value_ref, gate_ref, attn_ref, query_ref, sems) = (
         refs[0],
         refs[1:5],
@@ -146,14 +152,17 @@
                     c * 64 : (c + 1) * 64, h * HD : (h + 1) * HD
                 ]
     copies[4].wait()
+    head = place()[1]
     for d in range(4):
-        col = pl.multiple_of(lax.rem(idx_ref[0] + d, 4) * HD, HD)
+        col = pl.multiple_of(lax.rem(head + d, 4) * HD, HD)
         q_refs[d][...] = query_ref[:, pl.ds(col, HD)]
 
 
-def taps_kernel(idx_ref, taps_hbm, tw_hbm, mh_hbm, ml_hbm, *refs):
-    out_ref, taps_ref, buf, tw_ref, mh_ref, ml_ref, sems = refs[-7:]
-    col = pl.multiple_of(idx_ref[0] * HD, HD)
+def taps_kernel(
+    taps_hbm, tw_hbm, mh_hbm, ml_hbm, out_ref, taps_ref, buf, tw_ref, mh_ref, ml_ref, sems
+):
+    _, head, k, core = place()
+    col = pl.multiple_of(head * HD, HD)
     parts = 4
     size = SEQ // parts
     copies = load(
@@ -167,7 +176,7 @@
         + [(tw_hbm, tw_ref), (mh_hbm, mh_ref), (ml_hbm, ml_ref)],
         sems,
     )
-    first = idx_ref[1]
+    first = core * 64 + k * CH
     row = lax.broadcasted_iota(jnp.int32, (CH, G), 0)
     lane = lax.broadcasted_iota(jnp.int32, (CH, G), 1)
     pick = jnp.where(lane == row + first, 1.0, 0.0).astype(BF)
@@ -181,9 +190,10 @@
 
 
 def conv_kernel(
-    idx_ref, in_ref, spec_ref, skip_ref, tw_ref, mh_ref, ml_ref, nh_ref, nl_ref, out_ref, buf
+    valid_ref, in_ref, spec_ref, skip_ref, tw_ref, mh_ref, ml_ref, nh_ref, nl_ref, out_ref, buf
 ):
-    valid = idx_ref[2]
+    valid = valid_ref[0]
+    _, head, k, core = place()
     blocks = [in_ref[i, 64:80, :].astype(F32) for i in range(NB)]
     x = spectrum(blocks, tw_ref, mh_ref, ml_ref, buf)
     xr, xi, hr, hi = x[:, :G], x[:, G:], spec_ref[:, :G], spec_ref[:, G:]
@@ -200,7 +210,7 @@
     lane = lax.broadcasted_iota(jnp.int32, (CH, G), 1)
     skip = jnp.zeros((CH, G), F32)
     for r in range(CH):
-        skip = jnp.where(row == r, skip_ref[idx_ref[0] * HD + idx_ref[1] + r], skip)
+        skip = jnp.where(row == r, skip_ref[head * HD + core * 64 + k * CH + r], skip)
     for i, (re, im) in enumerate(z):
         ang = 2.0 * math.pi * DELTA * i / NB
         y = (re * math.cos(ang) - im * math.sin(ang)) * (1.0 / SEQ)
@@ -208,10 +218,11 @@
         out_ref[i] = jnp.where(lane + i * G < valid, y, 0.0).astype(BF)
 
 
-def weights_kernel(idx_ref, *refs):
+def weights_kernel(valid_ref, *refs):
     q_refs, own_ref, other_ref, w_ref, total_ref = refs[:8], refs[8], refs[9], refs[10], refs[11]
     qs, keys, scores = refs[12:]
-    head, k, core, valid = idx_ref[0], idx_ref[3], idx_ref[4], idx_ref[2]
+    _, head, k, core = place()
+    valid = valid_ref[0]
     flip = core == 1
     for d in range(4):
         own, other = q_refs[d][...], q_refs[4 + d][...]
@@ -249,8 +260,8 @@
         total_ref[2 * t * G : (2 * t + 2) * G, :] = jnp.broadcast_to(total, (2 * G, G))
 
 
-def values_kernel(idx_ref, w_ref, total_ref, v0, v1, v2, v3, msg_ref, vals):
-    k, core = idx_ref[3], idx_ref[4]
+def values_kernel(w_ref, total_ref, v0, v1, v2, v3, msg_ref, vals):
+    _, _, k, core = place()
     for d, v_ref in enumerate((v0, v1, v2, v3)):
         row = pl.multiple_of(lax.rem(k + 4 - d, 4) * CH, CH)
         for s in range(NB):
@@ -296,8 +307,8 @@
         hyena_ref[:, h * HD : (h + 1) * HD] = block.T.astype(BF)
 
 
-def final_kernel(idx_ref, attended_ref, sum_ref, attn_ref):
-    valid, own = idx_ref[2], idx_ref[5]
+def final_kernel(valid_ref, attended_ref, sum_ref, attn_ref):
+    valid, own = valid_ref[0], place()[0]
     total = jnp.sum(sum_ref[...], axis=0, keepdims=True)
     norm = jnp.sqrt(total * (1.0 / DW) + 1e-06)
     inv = jnp.broadcast_to(1.0 / norm, (G, G)).T
@@ -340,28 +351,23 @@
 def shards(
     hyena_gate, hyena_key, hyena_value, filter_taps, skip_weight, queries, attn_keys, valid_length
 ):
-    own = lax.axis_index("ctx").astype(jnp.int32)
-    head = lax.shift_right_logical(own, 3)
-    k = lax.bitwise_and(lax.shift_right_logical(own, 1), 3)
-    core = lax.bitwise_and(own, 1)
-    idx = jnp.stack([head, core * 64 + k * CH, valid_length[0], k, core, own])
     high, low, high_t, low_t, twiddle = (jnp.asarray(t) for t in tables())
 
     block = pltpu.VMEM((G, 4 * HD), BF)
     msg, *q = call(
         pre_kernel,
         (sds((NB, 96, G), BF),) + (sds((G, HD), BF),) * 4,
-        [SM] + [HB] * 5,
+        [HB] * 5,
         [block] * 5 + [dma(5)],
         vmem=60,
-    )(idx, hyena_key, hyena_value, hyena_gate, attn_keys, queries)
+    )(hyena_key, hyena_value, hyena_gate, attn_keys, queries)
     got = lax.all_to_all(msg, "ctx", 0, 0, tiled=True)
     q = [q[0]] + [lax.ppermute(q[d], "ctx", along_y(d)) for d in (1, 2, 3)]
     q += [lax.ppermute(x, "ctx", CORES) for x in q]
     spec = call(
         taps_kernel,
         sds((NB * CH, 2 * G), F32),
-        [SM, HB] + [AN] * 10,
+        [HB] + [AN] * 3,
         [
             pltpu.VMEM((SEQ, HD), BF),
             pltpu.VMEM((NB * CH, 2 * G), F32),
@@ -372,7 +378,7 @@
         ],
         us=2,
         vmem=50,
-    )(idx, filter_taps, twiddle, high, low, *q[1:])
+    )(filter_taps, twiddle, high, low)
     got_other = lax.ppermute(got, "ctx", CORES)
     values = call(
         conv_kernel,
@@ -380,7 +386,7 @@
         [SM, VM, VM, SM] + [VM] * 5,
         [pltpu.VMEM((NB * CH, 2 * G), F32)],
         us=3,
-    )(idx, got, spec, skip_weight, twiddle, high, low, high_t, low_t)
+    )(valid_length, got, spec, skip_weight, twiddle, high, low, high_t, low_t)
     v = [values] + [lax.ppermute(values, "ctx", along_x(d)) for d in (1, 2, 3)]
     weights, totals = call(
         weights_kernel,
@@ -388,19 +394,19 @@
         [SM] + [VM] * 8 + [VM] * 2,
         [pltpu.VMEM((4, 2 * G, HD), BF), pltpu.VMEM((SEQ, HD), BF), pltpu.VMEM((2 * G, SEQ), F32)],
         us=4,
-    )(idx, *q, got, got_other)
+    )(valid_length, *q, got, got_other)
     back = call(
         values_kernel,
         sds((8, G, G), BF),
-        [SM] + [VM] * 6,
+        [VM] * 6,
         [pltpu.VMEM((G, SEQ), BF)],
         us=4,
-    )(idx, weights, totals, *v)
+    )(weights, totals, *v)
     got_back = lax.all_to_all(back, "ctx", 0, 0, tiled=True, axis_index_groups=COLS)
     attended, sums = call(gather_kernel, (sds((G, 4 * HD), BF), sds((8, G), F32)), [VM])(got_back)
     sums = lax.all_to_all(sums, "tp", 0, 0, tiled=True)
     hyena_out = call(hyena_kernel, sds((G, 4 * HD), BF), [VM])(got_back)
-    attn_out = call(final_kernel, sds((G, 4 * HD), BF), [SM, VM, VM])(idx, attended, sums)
+    attn_out = call(final_kernel, sds((G, 4 * HD), BF), [SM, VM, VM])(valid_length, attended, sums)
     return hyena_out, attn_out
 
 

time: 84.8 us -> 77.9 us (0.919)
  Pallas kernels: 16.8 us -> 14 us
  waiting for transfers between devices: 10.1 us -> 8.12 us
  starting transfers between devices: 18.1 us -> 16.2 us
  local copies, waits for them, and re-layouts: 3.79 us -> 2.59 us
  blocking collectives: 34.1 us -> 35.2 us
    pallas_call x4, Pallas kernels: 9.22 us -> 6.96 us  [the longest x1 2.33 us: shards(): call(taps_kernel, sds((NB * CH, 2 * G), F32), [HB] + [AN] * 3, [pltpu.VME...]
    ppermute x4, starting transfers between devices: 3.69 us -> 2.04 us  [shards(): q += [lax.ppermute(x, 'ctx', CORES) for x in q]]
    all_to_all x1, blocking collectives: 11.2 us -> 12.4 us  [shards(): lax.all_to_all(back, 'ctx', 0, 0, tiled=True, axis_index_groups=COLS)]
    ppermute x3, waiting for transfers between devices: 3.37 us -> 2.37 us  [shards(): v = [values] + [lax.ppermute(values, 'ctx', along_x(d)) for d in (1, 2, 3)]]
    unnamed x20 -> x14, local copies, waits for them, and re-layouts: 3.19 us -> 2.59 us
  transfers between devices with their start and end apart: 12 -> 12, of which waited for: 6 -> 3; matrix products, arithmetic and copies ran while one was open for 0% -> 0% of each run, Pallas kernels for 11% -> 11%
where the time goes in v3:
time: 77.9 us; the launch traced here: 77.5 us
  blocking collectives  35.2 us (45%)
  starting transfers between devices  16.2 us (21%)
  Pallas kernels  14 us (18%)
  waiting for transfers between devices  8.12 us (10%)
  local copies, waits for them, and re-layouts  2.59 us (3%)
  between operations  1.38 us (2%)
    all_to_all x1, blocking collectives, shards(): got = lax.all_to_all(msg, 'ctx', 0, 0, tiled=True)  22.8 us
    all_to_all x1, blocking collectives, shards(): lax.all_to_all(back, 'ctx', 0, 0, tiled=True, axis_index_groups=COLS)  12.4 us
    all_to_all x1, starting transfers between devices, shards(): sums = lax.all_to_all(sums, 'tp', 0, 0, tiled=True)  8.19 us
    all_to_all x1, waiting for transfers between devices, shards(): sums = lax.all_to_all(sums, 'tp', 0, 0, tiled=True)  5.72 us
    pallas_call x1, Pallas kernels, shards(): call(weights_kernel, (sds((8 * G, SEQ), BF), sds((8 * G, G), F32)), [SM]...  3.52 us
    ppermute x3, starting transfers between devices, shards(): q = [q[0]] + [lax.ppermute(q[d], 'ctx', along_y(d)) for d in (1, 2, 3)]  2.75 us
    ppermute x3, starting transfers between devices, shards(): v = [values] + [lax.ppermute(values, 'ctx', along_x(d)) for d in (1, 2, 3)]  2.7 us
    unnamed x14, local copies, waits for them, and re-layouts  2.59 us
  transfers between devices with their start and end apart: 12, of which 3 were waited for; matrix products, arithmetic and copies ran while one was open for 0% of the time, Pallas kernels for 11%

profile of v3, /device:TPU:1, one launch (start us, length us, event | category | flops | bytes accessed | tf_op | source)
XLA Modules:
  0.0 77.5 jit_solution(9296416550625138870)
XLA Ops:
  0.6 0.0 copy-start.4
  0.6 0.0 copy-start.5
  0.7 0.0 copy-start.1
  0.7 2.2 %shard_map.140 = (bf16[32,96,128]{2,1,0:T(8,128)(2,1)}, bf16[128,128]{1,0:T(8,128)(2,1)}, bf16[128,128]{1,0:T(8,128)(2,1)}, bf16[128,128]{1,0:T(8,128)(2,1)}, bf16[128,128]{1,0:T(8,128)(2,1)}) custom-call(bf16[128,512]{1,0:T(8,128)(2,1)} %key_hbm.1, bf16[128,512]{1,0:T(8,128)(2,1)} %value_hbm.1, bf16[128,512]{1,0:T(8,128)(2,1)} %gate_hbm.1, ...), custom_call_target="tpu_custom_call" | custom-call | flops 1000000000 | bytes 2000000 | tf_op jit(solution)/shard_map/pallas_call | solution.py:357
  2.9 22.8 %all_to_all.21.refs_8_.in_ref = bf16[32,96,128]{2,1,0:T(8,128)(2,1)S(1)} all-to-all(bf16[32,96,128]{2,1,0:T(8,128)(2,1)} %get-tuple-element.15), channel_id=1, replica_groups=mesh['ctx'=32,'tp'=8] {'ctx'}, dimensions={0} | all-to-all | bytes 1572864 | tf_op jit(solution)/shard_map/all_to_all | solution.py:364
  25.7 0.5 collective-permute-start.7
  26.3 0.0 collective-permute-start
  26.3 1.6 %collective-permute-start.1 = (bf16[128,128]{1,0:T(8,128)(2,1)}, bf16[128,128]{1,0:T(8,128)(2,1)S(1)}, u32[]{:S(2)}, u32[]{:S(2)}) collective-permute-start(bf16[128,128]{1,0:T(8,128)(2,1)} %get-tuple-element.13), channel_id=1, source_target_pairs={{0,128},{8,136},{16,144},{24,152},{32,160},{40,168},{48,176},{56,1... | collective-permute-start | bytes 98312 | tf_op jit(solution)/shard_map/ppermute | solution.py:365
  27.8 1.2 %collective-permute-start.2 = (bf16[128,128]{1,0:T(8,128)(2,1)}, bf16[128,128]{1,0:T(8,128)(2,1)S(1)}, u32[]{:S(2)}, u32[]{:S(2)}) collective-permute-start(bf16[128,128]{1,0:T(8,128)(2,1)} %get-tuple-element.14), channel_id=1, source_target_pairs={{0,192},{8,200},{16,208},{24,216},{32,224},{40,232},{48,240},{56,2... | collective-permute-start | bytes 98312 | tf_op jit(solution)/shard_map/ppermute | solution.py:365
  29.0 0.0 copy-start
  29.0 1.3 %collective-permute-start.3 = (bf16[128,128]{1,0:T(8,128)(2,1)}, bf16[128,128]{1,0:T(8,128)(2,1)S(1)}, u32[]{:S(2)}, u32[]{:S(2)}) collective-permute-start(bf16[128,128]{1,0:T(8,128)(2,1)} %get-tuple-element.11.refs_0_), channel_id=1, source_target_pairs={{0,8},{8,0},{16,24},{24,16},{32,40},{40,32},{48,56},{56,48},{64,72... | collective-permute-start | bytes 98312 | tf_op jit(solution)/shard_map/ppermute | solution.py:366
  30.4 0.0 copy-start.2
  30.4 0.9 %copy-done.2 = bf16[256,256]{1,0:T(8,128)(2,1)S(1)} copy-done((bf16[256,256]{1,0:T(8,128)(2,1)S(1)}, bf16[256,256]{1,0:T(8,128)(2,1)}, u32[]{:S(2)}) %copy-start.2) | copy-done | bytes 131096
  31.3 0.0 copy-start.3
  31.3 0.9 %copy-done.3 = bf16[256,256]{1,0:T(8,128)(2,1)S(1)} copy-done((bf16[256,256]{1,0:T(8,128)(2,1)S(1)}, bf16[256,256]{1,0:T(8,128)(2,1)}, u32[]{:S(2)}) %copy-start.3) | copy-done | bytes 131096
  32.2 0.0 copy-start.6
  32.2 0.8 copy-done.6
  32.9 2.3 %shard_map.142.spec_ref = f32[512,256]{1,0:T(8,128)S(1)} custom-call(bf16[4096,512]{1,0:T(8,128)(2,1)} %taps_hbm.1, f32[2,32,128]{2,1,0:T(8,128)S(1)} %copy-done.6, bf16[256,256]{1,0:T(8,128)(2,1)S(1)} %copy-done.2, bf16[256,256]{1,0:T(8,128)(2,1)S(1)} %copy-done.3), custom_call_target="tpu_custom_call" | custom-call | flops 2000000000 | bytes 4000000 | tf_op jit(solution)/shard_map/pallas_call | solution.py:367
  35.9 0.0 collective-permute-done.refs_1_
  35.9 0.1 collective-permute-start.4
  36.0 0.0 collective-permute-done.1.refs_2_
  36.0 0.5 collective-permute-start.5
  36.5 0.0 collective-permute-done.2.refs_3_
  36.5 0.1 collective-permute-start.6
  36.6 0.0 copy-done.4
  36.6 0.0 copy-done.5
  36.6 0.0 copy-done.1
  36.6 1.9 %shard_map.143.v0 = bf16[32,16,128]{2,1,0:T(8,128)(2,1)S(1)} custom-call(s32[1]{0:T(128)S(6)} %copy.16.valid_ref, bf16[32,96,128]{2,1,0:T(8,128)(2,1)S(1)} %all_to_all.21.refs_8_.in_ref, f32[512,256]{1,0:T(8,128)S(1)} %shard_map.142.spec_ref, f32[512]{0:T(512)S(1)} %copy-done.1, f32[2,32,128]{2,1,0:T(8,128)S(1)} %copy-done.6, ...), custom_call_target="tpu_custom_call" | custom-call | flops 3000000000 | bytes 6000000 | tf_op jit(solution)/shard_map/pallas_call | solution.py:383
  38.5 0.0 collective-permute-done.3.refs_4_
  38.6 0.7 collective-permute-start.10
  39.2 0.0 collective-permute-done.4.refs_5_
  39.2 0.9 %collective-permute-start.8 = (bf16[32,16,128]{2,1,0:T(8,128)(2,1)S(1)}, bf16[32,16,128]{2,1,0:T(8,128)(2,1)S(1)}, u32[]{:S(2)}, u32[]{:S(2)}) collective-permute-start(bf16[32,16,128]{2,1,0:T(8,128)(2,1)S(1)} %shard_map.143.v0), channel_id=1, source_target_pairs={{0,16},{8,24},{16,32},{24,40},{32,48},{40,56},{48,0},{56,8},{64,80... | collective-permute-start | bytes 393224 | tf_op jit(solution)/shard_map/ppermute | solution.py:390
  40.1 0.0 collective-permute-done.5.refs_6_
  40.1 1.2 %collective-permute-start.9 = (bf16[32,16,128]{2,1,0:T(8,128)(2,1)S(1)}, bf16[32,16,128]{2,1,0:T(8,128)(2,1)S(1)}, u32[]{:S(2)}, u32[]{:S(2)}) collective-permute-start(bf16[32,16,128]{2,1,0:T(8,128)(2,1)S(1)} %shard_map.143.v0), channel_id=1, source_target_pairs={{0,32},{8,40},{16,48},{24,56},{32,0},{40,8},{48,16},{56,24},{64,96... | collective-permute-start | bytes 393224 | tf_op jit(solution)/shard_map/ppermute | solution.py:390
  41.3 0.0 collective-permute-done.6.refs_7_
  41.3 0.0 collective-permute-done.7.refs_9_
  41.3 0.0 copy-done
  41.3 3.5 %shard_map.141 = (bf16[1024,4096]{1,0:T(8,128)(2,1)S(1)}, f32[1024,128]{1,0:T(8,128)S(1)}) custom-call(s32[1]{0:T(128)S(6)} %copy.16.valid_ref, bf16[128,128]{1,0:T(8,128)(2,1)S(1)} %copy-done, bf16[128,128]{1,0:T(8,128)(2,1)S(1)} %collective-permute-done.refs_1_, bf16[128,128]{1,0:T(8,128)(2,1)S(1)} %collective-permute-done.1.refs_2_, ...), custom_call_target="tpu_custom_call" | custom-call | flops 4000000000 | bytes 8000000 | tf_op jit(solution)/shard_map/pallas_call | solution.py:391
  44.8 0.0 collective-permute-done.10.v3
  44.8 0.5 collective-permute-done.8.v1
  45.3 1.9 %collective-permute-done.9.v2 = bf16[32,16,128]{2,1,0:T(8,128)(2,1)S(1)} collective-permute-done((bf16[32,16,128]{2,1,0:T(8,128)(2,1)S(1)}, bf16[32,16,128]{2,1,0:T(8,128)(2,1)S(1)}, u32[]{:S(2)}, u32[]{:S(2)}) %collective-permute-start.9) | collective-permute-done | bytes 131104 | tf_op jit(solution)/shard_map/ppermute | solution.py:390
  47.2 1.6 %shard_map.144 = bf16[8,128,128]{2,1,0:T(8,128)(2,1)S(1)} custom-call(bf16[1024,4096]{1,0:T(8,128)(2,1)S(1)} %get-tuple-element.16.w_ref, f32[1024,128]{1,0:T(8,128)S(1)} %get-tuple-element.17.total_ref, bf16[32,16,128]{2,1,0:T(8,128)(2,1)S(1)} %shard_map.143.v0, bf16[32,16,128]{2,1,0:T(8,128)(2,1)S(1)} %collective-permute-done.8.v1, ...), custom_call_target="tpu_custom_call" | custom-call | flops 4000000000 | bytes 8000000 | tf_op jit(solution)/shard_map/pallas_call | solution.py:398
  48.8 12.4 %all_to_all.22.msg_ref = bf16[8,128,128]{2,1,0:T(8,128)(2,1)S(1)} all-to-all(bf16[8,128,128]{2,1,0:T(8,128)(2,1)S(1)} %shard_map.144), channel_id=1, replica_groups={{0,8,64,72,128,136,192,200},{16,24,80,88,144,152,208,216},{32,40,96,104..., dimensions={0} | all-to-all | bytes 524288 | tf_op jit(solution)/shard_map/all_to_all | solution.py:405
  61.2 0.9 %shard_map.146 = (bf16[128,512]{1,0:T(8,128)(2,1)S(1)}, f32[8,128]{1,0:T(8,128)}) custom-call(bf16[8,128,128]{2,1,0:T(8,128)(2,1)S(1)} %all_to_all.22.msg_ref), custom_call_target="tpu_custom_call" | custom-call | flops 1000000000 | bytes 2000000 | tf_op jit(solution)/shard_map/pallas_call | solution.py:406
  62.1 8.2 %all-to-all-start.2 = ((f32[8,1,128]{2,1,0:T(1,128)}), f32[8,1,128]{2,1,0:T(1,128)S(1)}, u32[]{:S(2)}, u32[]{:S(2)}) async-start(f32[8,1,128]{2,1,0:T(1,128)} %bitcast.1), calls=%async_computation.2 | async-start | bytes 8192 | tf_op jit(solution)/shard_map/all_to_all | solution.py:407
  70.3 0.8 shard_map.145
  71.0 5.7 %all-to-all-done.2 = f32[8,1,128]{2,1,0:T(1,128)S(1)} async-done(((f32[8,1,128]{2,1,0:T(1,128)}), f32[8,1,128]{2,1,0:T(1,128)S(1)}, u32[]{:S(2)}, u32[]{:S(2)}) %all-to-all-start.2) | async-done | bytes 4128 | tf_op jit(solution)/shard_map/all_to_all | solution.py:407
  76.7 0.8 %shard_map.147 = bf16[128,512]{1,0:T(8,128)(2,1)} custom-call(s32[1]{0:T(128)S(6)} %copy.16.valid_ref, bf16[128,512]{1,0:T(8,128)(2,1)S(1)} %get-tuple-element.18.attended_ref, f32[8,128]{1,0:T(8,128)S(1)} %bitcast.4), custom_call_target="tpu_custom_call" | custom-call | flops 1000000000 | bytes 2000000 | tf_op jit(solution)/shard_map/pallas_call | solution.py:409
Async XLA Ops:
  0.6 36.0 %copy-start.4 = (bf16[256,256]{1,0:T(8,128)(2,1)S(1)}, bf16[256,256]{1,0:T(8,128)(2,1)}, u32[]{:S(2)}) copy-start(bf16[256,256]{1,0:T(8,128)(2,1)} %constant.12.clone.nh_ref) | copy-start | bytes 393220
  0.6 36.0 %copy-start.5 = (bf16[256,256]{1,0:T(8,128)(2,1)S(1)}, bf16[256,256]{1,0:T(8,128)(2,1)}, u32[]{:S(2)}) copy-start(bf16[256,256]{1,0:T(8,128)(2,1)} %constant.13.clone.nl_ref) | copy-start | bytes 393220
  0.7 36.0 %copy-start.1 = (f32[512]{0:T(512)S(1)}, f32[512]{0:T(512)}, u32[]{:S(2)}) copy-start(f32[512]{0:T(512)} %skip_ref.1) | copy-start | bytes 6148
  25.7 15.5 %collective-permute-start.7 = (bf16[32,96,128]{2,1,0:T(8,128)(2,1)S(1)}, bf16[32,96,128]{2,1,0:T(8,128)(2,1)S(1)}, u32[]{:S(2)}, u32[]{:S(2)}) collective-permute-start(bf16[32,96,128]{2,1,0:T(8,128)(2,1)S(1)} %all_to_all.21.refs_8_.in_ref), channel_id=1, source_target_pairs={{0,8},{8,0},{16,24},{24,16},{32,40},{40,32},{48,56},{56,48},{64,72... | collective-permute-start | bytes 2359304 | tf_op jit(solution)/shard_map/ppermute | solution.py:382
  26.3 9.7 %collective-permute-start = (bf16[128,128]{1,0:T(8,128)(2,1)}, bf16[128,128]{1,0:T(8,128)(2,1)S(1)}, u32[]{:S(2)}, u32[]{:S(2)}) collective-permute-start(bf16[128,128]{1,0:T(8,128)(2,1)} %get-tuple-element.12), channel_id=1, source_target_pairs={{0,64},{8,72},{16,80},{24,88},{32,96},{40,104},{48,112},{56,120},{... | collective-permute-start | bytes 98312 | tf_op jit(solution)/shard_map/ppermute | solution.py:365
  26.3 9.8 %collective-permute-start.1 = (bf16[128,128]{1,0:T(8,128)(2,1)}, bf16[128,128]{1,0:T(8,128)(2,1)S(1)}, u32[]{:S(2)}, u32[]{:S(2)}) collective-permute-start(bf16[128,128]{1,0:T(8,128)(2,1)} %get-tuple-element.13), channel_id=1, source_target_pairs={{0,128},{8,136},{16,144},{24,152},{32,160},{40,168},{48,176},{56,1... | collective-permute-start | bytes 98312 | tf_op jit(solution)/shard_map/ppermute | solution.py:365
  27.8 8.7 %collective-permute-start.2 = (bf16[128,128]{1,0:T(8,128)(2,1)}, bf16[128,128]{1,0:T(8,128)(2,1)S(1)}, u32[]{:S(2)}, u32[]{:S(2)}) collective-permute-start(bf16[128,128]{1,0:T(8,128)(2,1)} %get-tuple-element.14), channel_id=1, source_target_pairs={{0,192},{8,200},{16,208},{24,216},{32,224},{40,232},{48,240},{56,2... | collective-permute-start | bytes 98312 | tf_op jit(solution)/shard_map/ppermute | solution.py:365
  29.0 12.3 %copy-start = (bf16[128,128]{1,0:T(8,128)(2,1)S(1)}, bf16[128,128]{1,0:T(8,128)(2,1)}, u32[]{:S(2)}) copy-start(bf16[128,128]{1,0:T(8,128)(2,1)} %get-tuple-element.11.refs_0_) | copy-start | bytes 98308
  29.0 9.5 %collective-permute-start.3 = (bf16[128,128]{1,0:T(8,128)(2,1)}, bf16[128,128]{1,0:T(8,128)(2,1)S(1)}, u32[]{:S(2)}, u32[]{:S(2)}) collective-permute-start(bf16[128,128]{1,0:T(8,128)(2,1)} %get-tuple-element.11.refs_0_), channel_id=1, source_target_pairs={{0,8},{8,0},{16,24},{24,16},{32,40},{40,32},{48,56},{56,48},{64,72... | collective-permute-start | bytes 98312 | tf_op jit(solution)/shard_map/ppermute | solution.py:366
  30.4 0.9 %copy-start.2 = (bf16[256,256]{1,0:T(8,128)(2,1)S(1)}, bf16[256,256]{1,0:T(8,128)(2,1)}, u32[]{:S(2)}) copy-start(bf16[256,256]{1,0:T(8,128)(2,1)} %constant.10.clone.mh_hbm.mh_ref) | copy-start | bytes 393220
  31.3 0.9 %copy-start.3 = (bf16[256,256]{1,0:T(8,128)(2,1)S(1)}, bf16[256,256]{1,0:T(8,128)(2,1)}, u32[]{:S(2)}) copy-start(bf16[256,256]{1,0:T(8,128)(2,1)} %constant.11.clone.ml_hbm.ml_ref) | copy-start | bytes 393220
  32.2 0.8 copy-start.6
  35.9 3.3 %collective-permute-start.4 = (bf16[128,128]{1,0:T(8,128)(2,1)S(1)}, bf16[128,128]{1,0:T(8,128)(2,1)S(1)}, u32[]{:S(2)}, u32[]{:S(2)}) collective-permute-start(bf16[128,128]{1,0:T(8,128)(2,1)S(1)} %collective-permute-done.refs_1_), channel_id=1, source_target_pairs={{0,8},{8,0},{16,24},{24,16},{32,40},{40,32},{48,56},{56,48},{64,72... | collective-permute-start | bytes 98312 | tf_op jit(solution)/shard_map/ppermute | solution.py:366
  36.0 4.1 %collective-permute-start.5 = (bf16[128,128]{1,0:T(8,128)(2,1)S(1)}, bf16[128,128]{1,0:T(8,128)(2,1)S(1)}, u32[]{:S(2)}, u32[]{:S(2)}) collective-permute-start(bf16[128,128]{1,0:T(8,128)(2,1)S(1)} %collective-permute-done.1.refs_2_), channel_id=1, source_target_pairs={{0,8},{8,0},{16,24},{24,16},{32,40},{40,32},{48,56},{56,48},{64,72... | collective-permute-start | bytes 98312 | tf_op jit(solution)/shard_map/ppermute | solution.py:366
  36.5 4.7 %collective-permute-start.6 = (bf16[128,128]{1,0:T(8,128)(2,1)S(1)}, bf16[128,128]{1,0:T(8,128)(2,1)S(1)}, u32[]{:S(2)}, u32[]{:S(2)}) collective-permute-start(bf16[128,128]{1,0:T(8,128)(2,1)S(1)} %collective-permute-done.2.refs_3_), channel_id=1, source_target_pairs={{0,8},{8,0},{16,24},{24,16},{32,40},{40,32},{48,56},{56,48},{64,72... | collective-permute-start | bytes 98312 | tf_op jit(solution)/shard_map/ppermute | solution.py:366
  38.6 6.2 %collective-permute-start.10 = (bf16[32,16,128]{2,1,0:T(8,128)(2,1)S(1)}, bf16[32,16,128]{2,1,0:T(8,128)(2,1)S(1)}, u32[]{:S(2)}, u32[]{:S(2)}) collective-permute-start(bf16[32,16,128]{2,1,0:T(8,128)(2,1)S(1)} %shard_map.143.v0), channel_id=1, source_target_pairs={{0,48},{8,56},{16,0},{24,8},{32,16},{40,24},{48,32},{56,40},{64,11... | collective-permute-start | bytes 393224 | tf_op jit(solution)/shard_map/ppermute | solution.py:390
  39.2 6.1 %collective-permute-start.8 = (bf16[32,16,128]{2,1,0:T(8,128)(2,1)S(1)}, bf16[32,16,128]{2,1,0:T(8,128)(2,1)S(1)}, u32[]{:S(2)}, u32[]{:S(2)}) collective-permute-start(bf16[32,16,128]{2,1,0:T(8,128)(2,1)S(1)} %shard_map.143.v0), channel_id=1, source_target_pairs={{0,16},{8,24},{16,32},{24,40},{32,48},{40,56},{48,0},{56,8},{64,80... | collective-permute-start | bytes 393224 | tf_op jit(solution)/shard_map/ppermute | solution.py:390
  40.1 7.1 %collective-permute-start.9 = (bf16[32,16,128]{2,1,0:T(8,128)(2,1)S(1)}, bf16[32,16,128]{2,1,0:T(8,128)(2,1)S(1)}, u32[]{:S(2)}, u32[]{:S(2)}) collective-permute-start(bf16[32,16,128]{2,1,0:T(8,128)(2,1)S(1)} %shard_map.143.v0), channel_id=1, source_target_pairs={{0,32},{8,40},{16,48},{24,56},{32,0},{40,8},{48,16},{56,24},{64,96... | collective-permute-start | bytes 393224 | tf_op jit(solution)/shard_map/ppermute | solution.py:390
  62.1 14.7 %all-to-all-start.2 = ((f32[8,1,128]{2,1,0:T(1,128)}), f32[8,1,128]{2,1,0:T(1,128)S(1)}, u32[]{:S(2)}, u32[]{:S(2)}) async-start(f32[8,1,128]{2,1,0:T(1,128)} %bitcast.1), calls=%async_computation.2 | async-start | bytes 8192 | tf_op jit(solution)/shard_map/all_to_all | solution.py:407

commit v4 on v3

--- a/solution.py
+++ b/solution.py
@@ -112,50 +112,52 @@
     return copies
 
 
-def pre_kernel(key_hbm, value_hbm, gate_hbm, attn_hbm, query_hbm, *refs):
-    msg_ref, q_refs, (key_ref, value_ref, gate_ref, attn_ref, query_ref, sems) = (
-        refs[0],
-        refs[1:5],
-        refs[5:],
+def flip(eye, block):
+    return lax.dot_general(eye, block, NT, preferred_element_type=F32).astype(BF)
+
+
+def identity():
+    row = lax.broadcasted_iota(jnp.int32, (G, G), 0)
+    lane = lax.broadcasted_iota(jnp.int32, (G, G), 1)
+    return jnp.where(row == lane, 1.0, 0.0).astype(BF)
+
+
+def pre_kernel(key_hbm, value_hbm, gate_hbm, attn_hbm, msg_hbm, key, value, gate, attn, msg, sems, done):
+    copies = load(
+        [(key_hbm, key), (value_hbm, value), (gate_hbm, gate), (attn_hbm, attn)], sems
     )
-    copies = load(
-        [
-            (key_hbm, key_ref),
-            (value_hbm, value_ref),
-            (gate_hbm, gate_ref),
-            (attn_hbm, attn_ref),
-            (query_hbm, query_ref),
-        ],
-        sems,
-    )
-    copies[0].wait()
-    copies[1].wait()
+    eye = identity()
+    for copy in copies:
+        copy.wait()
+    out = []
     for h in range(4):
         cols = slice(h * HD, (h + 1) * HD)
-        mixed = (key_ref[:, cols].astype(F32) * value_ref[:, cols].astype(F32)).T.astype(BF)
+        mixed = flip(eye, (key[:, cols].astype(F32) * value[:, cols].astype(F32)).astype(BF))
+        gated = flip(eye, gate[:, cols])
         for c in range(2):
             for k in range(4):
+                e = 8 * h + 2 * k + c
                 rows = slice(c * 64 + k * CH, c * 64 + (k + 1) * CH)
-                msg_ref[8 * h + 2 * k + c, 64:80, :] = mixed[rows]
-    copies[2].wait()
-    for h in range(4):
-        gate = gate_ref[:, h * HD : (h + 1) * HD].astype(F32).T.astype(BF)
-        for c in range(2):
-            for k in range(4):
-                rows = slice(c * 64 + k * CH, c * 64 + (k + 1) * CH)
-                msg_ref[8 * h + 2 * k + c, 80:96, :] = gate[rows]
-    copies[3].wait()
-    for h in range(4):
-        for c in range(2):
-            for k in range(4):
-                msg_ref[8 * h + 2 * k + c, 0:64, :] = attn_ref[
-                    c * 64 : (c + 1) * 64, h * HD : (h + 1) * HD
-                ]
-    copies[4].wait()
-    head = place()[1]
-    for d in range(4):
-        col = pl.multiple_of(lax.rem(head + d, 4) * HD, HD)
-        q_refs[d][...] = query_ref[:, pl.ds(col, HD)]
+                msg[e, 0:64, :] = attn[c * 64 : (c + 1) * 64, cols]
+                msg[e, 64:80, :] = mixed[rows]
+                msg[e, 80:96, :] = gated[rows]
+        part = pl.ds(8 * h, 8)
+        out += load([(msg.at[part], msg_hbm.at[part])], done.at[pl.ds(h, 1)])
+    for copy in out:
+        copy.wait()
+
+
+def query_kernel(own_hbm, other_hbm, q0, q1, q2, q3, own_ref, other_ref, sems):
+    copies = load([(own_hbm, own_ref), (other_hbm, other_ref)], sems)
+    _, head, _, core = place()
+    swap = core == 1
+    for copy in copies:
+        copy.wait()
+    for d, q_ref in enumerate((q0, q1, q2, q3)):
+        cols = pl.ds(pl.multiple_of(lax.rem(head + d, 4) * HD, HD), HD)
+        own, other = own_ref[:, cols], other_ref[:, cols]
+        q_ref[0] = jnp.where(swap, other, own)
+        q_ref[1] = jnp.where(swap, own, other)
 
 
 def taps_kernel(
@@ -219,19 +221,16 @@
 
 
 def weights_kernel(valid_ref, *refs):
-    q_refs, own_ref, other_ref, w_ref, total_ref = refs[:8], refs[8], refs[9], refs[10], refs[11]
-    qs, keys, scores = refs[12:]
+    q_refs, (own_ref, other_ref, w_ref, total_ref, qs, keys, scores) = refs[:4], refs[4:]
     _, head, k, core = place()
     valid = valid_ref[0]
-    flip = core == 1
+    swap = core == 1
     for d in range(4):
-        own, other = q_refs[d][...], q_refs[4 + d][...]
-        qs[d, 0:G] = jnp.where(flip, other, own)
-        qs[d, G : 2 * G] = jnp.where(flip, own, other)
+        qs[d] = q_refs[d][...].reshape(2 * G, HD)
     for s in range(NB):
         own, other = own_ref[s, 0:64], other_ref[s, 0:64]
-        keys[s * G : s * G + 64] = jnp.where(flip, other, own)
-        keys[s * G + 64 : (s + 1) * G] = jnp.where(flip, own, other)
+        keys[s * G : s * G + 64] = jnp.where(swap, other, own)
+        keys[s * G + 64 : (s + 1) * G] = jnp.where(swap, own, other)
     factor = math.log2(math.e) / math.sqrt(HD)
     row = lax.broadcasted_iota(jnp.int32, (2 * G, G), 0)
     lane = lax.broadcasted_iota(jnp.int32, (2 * G, G), 1)
@@ -286,25 +285,23 @@
 
 def gather_kernel(msg_ref, attended_ref, sum_ref):
     left = lax.broadcasted_iota(jnp.int32, (64, G), 1) < 64
-    ones = jnp.ones((8, G), BF)
-    sums = jnp.zeros((8, G), F32)
+    sums = jnp.zeros((G, G), F32)
     for h in range(4):
-        cols = slice(h * HD, (h + 1) * HD)
         p0 = msg_ref[2 * h, 0:64, :].astype(F32)
         p1 = msg_ref[2 * h + 1, 0:64, :].astype(F32)
         low = jnp.where(left, p0, p1)
         high = pltpu.roll(jnp.where(left, p1, p0), 64, 1)
         both = jnp.concatenate([low, high], axis=0)
-        attended_ref[:, cols] = both.astype(BF)
-        for part in split(both * both):
-            sums += lax.dot_general(ones, part, NT, preferred_element_type=F32)
-    sum_ref[...] = sums
+        attended_ref[:, h * HD : (h + 1) * HD] = both.astype(BF)
+        sums += both * both
+    sum_ref[...] = jnp.broadcast_to(jnp.sum(sums.T, axis=0, keepdims=True), (8, G))
 
 
 def hyena_kernel(msg_ref, hyena_ref):
+    eye = identity()
     for h in range(4):
-        block = msg_ref[2 * h : 2 * h + 2, 64:128, :].reshape(G, G).astype(F32)
-        hyena_ref[:, h * HD : (h + 1) * HD] = block.T.astype(BF)
+        block = msg_ref[2 * h : 2 * h + 2, 64:128, :].reshape(G, G)
+        hyena_ref[:, h * HD : (h + 1) * HD] = flip(eye, block)
 
 
 def final_kernel(valid_ref, attended_ref, sum_ref, attn_ref):
@@ -344,6 +341,9 @@
     )
 
 
+QV = 50
+
+
 def dma(n):
     return pltpu.SemaphoreType.DMA((n,))
 
@@ -354,16 +354,24 @@
     high, low, high_t, low_t, twiddle = (jnp.asarray(t) for t in tables())
 
     block = pltpu.VMEM((G, 4 * HD), BF)
-    msg, *q = call(
+    other_queries = lax.ppermute(queries, "ctx", CORES)
+    msg = call(
         pre_kernel,
-        (sds((NB, 96, G), BF),) + (sds((G, HD), BF),) * 4,
-        [HB] * 5,
-        [block] * 5 + [dma(5)],
+        sds((NB, 96, G), BF),
+        [HB] * 4,
+        [block] * 4 + [pltpu.VMEM((NB, 96, G), BF), dma(4), dma(4)],
+        out_specs=HB,
         vmem=60,
-    )(hyena_key, hyena_value, hyena_gate, attn_keys, queries)
+    )(hyena_key, hyena_value, hyena_gate, attn_keys)
     got = lax.all_to_all(msg, "ctx", 0, 0, tiled=True)
+    q = call(
+        query_kernel,
+        (sds((2, G, HD), BF),) * 4,
+        [HB, AN],
+        [block, block, dma(2)],
+        vmem=QV,
+    )(queries, other_queries)
     q = [q[0]] + [lax.ppermute(q[d], "ctx", along_y(d)) for d in (1, 2, 3)]
-    q += [lax.ppermute(x, "ctx", CORES) for x in q]
     spec = call(
         taps_kernel,
         sds((NB * CH, 2 * G), F32),
@@ -387,11 +395,13 @@
         [pltpu.VMEM((NB * CH, 2 * G), F32)],
         us=3,
     )(valid_length, got, spec, skip_weight, twiddle, high, low, high_t, low_t)
-    v = [values] + [lax.ppermute(values, "ctx", along_x(d)) for d in (1, 2, 3)]
+    far = lax.ppermute(values, "ctx", along_x(2))
+    near = [lax.ppermute(values, "ctx", along_x(d)) for d in (1, 3)]
+    v = [values, near[0], far, near[1]]
     weights, totals = call(
         weights_kernel,
         (sds((8 * G, SEQ), BF), sds((8 * G, G), F32)),
-        [SM] + [VM] * 8 + [VM] * 2,
+        [SM] + [VM] * 6,
         [pltpu.VMEM((4, 2 * G, HD), BF), pltpu.VMEM((SEQ, HD), BF), pltpu.VMEM((2 * G, SEQ), F32)],
         us=4,
     )(valid_length, *q, got, got_other)

time: 77.9 us -> 77.1 us (0.990); the launches traced: 77.5 us -> 75.7 us
  starting transfers between devices: 16.2 us -> 14.9 us
  blocking collectives: 35.2 us -> 34.4 us
    ppermute x7 -> x4, starting transfers between devices: 4.74 us -> 2.92 us  [the longest x2 1.56 us: shards(): near = [lax.ppermute(values, 'ctx', along_x(d)) for d in (1, 3)]]
    all_to_all x1, blocking collectives: 12.4 us -> 11.6 us  [shards(): lax.all_to_all(back, 'ctx', 0, 0, tiled=True, axis_index_groups=COLS)]
    pallas_call x1 -> x2, Pallas kernels: 2.24 us -> 2.79 us  [the longest x1 2.37 us: shards(): call(pre_kernel, sds((NB, 96, G), BF), [HB] * 4, [block] * 4 + [pltpu.VME...]
    ppermute x7 -> x4, waiting for transfers between devices: 2.38 us -> 2.02 us  [the longest x1 1.29 us: shards(): far = lax.ppermute(values, 'ctx', along_x(2))]
    unnamed x14 -> x20, local copies, waits for them, and re-layouts: 2.59 us -> 2.61 us
  transfers between devices with their start and end apart: 12 -> 9, of which waited for: 3 -> 4; matrix products, arithmetic and copies ran while one was open for 0% -> 0% of each run, Pallas kernels for 11% -> 12%
where the time goes in v4:
time: 77.1 us; the launch traced here: 75.7 us
  blocking collectives  34.4 us (45%)
  starting transfers between devices  14.9 us (19%)
  Pallas kernels  14.5 us (19%)
  waiting for transfers between devices  7.87 us (10%)
  local copies, waits for them, and re-layouts  2.61 us (3%)
  between operations  1.44 us (2%)
    all_to_all x1, blocking collectives, shards(): got = lax.all_to_all(msg, 'ctx', 0, 0, tiled=True)  22.8 us
    all_to_all x1, blocking collectives, shards(): lax.all_to_all(back, 'ctx', 0, 0, tiled=True, axis_index_groups=COLS)  11.6 us
    all_to_all x1, starting transfers between devices, shards(): sums = lax.all_to_all(sums, 'tp', 0, 0, tiled=True)  8.18 us
    all_to_all x1, waiting for transfers between devices, shards(): sums = lax.all_to_all(sums, 'tp', 0, 0, tiled=True)  5.62 us
    pallas_call x1, Pallas kernels, shards(): call(weights_kernel, (sds((8 * G, SEQ), BF), sds((8 * G, G), F32)), [SM]...  3.43 us
    ppermute x3, starting transfers between devices, shards(): q = [q[0]] + [lax.ppermute(q[d], 'ctx', along_y(d)) for d in (1, 2, 3)]  3.32 us
    unnamed x20, local copies, waits for them, and re-layouts  2.61 us
    pallas_call x1, Pallas kernels, shards(): call(pre_kernel, sds((NB, 96, G), BF), [HB] * 4, [block] * 4 + [pltpu.VME...  2.37 us
  transfers between devices with their start and end apart: 9, of which 4 were waited for; matrix products, arithmetic and copies ran while one was open for 0% of the time, Pallas kernels for 12%

profile of v4, /device:TPU:1, one launch (start us, length us, event | category | flops | bytes accessed | tf_op | source)
XLA Modules:
  0.0 75.7 jit_solution(15663566958403220396)
XLA Ops:
  0.6 0.0 copy-start.3
  0.6 0.0 copy-start.5
  0.7 0.0 copy-start.9
  0.7 0.0 copy-start.6
  0.7 0.0 copy-start.7
  0.7 0.0 copy-start
  0.7 0.0 copy-start.1
  0.7 2.4 %shard_map.141 = bf16[32,96,128]{2,1,0:T(8,128)(2,1)} custom-call(bf16[128,512]{1,0:T(8,128)(2,1)} %key_hbm.1, bf16[128,512]{1,0:T(8,128)(2,1)} %value_hbm.1, bf16[128,512]{1,0:T(8,128)(2,1)} %gate_hbm.1, bf16[128,512]{1,0:T(8,128)(2,1)} %attn_hbm.1), custom_call_target="tpu_custom_call" | custom-call | flops 1000000000 | bytes 2000000 | tf_op jit(solution)/shard_map/pallas_call | solution.py:358
  3.1 22.8 %all_to_all.21.refs_4_.in_ref = bf16[32,96,128]{2,1,0:T(8,128)(2,1)S(1)} all-to-all(bf16[32,96,128]{2,1,0:T(8,128)(2,1)} %shard_map.141), channel_id=1, replica_groups=mesh['ctx'=32,'tp'=8] {'ctx'}, dimensions={0} | all-to-all | bytes 1572864 | tf_op jit(solution)/shard_map/all_to_all | solution.py:366
  25.9 0.5 collective-permute-start.4
  26.4 0.0 collective-permute-start
  27.1 0.0 copy-start.2
  27.1 0.9 %copy-done.2 = bf16[256,256]{1,0:T(8,128)(2,1)S(1)} copy-done((bf16[256,256]{1,0:T(8,128)(2,1)S(1)}, bf16[256,256]{1,0:T(8,128)(2,1)}, u32[]{:S(2)}) %copy-start.2) | copy-done | bytes 131096
  28.0 0.0 copy-start.4
  28.0 0.9 %copy-done.4 = bf16[256,256]{1,0:T(8,128)(2,1)S(1)} copy-done((bf16[256,256]{1,0:T(8,128)(2,1)S(1)}, bf16[256,256]{1,0:T(8,128)(2,1)}, u32[]{:S(2)}) %copy-start.4) | copy-done | bytes 131096
  28.9 0.0 copy-start.8
  28.9 0.8 copy-done.8
  29.7 2.3 %shard_map.143.spec_ref = f32[512,256]{1,0:T(8,128)S(1)} custom-call(bf16[4096,512]{1,0:T(8,128)(2,1)} %taps_hbm.1, f32[2,32,128]{2,1,0:T(8,128)S(1)} %copy-done.8, bf16[256,256]{1,0:T(8,128)(2,1)S(1)} %copy-done.2, bf16[256,256]{1,0:T(8,128)(2,1)S(1)} %copy-done.4), custom_call_target="tpu_custom_call" | custom-call | flops 2000000000 | bytes 4000000 | tf_op jit(solution)/shard_map/pallas_call | solution.py:375
  32.0 0.0 collective-permute-done.other_hbm
  32.0 0.0 copy-done
  32.0 0.4 shard_map.140
  32.5 0.1 collective-permute-start.1
  32.5 1.7 %collective-permute-start.2 = (bf16[2,128,128]{2,1,0:T(8,128)(2,1)S(1)}, bf16[2,128,128]{2,1,0:T(8,128)(2,1)S(1)}, u32[]{:S(2)}, u32[]{:S(2)}) collective-permute-start(bf16[2,128,128]{2,1,0:T(8,128)(2,1)S(1)} %get-tuple-element.12), channel_id=1, source_target_pairs={{0,128},{8,136},{16,144},{24,152},{32,160},{40,168},{48,176},{56,1... | collective-permute-start | bytes 196616 | tf_op jit(solution)/shard_map/ppermute | solution.py:374
  34.2 1.6 %collective-permute-start.3 = (bf16[2,128,128]{2,1,0:T(8,128)(2,1)S(1)}, bf16[2,128,128]{2,1,0:T(8,128)(2,1)S(1)}, u32[]{:S(2)}, u32[]{:S(2)}) collective-permute-start(bf16[2,128,128]{2,1,0:T(8,128)(2,1)S(1)} %get-tuple-element.13), channel_id=1, source_target_pairs={{0,192},{8,200},{16,208},{24,216},{32,224},{40,232},{48,240},{56,2... | collective-permute-start | bytes 196616 | tf_op jit(solution)/shard_map/ppermute | solution.py:374
  35.8 0.0 copy-done.3
  35.8 0.0 copy-done.5
  35.8 0.0 copy-done.9
  35.8 0.0 copy-done.6
  35.8 0.0 copy-done.7
  35.8 0.0 copy-done.1
  35.8 1.9 %shard_map.144.v0 = bf16[32,16,128]{2,1,0:T(8,128)(2,1)S(1)} custom-call(s32[1]{0:T(128)S(6)} %copy.16.valid_ref, bf16[32,96,128]{2,1,0:T(8,128)(2,1)S(1)} %all_to_all.21.refs_4_.in_ref, f32[512,256]{1,0:T(8,128)S(1)} %shard_map.143.spec_ref, f32[512]{0:T(512)S(1)} %copy-done.1, f32[2,32,128]{2,1,0:T(8,128)S(1)} %copy-done.9, ...), custom_call_target="tpu_custom_call" | custom-call | flops 3000000000 | bytes 6000000 | tf_op jit(solution)/shard_map/pallas_call | solution.py:391
  37.7 0.6 collective-permute-start.5
  38.4 0.2 collective-permute-done.1.refs_1_
  38.6 1.4 %collective-permute-start.6 = (bf16[32,16,128]{2,1,0:T(8,128)(2,1)S(1)}, bf16[32,16,128]{2,1,0:T(8,128)(2,1)S(1)}, u32[]{:S(2)}, u32[]{:S(2)}) collective-permute-start(bf16[32,16,128]{2,1,0:T(8,128)(2,1)S(1)} %shard_map.144.v0), channel_id=1, source_target_pairs={{0,32},{8,40},{16,48},{24,56},{32,0},{40,8},{48,16},{56,24},{64,96... | collective-permute-start | bytes 393224 | tf_op jit(solution)/shard_map/ppermute | solution.py:398
  39.9 0.0 collective-permute-done.2.refs_2_
  39.9 0.9 %collective-permute-start.7 = (bf16[32,16,128]{2,1,0:T(8,128)(2,1)S(1)}, bf16[32,16,128]{2,1,0:T(8,128)(2,1)S(1)}, u32[]{:S(2)}, u32[]{:S(2)}) collective-permute-start(bf16[32,16,128]{2,1,0:T(8,128)(2,1)S(1)} %shard_map.144.v0), channel_id=1, source_target_pairs={{0,48},{8,56},{16,0},{24,8},{32,16},{40,24},{48,32},{56,40},{64,11... | collective-permute-start | bytes 393224 | tf_op jit(solution)/shard_map/ppermute | solution.py:399
  40.9 0.0 collective-permute-done.3.refs_3_
  40.9 0.0 collective-permute-done.4.refs_5_
  40.9 3.4 %shard_map.142 = (bf16[1024,4096]{1,0:T(8,128)(2,1)S(1)}, f32[1024,128]{1,0:T(8,128)S(1)}) custom-call(s32[1]{0:T(128)S(6)} %copy.16.valid_ref, bf16[2,128,128]{2,1,0:T(8,128)(2,1)S(1)} %get-tuple-element.10.refs_0_, bf16[2,128,128]{2,1,0:T(8,128)(2,1)S(1)} %collective-permute-done.1.refs_1_, bf16[2,128,128]{2,1,0:T(8,128)(2,1)S(1)} %collective-permute-done.2.refs_2_, ...), custom_call_target="tpu_custom_call" | custom-call | flops 4000000000 | bytes 8000000 | tf_op jit(solution)/shard_map/pallas_call | solution.py:401
  44.3 0.0 collective-permute-done.5.v1
  44.3 1.3 %collective-permute-done.6.v2 = bf16[32,16,128]{2,1,0:T(8,128)(2,1)S(1)} collective-permute-done((bf16[32,16,128]{2,1,0:T(8,128)(2,1)S(1)}, bf16[32,16,128]{2,1,0:T(8,128)(2,1)S(1)}, u32[]{:S(2)}, u32[]{:S(2)}) %collective-permute-start.6) | collective-permute-done | bytes 131104 | tf_op jit(solution)/shard_map/ppermute | solution.py:398
  45.6 0.7 collective-permute-done.7.v3
  46.3 1.6 %shard_map.145 = bf16[8,128,128]{2,1,0:T(8,128)(2,1)S(1)} custom-call(bf16[1024,4096]{1,0:T(8,128)(2,1)S(1)} %get-tuple-element.14.w_ref, f32[1024,128]{1,0:T(8,128)S(1)} %get-tuple-element.15.total_ref, bf16[32,16,128]{2,1,0:T(8,128)(2,1)S(1)} %shard_map.144.v0, bf16[32,16,128]{2,1,0:T(8,128)(2,1)S(1)} %collective-permute-done.5.v1, ...), custom_call_target="tpu_custom_call" | custom-call | flops 4000000000 | bytes 8000000 | tf_op jit(solution)/shard_map/pallas_call | solution.py:408
  47.9 11.6 %all_to_all.22.msg_ref = bf16[8,128,128]{2,1,0:T(8,128)(2,1)S(1)} all-to-all(bf16[8,128,128]{2,1,0:T(8,128)(2,1)S(1)} %shard_map.145), channel_id=1, replica_groups={{0,8,64,72,128,136,192,200},{16,24,80,88,144,152,208,216},{32,40,96,104..., dimensions={0} | all-to-all | bytes 524288 | tf_op jit(solution)/shard_map/all_to_all | solution.py:415
  59.5 0.8 %shard_map.147 = (bf16[128,512]{1,0:T(8,128)(2,1)S(1)}, f32[8,128]{1,0:T(8,128)}) custom-call(bf16[8,128,128]{2,1,0:T(8,128)(2,1)S(1)} %all_to_all.22.msg_ref), custom_call_target="tpu_custom_call" | custom-call | flops 1000000000 | bytes 2000000 | tf_op jit(solution)/shard_map/pallas_call | solution.py:416
  60.3 8.2 %all-to-all-start.2 = ((f32[8,1,128]{2,1,0:T(1,128)}), f32[8,1,128]{2,1,0:T(1,128)S(1)}, u32[]{:S(2)}, u32[]{:S(2)}) async-start(f32[8,1,128]{2,1,0:T(1,128)} %bitcast.1), calls=%async_computation.2 | async-start | bytes 8192 | tf_op jit(solution)/shard_map/all_to_all | solution.py:417
  68.5 0.9 %shard_map.146 = bf16[128,512]{1,0:T(8,128)(2,1)} custom-call(bf16[8,128,128]{2,1,0:T(8,128)(2,1)S(1)} %all_to_all.22.msg_ref), custom_call_target="tpu_custom_call" | custom-call | flops 1000000000 | bytes 2000000 | tf_op jit(solution)/shard_map/pallas_call | solution.py:418
  69.3 5.6 %all-to-all-done.2 = f32[8,1,128]{2,1,0:T(1,128)S(1)} async-done(((f32[8,1,128]{2,1,0:T(1,128)}), f32[8,1,128]{2,1,0:T(1,128)S(1)}, u32[]{:S(2)}, u32[]{:S(2)}) %all-to-all-start.2) | async-done | bytes 4128 | tf_op jit(solution)/shard_map/all_to_all | solution.py:417
  75.0 0.8 %shard_map.148 = bf16[128,512]{1,0:T(8,128)(2,1)} custom-call(s32[1]{0:T(128)S(6)} %copy.16.valid_ref, bf16[128,512]{1,0:T(8,128)(2,1)S(1)} %get-tuple-element.16.attended_ref, f32[8,128]{1,0:T(8,128)S(1)} %bitcast.4), custom_call_target="tpu_custom_call" | custom-call | flops 1000000000 | bytes 2000000 | tf_op jit(solution)/shard_map/pallas_call | solution.py:419
Async XLA Ops:
  0.6 35.2 %copy-start.3 = (bf16[256,256]{1,0:T(8,128)(2,1)S(1)}, bf16[256,256]{1,0:T(8,128)(2,1)}, u32[]{:S(2)}) copy-start(bf16[256,256]{1,0:T(8,128)(2,1)} %constant.10.clone.mh_hbm.mh_ref) | copy-start | bytes 393220
  0.6 35.1 %copy-start.5 = (bf16[256,256]{1,0:T(8,128)(2,1)S(1)}, bf16[256,256]{1,0:T(8,128)(2,1)}, u32[]{:S(2)}) copy-start(bf16[256,256]{1,0:T(8,128)(2,1)} %constant.11.clone.ml_hbm.ml_ref) | copy-start | bytes 393220
  0.7 35.1 %copy-start.9 = (f32[2,32,128]{2,1,0:T(8,128)S(1)}, f32[2,32,128]{2,1,0:T(8,128)}, u32[]{:S(2)}) copy-start(f32[2,32,128]{2,1,0:T(8,128)} %constant.14.clone.tw_hbm.tw_ref) | copy-start | bytes 98308
  0.7 35.1 %copy-start.6 = (bf16[256,256]{1,0:T(8,128)(2,1)S(1)}, bf16[256,256]{1,0:T(8,128)(2,1)}, u32[]{:S(2)}) copy-start(bf16[256,256]{1,0:T(8,128)(2,1)} %constant.12.clone.nh_ref) | copy-start | bytes 393220
  0.7 35.1 %copy-start.7 = (bf16[256,256]{1,0:T(8,128)(2,1)S(1)}, bf16[256,256]{1,0:T(8,128)(2,1)}, u32[]{:S(2)}) copy-start(bf16[256,256]{1,0:T(8,128)(2,1)} %constant.13.clone.nl_ref) | copy-start | bytes 393220
  0.7 31.3 %copy-start = (bf16[128,512]{1,0:T(8,128)(2,1)S(1)}, bf16[128,512]{1,0:T(8,128)(2,1)}, u32[]{:S(2)}) copy-start(bf16[128,512]{1,0:T(8,128)(2,1)} %own_hbm.1) | copy-start | bytes 393220
  0.7 35.1 %copy-start.1 = (f32[512]{0:T(512)S(1)}, f32[512]{0:T(512)}, u32[]{:S(2)}) copy-start(f32[512]{0:T(512)} %skip_ref.1) | copy-start | bytes 6148
  25.9 14.9 %collective-permute-start.4 = (bf16[32,96,128]{2,1,0:T(8,128)(2,1)S(1)}, bf16[32,96,128]{2,1,0:T(8,128)(2,1)S(1)}, u32[]{:S(2)}, u32[]{:S(2)}) collective-permute-start(bf16[32,96,128]{2,1,0:T(8,128)(2,1)S(1)} %all_to_all.21.refs_4_.in_ref), channel_id=1, source_target_pairs={{0,8},{8,0},{16,24},{24,16},{32,40},{40,32},{48,56},{56,48},{64,72... | collective-permute-start | bytes 2359304 | tf_op jit(solution)/shard_map/ppermute | solution.py:390
  26.4 5.6 %collective-permute-start = (bf16[128,512]{1,0:T(8,128)(2,1)}, bf16[128,512]{1,0:T(8,128)(2,1)S(1)}, u32[]{:S(2)}, u32[]{:S(2)}) collective-permute-start(bf16[128,512]{1,0:T(8,128)(2,1)} %own_hbm.1), channel_id=1, source_target_pairs={{0,8},{8,0},{16,24},{24,16},{32,40},{40,32},{48,56},{56,48},{64,72... | collective-permute-start | bytes 393224 | tf_op jit(solution)/shard_map/ppermute | solution.py:357
  27.1 0.9 %copy-start.2 = (bf16[256,256]{1,0:T(8,128)(2,1)S(1)}, bf16[256,256]{1,0:T(8,128)(2,1)}, u32[]{:S(2)}) copy-start(bf16[256,256]{1,0:T(8,128)(2,1)} %constant.10.clone.mh_hbm.mh_ref) | copy-start | bytes 393220
  28.0 0.9 %copy-start.4 = (bf16[256,256]{1,0:T(8,128)(2,1)S(1)}, bf16[256,256]{1,0:T(8,128)(2,1)}, u32[]{:S(2)}) copy-start(bf16[256,256]{1,0:T(8,128)(2,1)} %constant.11.clone.ml_hbm.ml_ref) | copy-start | bytes 393220
  28.9 0.8 %copy-start.8 = (f32[2,32,128]{2,1,0:T(8,128)S(1)}, f32[2,32,128]{2,1,0:T(8,128)}, u32[]{:S(2)}) copy-start(f32[2,32,128]{2,1,0:T(8,128)} %constant.14.clone.tw_hbm.tw_ref) | copy-start | bytes 98308
  32.5 6.1 %collective-permute-start.1 = (bf16[2,128,128]{2,1,0:T(8,128)(2,1)S(1)}, bf16[2,128,128]{2,1,0:T(8,128)(2,1)S(1)}, u32[]{:S(2)}, u32[]{:S(2)}) collective-permute-start(bf16[2,128,128]{2,1,0:T(8,128)(2,1)S(1)} %get-tuple-element.11), channel_id=1, source_target_pairs={{0,64},{8,72},{16,80},{24,88},{32,96},{40,104},{48,112},{56,120},{... | collective-permute-start | bytes 196616 | tf_op jit(solution)/shard_map/ppermute | solution.py:374
  32.5 7.4 %collective-permute-start.2 = (bf16[2,128,128]{2,1,0:T(8,128)(2,1)S(1)}, bf16[2,128,128]{2,1,0:T(8,128)(2,1)S(1)}, u32[]{:S(2)}, u32[]{:S(2)}) collective-permute-start(bf16[2,128,128]{2,1,0:T(8,128)(2,1)S(1)} %get-tuple-element.12), channel_id=1, source_target_pairs={{0,128},{8,136},{16,144},{24,152},{32,160},{40,168},{48,176},{56,1... | collective-permute-start | bytes 196616 | tf_op jit(solution)/shard_map/ppermute | solution.py:374
  34.2 6.6 %collective-permute-start.3 = (bf16[2,128,128]{2,1,0:T(8,128)(2,1)S(1)}, bf16[2,128,128]{2,1,0:T(8,128)(2,1)S(1)}, u32[]{:S(2)}, u32[]{:S(2)}) collective-permute-start(bf16[2,128,128]{2,1,0:T(8,128)(2,1)S(1)} %get-tuple-element.13), channel_id=1, source_target_pairs={{0,192},{8,200},{16,208},{24,216},{32,224},{40,232},{48,240},{56,2... | collective-permute-start | bytes 196616 | tf_op jit(solution)/shard_map/ppermute | solution.py:374
  37.7 6.6 %collective-permute-start.5 = (bf16[32,16,128]{2,1,0:T(8,128)(2,1)S(1)}, bf16[32,16,128]{2,1,0:T(8,128)(2,1)S(1)}, u32[]{:S(2)}, u32[]{:S(2)}) collective-permute-start(bf16[32,16,128]{2,1,0:T(8,128)(2,1)S(1)} %shard_map.144.v0), channel_id=1, source_target_pairs={{0,16},{8,24},{16,32},{24,40},{32,48},{40,56},{48,0},{56,8},{64,80... | collective-permute-start | bytes 393224 | tf_op jit(solution)/shard_map/ppermute | solution.py:399
  38.6 7.0 %collective-permute-start.6 = (bf16[32,16,128]{2,1,0:T(8,128)(2,1)S(1)}, bf16[32,16,128]{2,1,0:T(8,128)(2,1)S(1)}, u32[]{:S(2)}, u32[]{:S(2)}) collective-permute-start(bf16[32,16,128]{2,1,0:T(8,128)(2,1)S(1)} %shard_map.144.v0), channel_id=1, source_target_pairs={{0,32},{8,40},{16,48},{24,56},{32,0},{40,8},{48,16},{56,24},{64,96... | collective-permute-start | bytes 393224 | tf_op jit(solution)/shard_map/ppermute | solution.py:398
  39.9 6.4 %collective-permute-start.7 = (bf16[32,16,128]{2,1,0:T(8,128)(2,1)S(1)}, bf16[32,16,128]{2,1,0:T(8,128)(2,1)S(1)}, u32[]{:S(2)}, u32[]{:S(2)}) collective-permute-start(bf16[32,16,128]{2,1,0:T(8,128)(2,1)S(1)} %shard_map.144.v0), channel_id=1, source_target_pairs={{0,48},{8,56},{16,0},{24,8},{32,16},{40,24},{48,32},{56,40},{64,11... | collective-permute-start | bytes 393224 | tf_op jit(solution)/shard_map/ppermute | solution.py:399
  60.3 14.7 %all-to-all-start.2 = ((f32[8,1,128]{2,1,0:T(1,128)}), f32[8,1,128]{2,1,0:T(1,128)S(1)}, u32[]{:S(2)}, u32[]{:S(2)}) async-start(f32[8,1,128]{2,1,0:T(1,128)} %bitcast.1), calls=%async_computation.2 | async-start | bytes 8192 | tf_op jit(solution)/shard_map/all_to_all | solution.py:417

commit v5 on v4

--- a/solution.py
+++ b/solution.py
@@ -17,7 +17,6 @@
 CH = 16
 DELTA = 0.25
 
-COLS = [[8 * y + 2 * x + e for y in range(4) for e in range(2)] for x in range(4)]
 CORES = [(i, i ^ 1) for i in range(32)]
 
 
@@ -147,17 +146,13 @@
         copy.wait()
 
 
-def query_kernel(own_hbm, other_hbm, q0, q1, q2, q3, own_ref, other_ref, sems):
-    copies = load([(own_hbm, own_ref), (other_hbm, other_ref)], sems)
-    _, head, _, core = place()
-    swap = core == 1
-    for copy in copies:
-        copy.wait()
+def query_kernel(own_hbm, q0, q1, q2, q3, own_ref, sems):
+    copies = load([(own_hbm, own_ref)], sems)
+    head = place()[1]
+    copies[0].wait()
     for d, q_ref in enumerate((q0, q1, q2, q3)):
         cols = pl.ds(pl.multiple_of(lax.rem(head + d, 4) * HD, HD), HD)
-        own, other = own_ref[:, cols], other_ref[:, cols]
-        q_ref[0] = jnp.where(swap, other, own)
-        q_ref[1] = jnp.where(swap, own, other)
+        q_ref[...] = own_ref[:, cols]
 
 
 def taps_kernel(
@@ -221,87 +216,87 @@
 
 
 def weights_kernel(valid_ref, *refs):
-    q_refs, (own_ref, other_ref, w_ref, total_ref, qs, keys, scores) = refs[:4], refs[4:]
+    q_refs, (own_ref, other_ref, w_ref, inverse_ref, qs, keys, scores) = refs[:4], refs[4:]
     _, head, k, core = place()
-    valid = valid_ref[0]
+    last = valid_ref[0] - 1
     swap = core == 1
     for d in range(4):
-        qs[d] = q_refs[d][...].reshape(2 * G, HD)
+        row = pl.multiple_of(lax.rem(head + 4 - d, 4) * G, G)
+        qs[pl.ds(row, G), :] = q_refs[d][...]
     for s in range(NB):
         own, other = own_ref[s, 0:64], other_ref[s, 0:64]
         keys[s * G : s * G + 64] = jnp.where(swap, other, own)
         keys[s * G + 64 : (s + 1) * G] = jnp.where(swap, own, other)
+    for m in range(16):
+        low = m // 4 * G
+        s = lax.dot_general(
+            qs[low:, :], keys[m * 2 * G : (m + 1) * 2 * G], NT, preferred_element_type=F32
+        )
+        scores[low:, m * 2 * G : (m + 1) * 2 * G] = s
     factor = math.log2(math.e) / math.sqrt(HD)
-    row = lax.broadcasted_iota(jnp.int32, (2 * G, G), 0)
-    lane = lax.broadcasted_iota(jnp.int32, (2 * G, G), 1)
+    row = lax.broadcasted_iota(jnp.int32, (G, G), 0)
+    lane = lax.broadcasted_iota(jnp.int32, (G, G), 1)
     for t in range(4):
-        q = qs[lax.rem(head + 4 - t, 4)]
-        limit = jnp.minimum(row + (8 * t + 2 * k) * G, valid - 1)
-        top = None
-        for m in range(4 * t + 4):
-            s = lax.dot_general(
-                q, keys[m * 2 * G : (m + 1) * 2 * G], NT, preferred_element_type=F32
-            )
-            for u in range(2):
-                n = 2 * m + u
-                part = s[:, u * G : (u + 1) * G]
-                if n >= 8 * t:
-                    part = jnp.where(lane + n * G <= limit, part, -1e30)
-                scores[:, n * G : (n + 1) * G] = part
-                top = part if top is None else jnp.maximum(top, part)
+        rows = slice(t * G, (t + 1) * G)
+        limit = jnp.minimum(row + (8 * t + 2 * k + core) * G, last)
+
+        def part(n):
+            block = scores[rows, n * G : (n + 1) * G]
+            return jnp.where(lane + n * G <= limit, block, -1e30) if n >= 8 * t else block
+
+        top = part(0)
+        for n in range(1, 8 * t + 8):
+            top = jnp.maximum(top, part(n))
         top = jnp.max(top, axis=1, keepdims=True)
         total = None
         for n in range(8 * t + 8):
-            part = jnp.exp2((scores[:, n * G : (n + 1) * G] - top) * factor)
-            w_ref[2 * t * G : (2 * t + 2) * G, n * G : (n + 1) * G] = part.astype(BF)
-            total = part if total is None else total + part
+            w = jnp.exp2((part(n) - top) * factor)
+            w_ref[rows, n * G : (n + 1) * G] = w.astype(BF)
+            total = w if total is None else total + w
         total = jnp.sum(total, axis=1, keepdims=True)
-        total_ref[2 * t * G : (2 * t + 2) * G, :] = jnp.broadcast_to(total, (2 * G, G))
-
-
-def values_kernel(w_ref, total_ref, v0, v1, v2, v3, msg_ref, vals):
-    _, _, k, core = place()
-    for d, v_ref in enumerate((v0, v1, v2, v3)):
-        row = pl.multiple_of(lax.rem(k + 4 - d, 4) * CH, CH)
+        inverse_ref[rows, :] = jnp.broadcast_to(1.0 / total, (G, G))
+
+
+def values_kernel(w_ref, inverse_ref, *refs):
+    v_refs, out_refs, (vals, acc) = refs[:8], refs[8:12], refs[12:]
+    _, head, k, core = place()
+    for d, v_ref in enumerate(v_refs):
+        side = core if d < 4 else 1 - core
+        row = pl.multiple_of(side * 64 + lax.rem(k + 4 - d % 4, 4) * CH, CH)
         for s in range(NB):
-            block = v_ref[s]
-            vals[pl.ds(row, CH), s * G : (s + 1) * G] = block
-            vals[pl.ds(row + 64, CH), s * G : (s + 1) * G] = block
-    lane = lax.broadcasted_iota(jnp.int32, (64, G), 1)
-    mine = (lane < 64) != (core == 1)
+            vals[pl.ds(row, CH), s * G : (s + 1) * G] = v_ref[s]
     for t in range(4):
-        n = (8 * t + 8) * G
-        rows = slice(2 * t * G, (2 * t + 2) * G)
-        out = lax.dot_general(w_ref[rows, 0:n], vals[:, 0:n], NT, preferred_element_type=F32)
-        out = out / total_ref[rows, :]
-        for c in range(2):
-            j = 2 * t + c
-            a = out[c * G : c * G + 64]
-            b = out[c * G + 64 : (c + 1) * G]
-            msg_ref[j, 0:64, :] = jnp.where(mine, a, b).astype(BF)
-            col = pl.multiple_of((8 * t + 2 * k + c) * G, G)
-            msg_ref[j, 64:128, :] = vals[0:64, pl.ds(col, G)]
-
-
-def gather_kernel(msg_ref, attended_ref, sum_ref):
-    left = lax.broadcasted_iota(jnp.int32, (64, G), 1) < 64
+        span = slice(8 * t * G, (8 * t + 8) * G)
+        part = lax.dot_general(w_ref[t * G :, span], vals[:, span], NT, preferred_element_type=F32)
+        if t == 0:
+            acc[...] = part
+        else:
+            acc[t * G :, :] += part
+    for d in range(4):
+        t = lax.rem(head + d, 4)
+        rows = pl.ds(pl.multiple_of(t * G, G), G)
+        out_refs[d][0:G] = (acc[rows, :] * inverse_ref[rows, :]).astype(BF)
+        col = pl.multiple_of((8 * t + 2 * k + core) * G, G)
+        out_refs[d][G : 2 * G] = vals[:, pl.ds(col, G)]
+
+
+def gather_kernel(a0, a1, a2, a3, attended_ref, sum_ref):
+    head = place()[1]
     sums = jnp.zeros((G, G), F32)
-    for h in range(4):
-        p0 = msg_ref[2 * h, 0:64, :].astype(F32)
-        p1 = msg_ref[2 * h + 1, 0:64, :].astype(F32)
-        low = jnp.where(left, p0, p1)
-        high = pltpu.roll(jnp.where(left, p1, p0), 64, 1)
-        both = jnp.concatenate([low, high], axis=0)
-        attended_ref[:, h * HD : (h + 1) * HD] = both.astype(BF)
-        sums += both * both
+    for d, a_ref in enumerate((a0, a1, a2, a3)):
+        cols = pl.ds(pl.multiple_of(lax.rem(head + 4 - d, 4) * HD, HD), HD)
+        block = a_ref[0:G]
+        attended_ref[:, cols] = block
+        sums += block.astype(F32) * block.astype(F32)
     sum_ref[...] = jnp.broadcast_to(jnp.sum(sums.T, axis=0, keepdims=True), (8, G))
 
 
-def hyena_kernel(msg_ref, hyena_ref):
+def hyena_kernel(h0, h1, h2, h3, hyena_ref):
     eye = identity()
-    for h in range(4):
-        block = msg_ref[2 * h : 2 * h + 2, 64:128, :].reshape(G, G)
-        hyena_ref[:, h * HD : (h + 1) * HD] = flip(eye, block)
+    head = place()[1]
+    for d, h_ref in enumerate((h0, h1, h2, h3)):
+        cols = pl.ds(pl.multiple_of(lax.rem(head + 4 - d, 4) * HD, HD), HD)
+        hyena_ref[:, cols] = flip(eye, h_ref[G : 2 * G])
 
 
 def final_kernel(valid_ref, attended_ref, sum_ref, attn_ref):
@@ -354,7 +349,6 @@
     high, low, high_t, low_t, twiddle = (jnp.asarray(t) for t in tables())
 
     block = pltpu.VMEM((G, 4 * HD), BF)
-    other_queries = lax.ppermute(queries, "ctx", CORES)
     msg = call(
         pre_kernel,
         sds((NB, 96, G), BF),
@@ -366,11 +360,11 @@
     got = lax.all_to_all(msg, "ctx", 0, 0, tiled=True)
     q = call(
         query_kernel,
-        (sds((2, G, HD), BF),) * 4,
-        [HB, AN],
-        [block, block, dma(2)],
+        (sds((G, HD), BF),) * 4,
+        [HB],
+        [block, dma(1)],
         vmem=QV,
-    )(queries, other_queries)
+    )(queries)
     q = [q[0]] + [lax.ppermute(q[d], "ctx", along_y(d)) for d in (1, 2, 3)]
     spec = call(
         taps_kernel,
@@ -398,24 +392,26 @@
     far = lax.ppermute(values, "ctx", along_x(2))
     near = [lax.ppermute(values, "ctx", along_x(d)) for d in (1, 3)]
     v = [values, near[0], far, near[1]]
-    weights, totals = call(
+    v += [lax.ppermute(x, "ctx", CORES) for x in v]
+    weights, inverses = call(
         weights_kernel,
-        (sds((8 * G, SEQ), BF), sds((8 * G, G), F32)),
+        (sds((4 * G, SEQ), BF), sds((4 * G, G), F32)),
         [SM] + [VM] * 6,
-        [pltpu.VMEM((4, 2 * G, HD), BF), pltpu.VMEM((SEQ, HD), BF), pltpu.VMEM((2 * G, SEQ), F32)],
-        us=4,
+        [pltpu.VMEM((4 * G, HD), BF), pltpu.VMEM((SEQ, HD), BF), pltpu.VMEM((4 * G, SEQ), F32)],
+        us=2,
     )(valid_length, *q, got, got_other)
-    back = call(
+    blocks = call(
         values_kernel,
-        sds((8, G, G), BF),
-        [VM] * 6,
-        [pltpu.VMEM((G, SEQ), BF)],
-        us=4,
-    )(weights, totals, *v)
-    got_back = lax.all_to_all(back, "ctx", 0, 0, tiled=True, axis_index_groups=COLS)
-    attended, sums = call(gather_kernel, (sds((G, 4 * HD), BF), sds((8, G), F32)), [VM])(got_back)
+        (sds((2 * G, G), BF),) * 4,
+        [VM] * 10,
+        [pltpu.VMEM((G, SEQ), BF), pltpu.VMEM((4 * G, G), F32)],
+        us=1,
+    )(weights, inverses, *v)
+    back = [blocks[0]] + [lax.ppermute(blocks[d], "ctx", along_y(d)) for d in (2, 1, 3)]
+    back = [back[0], back[2], back[1], back[3]]
+    attended, sums = call(gather_kernel, (sds((G, 4 * HD), BF), sds((8, G), F32)), [VM] * 4)(*back)
     sums = lax.all_to_all(sums, "tp", 0, 0, tiled=True)
-    hyena_out = call(hyena_kernel, sds((G, 4 * HD), BF), [VM])(got_back)
+    hyena_out = call(hyena_kernel, sds((G, 4 * HD), BF), [VM] * 4)(*back)
     attn_out = call(final_kernel, sds((G, 4 * HD), BF), [SM, VM, VM])(valid_length, attended, sums)
     return hyena_out, attn_out
 

time: 77.1 us -> 78.6 us (1.019)
  the two profiles are of different devices: /device:TPU:1 before, /device:TPU:2 now
where the time goes in v5:
time: 78.6 us; the launch traced here: 78.3 us
  waiting for transfers between devices  24.9 us (32%)
  blocking collectives  20.9 us (27%)
  starting transfers between devices  18.9 us (24%)
  Pallas kernels  12.1 us (15%)
  between operations  1.47 us (2%)
    all_to_all x1, blocking collectives, shards(): got = lax.all_to_all(msg, 'ctx', 0, 0, tiled=True)  20.9 us
    ppermute x3, waiting for transfers between devices, shards(): q = [q[0]] + [lax.ppermute(q[d], 'ctx', along_y(d)) for d in (1, 2, 3)]  13.8 us
    all_to_all x1, starting transfers between devices, shards(): sums = lax.all_to_all(sums, 'tp', 0, 0, tiled=True)  8.47 us
    all_to_all x1, waiting for transfers between devices, shards(): sums = lax.all_to_all(sums, 'tp', 0, 0, tiled=True)  6.78 us
    ppermute x3, waiting for transfers between devices, shards(): lax.ppermute(blocks[d], 'ctx', along_y(d))  4.22 us
    ppermute x3, starting transfers between devices, shards(): lax.ppermute(blocks[d], 'ctx', along_y(d))  3.31 us
    ppermute x1, starting transfers between devices, shards(): far = lax.ppermute(values, 'ctx', along_x(2))  2.91 us
    pallas_call x1, Pallas kernels, shards(): call(taps_kernel, sds((NB * CH, 2 * G), F32), [HB] + [AN] * 3, [pltpu.VME...  2.34 us
  transfers between devices with their start and end apart: 15, of which 6 were waited for; matrix products, arithmetic and copies ran while one was open for 0% of the time, Pallas kernels for 9%

profile of v5, /device:TPU:2, one launch (start us, length us, event | category | flops | bytes accessed | tf_op | source)
XLA Modules:
  0.0 78.3 jit_solution(267040122556782786)
XLA Ops:
  0.6 0.0 copy-start.2
  0.6 0.0 copy-start.3
  0.7 0.0 copy-start.6
  0.7 2.3 %shard_map.141 = bf16[32,96,128]{2,1,0:T(8,128)(2,1)} custom-call(bf16[128,512]{1,0:T(8,128)(2,1)} %key_hbm.1, bf16[128,512]{1,0:T(8,128)(2,1)} %value_hbm.1, bf16[128,512]{1,0:T(8,128)(2,1)} %gate_hbm.1, bf16[128,512]{1,0:T(8,128)(2,1)} %attn_hbm.1), custom_call_target="tpu_custom_call" | custom-call | flops 1000000000 | bytes 2000000 | tf_op jit(solution)/shard_map/pallas_call | solution.py:352
  3.0 0.0 copy-start.1
  3.0 0.0 copy-start.4
  3.0 0.0 copy-start.5
  3.0 20.9 %all_to_all.16.refs_4_.in_ref = bf16[32,96,128]{2,1,0:T(8,128)(2,1)S(1)} all-to-all(bf16[32,96,128]{2,1,0:T(8,128)(2,1)} %shard_map.141), channel_id=1, replica_groups=mesh['ctx'=32,'tp'=8] {'ctx'}, dimensions={0} | all-to-all | bytes 1572864 | tf_op jit(solution)/shard_map/all_to_all | solution.py:360
  24.0 0.4 collective-permute-start.3
  25.0 0.0 copy-done.2
  25.0 0.0 copy-done.3
  25.0 0.0 copy-done.6
  25.0 2.3 %shard_map.143.spec_ref = f32[512,256]{1,0:T(8,128)S(1)} custom-call(bf16[4096,512]{1,0:T(8,128)(2,1)} %taps_hbm.1, f32[2,32,128]{2,1,0:T(8,128)S(1)} %copy-done.6, bf16[256,256]{1,0:T(8,128)(2,1)S(1)} %copy-done.2, bf16[256,256]{1,0:T(8,128)(2,1)S(1)} %copy-done.3), custom_call_target="tpu_custom_call" | custom-call | flops 2000000000 | bytes 4000000 | tf_op jit(solution)/shard_map/pallas_call | solution.py:369
  27.4 0.0 copy-done.1
  27.4 0.0 copy-done.4
  27.4 0.0 copy-done.5
  27.4 0.0 copy-start
  27.4 1.9 %shard_map.144.refs_0_ = bf16[32,16,128]{2,1,0:T(8,128)(2,1)S(1)} custom-call(s32[1]{0:T(128)S(6)} %copy.16.valid_ref, bf16[32,96,128]{2,1,0:T(8,128)(2,1)S(1)} %all_to_all.16.refs_4_.in_ref, f32[512,256]{1,0:T(8,128)S(1)} %shard_map.143.spec_ref, f32[512]{0:T(512)S(1)} %copy-done.1, f32[2,32,128]{2,1,0:T(8,128)S(1)} %copy-done.6, ...), custom_call_target="tpu_custom_call" | custom-call | flops 3000000000 | bytes 6000000 | tf_op jit(solution)/shard_map/pallas_call | solution.py:385
  29.3 1.3 %collective-permute-start.6 = (bf16[32,16,128]{2,1,0:T(8,128)(2,1)S(1)}, bf16[32,16,128]{2,1,0:T(8,128)(2,1)S(1)}, u32[]{:S(2)}, u32[]{:S(2)}) collective-permute-start(bf16[32,16,128]{2,1,0:T(8,128)(2,1)S(1)} %shard_map.144.refs_0_), channel_id=1, source_target_pairs={{0,48},{8,56},{16,0},{24,8},{32,16},{40,24},{48,32},{56,40},{64,11... | collective-permute-start | bytes 393224 | tf_op jit(solution)/shard_map/ppermute | solution.py:393
  30.6 0.8 %collective-permute-start.4 = (bf16[32,16,128]{2,1,0:T(8,128)(2,1)S(1)}, bf16[32,16,128]{2,1,0:T(8,128)(2,1)S(1)}, u32[]{:S(2)}, u32[]{:S(2)}) collective-permute-start(bf16[32,16,128]{2,1,0:T(8,128)(2,1)S(1)} %shard_map.144.refs_0_), channel_id=1, source_target_pairs={{0,16},{8,24},{16,32},{24,40},{32,48},{40,56},{48,0},{56,8},{64,80... | collective-permute-start | bytes 393224 | tf_op jit(solution)/shard_map/ppermute | solution.py:393
  31.4 2.9 %collective-permute-start.5 = (bf16[32,16,128]{2,1,0:T(8,128)(2,1)S(1)}, bf16[32,16,128]{2,1,0:T(8,128)(2,1)S(1)}, u32[]{:S(2)}, u32[]{:S(2)}) collective-permute-start(bf16[32,16,128]{2,1,0:T(8,128)(2,1)S(1)} %shard_map.144.refs_0_), channel_id=1, source_target_pairs={{0,32},{8,40},{16,48},{24,56},{32,0},{40,8},{48,16},{56,24},{64,96... | collective-permute-start | bytes 393224 | tf_op jit(solution)/shard_map/ppermute | solution.py:392
  34.3 0.0 copy-done
  34.3 0.2 shard_map.140
  34.5 0.7 collective-permute-start
  35.2 4.5 %collective-permute-done.refs_1_ = bf16[128,128]{1,0:T(8,128)(2,1)S(1)} collective-permute-done((bf16[128,128]{1,0:T(8,128)(2,1)S(1)}, bf16[128,128]{1,0:T(8,128)(2,1)S(1)}, u32[]{:S(2)}, u32[]{:S(2)}) %collective-permute-start) | collective-permute-done | bytes 32800 | tf_op jit(solution)/shard_map/ppermute | solution.py:368
  39.7 0.0 collective-permute-start.1
  39.7 5.4 %collective-permute-done.1.refs_2_ = bf16[128,128]{1,0:T(8,128)(2,1)S(1)} collective-permute-done((bf16[128,128]{1,0:T(8,128)(2,1)S(1)}, bf16[128,128]{1,0:T(8,128)(2,1)S(1)}, u32[]{:S(2)}, u32[]{:S(2)}) %collective-permute-start.1) | collective-permute-done | bytes 32800 | tf_op jit(solution)/shard_map/ppermute | solution.py:368
  45.2 0.0 collective-permute-start.2
  45.2 3.9 %collective-permute-done.2.refs_3_ = bf16[128,128]{1,0:T(8,128)(2,1)S(1)} collective-permute-done((bf16[128,128]{1,0:T(8,128)(2,1)S(1)}, bf16[128,128]{1,0:T(8,128)(2,1)S(1)}, u32[]{:S(2)}, u32[]{:S(2)}) %collective-permute-start.2) | collective-permute-done | bytes 32800 | tf_op jit(solution)/shard_map/ppermute | solution.py:368
  49.1 0.0 collective-permute-start.7
  49.1 0.0 collective-permute-done.6.refs_3_
  49.1 0.5 collective-permute-start.10
  49.6 0.0 collective-permute-done.4.refs_1_
  49.6 0.1 collective-permute-start.8
  49.7 0.0 collective-permute-done.5.refs_2_
  49.7 0.4 collective-permute-start.9
  50.1 0.0 collective-permute-done.3.refs_5_
  50.1 2.0 %shard_map.142 = (bf16[512,4096]{1,0:T(8,128)(2,1)S(1)}, f32[512,128]{1,0:T(8,128)S(1)}) custom-call(s32[1]{0:T(128)S(6)} %copy.16.valid_ref, bf16[128,128]{1,0:T(8,128)(2,1)S(1)} %get-tuple-element.14.refs_0_, bf16[128,128]{1,0:T(8,128)(2,1)S(1)} %collective-permute-done.refs_1_, bf16[128,128]{1,0:T(8,128)(2,1)S(1)} %collective-permute-done.1.refs_2_, ...), custom_call_target="tpu_custom_call" | custom-call | flops 2000000000 | bytes 4000000 | tf_op jit(solution)/shard_map/pallas_call | solution.py:396
  52.1 0.0 collective-permute-done.7.refs_4_
  52.1 0.0 collective-permute-done.10.refs_7_
  52.1 0.0 collective-permute-done.8.refs_5_
  52.1 0.0 collective-permute-done.9.refs_6_
  52.1 1.1 %shard_map.145 = (bf16[256,128]{1,0:T(8,128)(2,1)S(1)}, bf16[256,128]{1,0:T(8,128)(2,1)S(1)}, bf16[256,128]{1,0:T(8,128)(2,1)S(1)}, bf16[256,128]{1,0:T(8,128)(2,1)S(1)}) custom-call(bf16[512,4096]{1,0:T(8,128)(2,1)S(1)} %get-tuple-element.18.w_ref, f32[512,128]{1,0:T(8,128)S(1)} %get-tuple-element.19.inverse_ref, ...), custom_call_target="tpu_custom_call" | custom-call | flops 1000000000 | bytes 2000000 | tf_op jit(solution)/shard_map/pallas_call | solution.py:403
  53.2 0.1 collective-permute-start.11
  53.3 2.7 %collective-permute-start.12 = (bf16[256,128]{1,0:T(8,128)(2,1)S(1)}, bf16[256,128]{1,0:T(8,128)(2,1)S(1)}, u32[]{:S(2)}, u32[]{:S(2)}) collective-permute-start(bf16[256,128]{1,0:T(8,128)(2,1)S(1)} %get-tuple-element.22), channel_id=1, source_target_pairs={{0,128},{8,136},{16,144},{24,152},{32,160},{40,168},{48,176},{56,1... | collective-permute-start | bytes 196616 | tf_op jit(solution)/shard_map/ppermute | solution.py:410
  56.0 0.6 collective-permute-start.13
  56.5 3.6 %collective-permute-done.11.h1.a1 = bf16[256,128]{1,0:T(8,128)(2,1)S(1)} collective-permute-done((bf16[256,128]{1,0:T(8,128)(2,1)S(1)}, bf16[256,128]{1,0:T(8,128)(2,1)S(1)}, u32[]{:S(2)}, u32[]{:S(2)}) %collective-permute-start.11) | collective-permute-done | bytes 65568 | tf_op jit(solution)/shard_map/ppermute | solution.py:410
  60.2 0.0 collective-permute-done.12.h2.a2
  60.2 0.6 collective-permute-done.13.h3.a3
  60.7 0.7 shard_map.147
  61.5 8.5 %all-to-all-start.1 = ((f32[8,1,128]{2,1,0:T(1,128)}), f32[8,1,128]{2,1,0:T(1,128)S(1)}, u32[]{:S(2)}, u32[]{:S(2)}) async-start(f32[8,1,128]{2,1,0:T(1,128)} %bitcast.1), calls=%async_computation.1 | async-start | bytes 8192 | tf_op jit(solution)/shard_map/all_to_all | solution.py:413
  69.9 0.9 %shard_map.146 = bf16[128,512]{1,0:T(8,128)(2,1)} custom-call(bf16[256,128]{1,0:T(8,128)(2,1)S(1)} %get-tuple-element.20.h0.a0, bf16[256,128]{1,0:T(8,128)(2,1)S(1)} %collective-permute-done.11.h1.a1, bf16[256,128]{1,0:T(8,128)(2,1)S(1)} %collective-permute-done.12.h2.a2, bf16[256,128]{1,0:T(8,128)(2,1)S(1)} %collective-permute-done.13.h3.a3), custom_call_target="tpu_custom_call" | custom-call | flops 1000000000 | bytes 2000000 | tf_op jit(solution)/shard_map/pallas_call | solution.py:414
  70.8 6.8 %all-to-all-done.1 = f32[8,1,128]{2,1,0:T(1,128)S(1)} async-done(((f32[8,1,128]{2,1,0:T(1,128)}), f32[8,1,128]{2,1,0:T(1,128)S(1)}, u32[]{:S(2)}, u32[]{:S(2)}) %all-to-all-start.1) | async-done | bytes 4128 | tf_op jit(solution)/shard_map/all_to_all | solution.py:413
  77.6 0.8 shard_map.148
Async XLA Ops:
  0.6 24.4 %copy-start.2 = (bf16[256,256]{1,0:T(8,128)(2,1)S(1)}, bf16[256,256]{1,0:T(8,128)(2,1)}, u32[]{:S(2)}) copy-start(bf16[256,256]{1,0:T(8,128)(2,1)} %constant.10.clone.mh_hbm.mh_ref) | copy-start | bytes 393220
  0.6 24.4 %copy-start.3 = (bf16[256,256]{1,0:T(8,128)(2,1)S(1)}, bf16[256,256]{1,0:T(8,128)(2,1)}, u32[]{:S(2)}) copy-start(bf16[256,256]{1,0:T(8,128)(2,1)} %constant.11.clone.ml_hbm.ml_ref) | copy-start | bytes 393220
  0.7 24.4 %copy-start.6 = (f32[2,32,128]{2,1,0:T(8,128)S(1)}, f32[2,32,128]{2,1,0:T(8,128)}, u32[]{:S(2)}) copy-start(f32[2,32,128]{2,1,0:T(8,128)} %constant.14.clone.tw_hbm.tw_ref) | copy-start | bytes 98308
  3.0 24.4 %copy-start.1 = (f32[512]{0:T(512)S(1)}, f32[512]{0:T(512)}, u32[]{:S(2)}) copy-start(f32[512]{0:T(512)} %skip_ref.1) | copy-start | bytes 6148
  3.0 24.4 %copy-start.4 = (bf16[256,256]{1,0:T(8,128)(2,1)S(1)}, bf16[256,256]{1,0:T(8,128)(2,1)}, u32[]{:S(2)}) copy-start(bf16[256,256]{1,0:T(8,128)(2,1)} %constant.12.clone.nh_ref) | copy-start | bytes 393220
  3.0 24.4 %copy-start.5 = (bf16[256,256]{1,0:T(8,128)(2,1)S(1)}, bf16[256,256]{1,0:T(8,128)(2,1)}, u32[]{:S(2)}) copy-start(bf16[256,256]{1,0:T(8,128)(2,1)} %constant.13.clone.nl_ref) | copy-start | bytes 393220
  24.0 26.1 %collective-permute-start.3 = (bf16[32,96,128]{2,1,0:T(8,128)(2,1)S(1)}, bf16[32,96,128]{2,1,0:T(8,128)(2,1)S(1)}, u32[]{:S(2)}, u32[]{:S(2)}) collective-permute-start(bf16[32,96,128]{2,1,0:T(8,128)(2,1)S(1)} %all_to_all.16.refs_4_.in_ref), channel_id=1, source_target_pairs={{0,8},{8,0},{16,24},{24,16},{32,40},{40,32},{48,56},{56,48},{64,72... | collective-permute-start | bytes 2359304 | tf_op jit(solution)/shard_map/ppermute | solution.py:384
  27.4 6.9 %copy-start = (bf16[128,512]{1,0:T(8,128)(2,1)S(1)}, bf16[128,512]{1,0:T(8,128)(2,1)}, u32[]{:S(2)}) copy-start(bf16[128,512]{1,0:T(8,128)(2,1)} %own_hbm.1) | copy-start | bytes 393220
  29.3 19.8 %collective-permute-start.6 = (bf16[32,16,128]{2,1,0:T(8,128)(2,1)S(1)}, bf16[32,16,128]{2,1,0:T(8,128)(2,1)S(1)}, u32[]{:S(2)}, u32[]{:S(2)}) collective-permute-start(bf16[32,16,128]{2,1,0:T(8,128)(2,1)S(1)} %shard_map.144.refs_0_), channel_id=1, source_target_pairs={{0,48},{8,56},{16,0},{24,8},{32,16},{40,24},{48,32},{56,40},{64,11... | collective-permute-start | bytes 393224 | tf_op jit(solution)/shard_map/ppermute | solution.py:393
  30.6 19.0 %collective-permute-start.4 = (bf16[32,16,128]{2,1,0:T(8,128)(2,1)S(1)}, bf16[32,16,128]{2,1,0:T(8,128)(2,1)S(1)}, u32[]{:S(2)}, u32[]{:S(2)}) collective-permute-start(bf16[32,16,128]{2,1,0:T(8,128)(2,1)S(1)} %shard_map.144.refs_0_), channel_id=1, source_target_pairs={{0,16},{8,24},{16,32},{24,40},{32,48},{40,56},{48,0},{56,8},{64,80... | collective-permute-start | bytes 393224 | tf_op jit(solution)/shard_map/ppermute | solution.py:393
  31.4 18.3 %collective-permute-start.5 = (bf16[32,16,128]{2,1,0:T(8,128)(2,1)S(1)}, bf16[32,16,128]{2,1,0:T(8,128)(2,1)S(1)}, u32[]{:S(2)}, u32[]{:S(2)}) collective-permute-start(bf16[32,16,128]{2,1,0:T(8,128)(2,1)S(1)} %shard_map.144.refs_0_), channel_id=1, source_target_pairs={{0,32},{8,40},{16,48},{24,56},{32,0},{40,8},{48,16},{56,24},{64,96... | collective-permute-start | bytes 393224 | tf_op jit(solution)/shard_map/ppermute | solution.py:392
  34.5 5.2 %collective-permute-start = (bf16[128,128]{1,0:T(8,128)(2,1)S(1)}, bf16[128,128]{1,0:T(8,128)(2,1)S(1)}, u32[]{:S(2)}, u32[]{:S(2)}) collective-permute-start(bf16[128,128]{1,0:T(8,128)(2,1)S(1)} %get-tuple-element.15), channel_id=1, source_target_pairs={{0,64},{8,72},{16,80},{24,88},{32,96},{40,104},{48,112},{56,120},{... | collective-permute-start | bytes 98312 | tf_op jit(solution)/shard_map/ppermute | solution.py:368
  39.7 5.4 %collective-permute-start.1 = (bf16[128,128]{1,0:T(8,128)(2,1)S(1)}, bf16[128,128]{1,0:T(8,128)(2,1)S(1)}, u32[]{:S(2)}, u32[]{:S(2)}) collective-permute-start(bf16[128,128]{1,0:T(8,128)(2,1)S(1)} %get-tuple-element.16), channel_id=1, source_target_pairs={{0,128},{8,136},{16,144},{24,152},{32,160},{40,168},{48,176},{56,1... | collective-permute-start | bytes 98312 | tf_op jit(solution)/shard_map/ppermute | solution.py:368
  45.2 3.9 %collective-permute-start.2 = (bf16[128,128]{1,0:T(8,128)(2,1)S(1)}, bf16[128,128]{1,0:T(8,128)(2,1)S(1)}, u32[]{:S(2)}, u32[]{:S(2)}) collective-permute-start(bf16[128,128]{1,0:T(8,128)(2,1)S(1)} %get-tuple-element.17), channel_id=1, source_target_pairs={{0,192},{8,200},{16,208},{24,216},{32,224},{40,232},{48,240},{56,2... | collective-permute-start | bytes 98312 | tf_op jit(solution)/shard_map/ppermute | solution.py:368
  49.1 3.0 %collective-permute-start.7 = (bf16[32,16,128]{2,1,0:T(8,128)(2,1)S(1)}, bf16[32,16,128]{2,1,0:T(8,128)(2,1)S(1)}, u32[]{:S(2)}, u32[]{:S(2)}) collective-permute-start(bf16[32,16,128]{2,1,0:T(8,128)(2,1)S(1)} %shard_map.144.refs_0_), channel_id=1, source_target_pairs={{0,8},{8,0},{16,24},{24,16},{32,40},{40,32},{48,56},{56,48},{64,72... | collective-permute-start | bytes 393224 | tf_op jit(solution)/shard_map/ppermute | solution.py:395
  49.1 3.0 %collective-permute-start.10 = (bf16[32,16,128]{2,1,0:T(8,128)(2,1)S(1)}, bf16[32,16,128]{2,1,0:T(8,128)(2,1)S(1)}, u32[]{:S(2)}, u32[]{:S(2)}) collective-permute-start(bf16[32,16,128]{2,1,0:T(8,128)(2,1)S(1)} %collective-permute-done.6.refs_3_), channel_id=1, source_target_pairs={{0,8},{8,0},{16,24},{24,16},{32,40},{40,32},{48,56},{56,48},{64,72... | collective-permute-start | bytes 393224 | tf_op jit(solution)/shard_map/ppermute | solution.py:395
  49.6 2.5 %collective-permute-start.8 = (bf16[32,16,128]{2,1,0:T(8,128)(2,1)S(1)}, bf16[32,16,128]{2,1,0:T(8,128)(2,1)S(1)}, u32[]{:S(2)}, u32[]{:S(2)}) collective-permute-start(bf16[32,16,128]{2,1,0:T(8,128)(2,1)S(1)} %collective-permute-done.4.refs_1_), channel_id=1, source_target_pairs={{0,8},{8,0},{16,24},{24,16},{32,40},{40,32},{48,56},{56,48},{64,72... | collective-permute-start | bytes 393224 | tf_op jit(solution)/shard_map/ppermute | solution.py:395
  49.7 2.4 %collective-permute-start.9 = (bf16[32,16,128]{2,1,0:T(8,128)(2,1)S(1)}, bf16[32,16,128]{2,1,0:T(8,128)(2,1)S(1)}, u32[]{:S(2)}, u32[]{:S(2)}) collective-permute-start(bf16[32,16,128]{2,1,0:T(8,128)(2,1)S(1)} %collective-permute-done.5.refs_2_), channel_id=1, source_target_pairs={{0,8},{8,0},{16,24},{24,16},{32,40},{40,32},{48,56},{56,48},{64,72... | collective-permute-start | bytes 393224 | tf_op jit(solution)/shard_map/ppermute | solution.py:395
  53.2 7.0 %collective-permute-start.11 = (bf16[256,128]{1,0:T(8,128)(2,1)S(1)}, bf16[256,128]{1,0:T(8,128)(2,1)S(1)}, u32[]{:S(2)}, u32[]{:S(2)}) collective-permute-start(bf16[256,128]{1,0:T(8,128)(2,1)S(1)} %get-tuple-element.21), channel_id=1, source_target_pairs={{0,64},{8,72},{16,80},{24,88},{32,96},{40,104},{48,112},{56,120},{... | collective-permute-start | bytes 196616 | tf_op jit(solution)/shard_map/ppermute | solution.py:410
  53.3 6.9 %collective-permute-start.12 = (bf16[256,128]{1,0:T(8,128)(2,1)S(1)}, bf16[256,128]{1,0:T(8,128)(2,1)S(1)}, u32[]{:S(2)}, u32[]{:S(2)}) collective-permute-start(bf16[256,128]{1,0:T(8,128)(2,1)S(1)} %get-tuple-element.22), channel_id=1, source_target_pairs={{0,128},{8,136},{16,144},{24,152},{32,160},{40,168},{48,176},{56,1... | collective-permute-start | bytes 196616 | tf_op jit(solution)/shard_map/ppermute | solution.py:410
  56.0 4.8 %collective-permute-start.13 = (bf16[256,128]{1,0:T(8,128)(2,1)S(1)}, bf16[256,128]{1,0:T(8,128)(2,1)S(1)}, u32[]{:S(2)}, u32[]{:S(2)}) collective-permute-start(bf16[256,128]{1,0:T(8,128)(2,1)S(1)} %get-tuple-element.23), channel_id=1, source_target_pairs={{0,192},{8,200},{16,208},{24,216},{32,224},{40,232},{48,240},{56,2... | collective-permute-start | bytes 196616 | tf_op jit(solution)/shard_map/ppermute | solution.py:410
  61.5 16.1 %all-to-all-start.1 = ((f32[8,1,128]{2,1,0:T(1,128)}), f32[8,1,128]{2,1,0:T(1,128)S(1)}, u32[]{:S(2)}, u32[]{:S(2)}) async-start(f32[8,1,128]{2,1,0:T(1,128)} %bitcast.1), calls=%async_computation.1 | async-start | bytes 8192 | tf_op jit(solution)/shard_map/all_to_all | solution.py:413

commit v6 on v5

--- a/solution.py
+++ b/solution.py
@@ -121,9 +121,9 @@
     return jnp.where(row == lane, 1.0, 0.0).astype(BF)
 
 
-def pre_kernel(key_hbm, value_hbm, gate_hbm, attn_hbm, msg_hbm, key, value, gate, attn, msg, sems, done):
+def pre_kernel(key_hbm, value_hbm, gate_hbm, msg_hbm, key, value, gate, msg, sems, done):
     copies = load(
-        [(key_hbm, key), (value_hbm, value), (gate_hbm, gate), (attn_hbm, attn)], sems
+        [(key_hbm, key), (value_hbm, value), (gate_hbm, gate)], sems
     )
     eye = identity()
     for copy in copies:
@@ -137,22 +137,21 @@
             for k in range(4):
                 e = 8 * h + 2 * k + c
                 rows = slice(c * 64 + k * CH, c * 64 + (k + 1) * CH)
-                msg[e, 0:64, :] = attn[c * 64 : (c + 1) * 64, cols]
-                msg[e, 64:80, :] = mixed[rows]
-                msg[e, 80:96, :] = gated[rows]
+                msg[e, 0:16, :] = mixed[rows]
+                msg[e, 16:32, :] = gated[rows]
         part = pl.ds(8 * h, 8)
         out += load([(msg.at[part], msg_hbm.at[part])], done.at[pl.ds(h, 1)])
     for copy in out:
         copy.wait()
 
 
-def query_kernel(own_hbm, q0, q1, q2, q3, own_ref, sems):
-    copies = load([(own_hbm, own_ref)], sems)
-    head = place()[1]
-    copies[0].wait()
-    for d, q_ref in enumerate((q0, q1, q2, q3)):
+def pack_kernel(q_ref, k0, k1, k2, k3, o0, o1, o2, o3):
+    _, head, k, _ = place()
+    for d, out in enumerate((o0, o1, o2, o3)):
         cols = pl.ds(pl.multiple_of(lax.rem(head + d, 4) * HD, HD), HD)
-        q_ref[...] = own_ref[:, cols]
+        out[4] = q_ref[:, cols]
+        for x, keys in enumerate((k0, k1, k2, k3)):
+            out[lax.rem(k + 4 - x, 4)] = keys[:, cols]
 
 
 def taps_kernel(
@@ -191,7 +190,7 @@
 ):
     valid = valid_ref[0]
     _, head, k, core = place()
-    blocks = [in_ref[i, 64:80, :].astype(F32) for i in range(NB)]
+    blocks = [in_ref[i, 0:16, :].astype(F32) for i in range(NB)]
     x = spectrum(blocks, tw_ref, mh_ref, ml_ref, buf)
     xr, xi, hr, hi = x[:, :G], x[:, G:], spec_ref[:, :G], spec_ref[:, G:]
     buf[:, :G] = xr * hr - xi * hi
@@ -211,22 +210,22 @@
     for i, (re, im) in enumerate(z):
         ang = 2.0 * math.pi * DELTA * i / NB
         y = (re * math.cos(ang) - im * math.sin(ang)) * (1.0 / SEQ)
-        y = in_ref[i, 80:96, :].astype(F32) * (y + skip * in_ref[i, 64:80, :].astype(F32))
+        y = in_ref[i, 16:32, :].astype(F32) * (y + skip * in_ref[i, 0:16, :].astype(F32))
         out_ref[i] = jnp.where(lane + i * G < valid, y, 0.0).astype(BF)
 
 
 def weights_kernel(valid_ref, *refs):
-    q_refs, (own_ref, other_ref, w_ref, inverse_ref, qs, keys, scores) = refs[:4], refs[4:]
+    own_refs, other_refs, (w_ref, inverse_ref, qs, keys, scores) = refs[:4], refs[4:8], refs[8:]
     _, head, k, core = place()
     last = valid_ref[0] - 1
-    swap = core == 1
     for d in range(4):
-        row = pl.multiple_of(lax.rem(head + 4 - d, 4) * G, G)
-        qs[pl.ds(row, G), :] = q_refs[d][...]
-    for s in range(NB):
-        own, other = own_ref[s, 0:64], other_ref[s, 0:64]
-        keys[s * G : s * G + 64] = jnp.where(swap, other, own)
-        keys[s * G + 64 : (s + 1) * G] = jnp.where(swap, own, other)
+        y = lax.rem(head + 4 - d, 4)
+        qs[pl.ds(pl.multiple_of(y * G, G), G), :] = own_refs[d][4]
+        for x in range(4):
+            own = pl.multiple_of((8 * y + 2 * x + core) * G, G)
+            other = pl.multiple_of((8 * y + 2 * x + 1 - core) * G, G)
+            keys[pl.ds(own, G), :] = own_refs[d][x]
+            keys[pl.ds(other, G), :] = other_refs[d][x]
     for m in range(16):
         low = m // 4 * G
         s = lax.dot_general(
@@ -349,23 +348,19 @@
     high, low, high_t, low_t, twiddle = (jnp.asarray(t) for t in tables())
 
     block = pltpu.VMEM((G, 4 * HD), BF)
+    spread = [attn_keys]
+    spread += [lax.ppermute(attn_keys, "ctx", along_x(d)) for d in (1, 2, 3)]
     msg = call(
         pre_kernel,
-        sds((NB, 96, G), BF),
-        [HB] * 4,
-        [block] * 4 + [pltpu.VMEM((NB, 96, G), BF), dma(4), dma(4)],
+        sds((NB, 2 * CH, G), BF),
+        [HB] * 3,
+        [block] * 3 + [pltpu.VMEM((NB, 2 * CH, G), BF), dma(3), dma(4)],
         out_specs=HB,
         vmem=60,
-    )(hyena_key, hyena_value, hyena_gate, attn_keys)
+    )(hyena_key, hyena_value, hyena_gate)
     got = lax.all_to_all(msg, "ctx", 0, 0, tiled=True)
-    q = call(
-        query_kernel,
-        (sds((G, HD), BF),) * 4,
-        [HB],
-        [block, dma(1)],
-        vmem=QV,
-    )(queries)
-    q = [q[0]] + [lax.ppermute(q[d], "ctx", along_y(d)) for d in (1, 2, 3)]
+    packs = call(pack_kernel, (sds((5, G, HD), BF),) * 4, [VM] * 5, vmem=QV)(queries, *spread)
+    packs = [packs[0]] + [lax.ppermute(packs[d], "ctx", along_y(d)) for d in (1, 2, 3)]
     spec = call(
         taps_kernel,
         sds((NB * CH, 2 * G), F32),
@@ -381,7 +376,7 @@
         us=2,
         vmem=50,
     )(filter_taps, twiddle, high, low)
-    got_other = lax.ppermute(got, "ctx", CORES)
+    others = [lax.ppermute(x, "ctx", CORES) for x in packs]
     values = call(
         conv_kernel,
         sds((NB, CH, G), BF),
@@ -396,10 +391,10 @@
     weights, inverses = call(
         weights_kernel,
         (sds((4 * G, SEQ), BF), sds((4 * G, G), F32)),
-        [SM] + [VM] * 6,
+        [SM] + [VM] * 8,
         [pltpu.VMEM((4 * G, HD), BF), pltpu.VMEM((SEQ, HD), BF), pltpu.VMEM((4 * G, SEQ), F32)],
         us=2,
-    )(valid_length, *q, got, got_other)
+    )(valid_length, *packs, *others)
     blocks = call(
         values_kernel,
         (sds((2 * G, G), BF),) * 4,
@@ -407,8 +402,9 @@
         [pltpu.VMEM((G, SEQ), BF), pltpu.VMEM((4 * G, G), F32)],
         us=1,
     )(weights, inverses, *v)
-    back = [blocks[0]] + [lax.ppermute(blocks[d], "ctx", along_y(d)) for d in (2, 1, 3)]
-    back = [back[0], back[2], back[1], back[3]]
+    back_far = lax.ppermute(blocks[2], "ctx", along_y(2))
+    back_near = [lax.ppermute(blocks[d], "ctx", along_y(d)) for d in (1, 3)]
+    back = [blocks[0], back_near[0], back_far, back_near[1]]
     attended, sums = call(gather_kernel, (sds((G, 4 * HD), BF), sds((8, G), F32)), [VM] * 4)(*back)
     sums = lax.all_to_all(sums, "tp", 0, 0, tiled=True)
     hyena_out = call(hyena_kernel, sds((G, 4 * HD), BF), [VM] * 4)(*back)

time: 78.6 us -> 68.9 us (0.88)
  blocking collectives: 20.9 us -> 0 us
  starting transfers between devices: 18.9 us -> 36.9 us
  waiting for transfers between devices: 24.9 us -> 18.4 us
    all_to_all x1 -> x0, blocking collectives: 20.9 us -> none  [shards(): got = lax.all_to_all(msg, 'ctx', 0, 0, tiled=True)]
    ppermute x7 -> x13, waiting for transfers between devices: 18.1 us -> 5.38 us  [the longest x3 2.61 us: shards(): lax.ppermute(packs[d], 'ctx', along_y(d))]
    ppermute x7 -> x13, starting transfers between devices: 4.38 us -> 16.5 us  [the longest x3 5.68 us: shards(): lax.ppermute(packs[d], 'ctx', along_y(d))]
    all_to_all x0 -> x1, starting transfers between devices: none -> 6.23 us  [shards(): got = lax.all_to_all(msg, 'ctx', 0, 0, tiled=True)]
    ppermute x1, waiting for transfers between devices: 0.01 us -> 4.36 us  [shards(): far = lax.ppermute(values, 'ctx', along_x(2))]
    ppermute x2, waiting for transfers between devices: 0.01 us -> 1.91 us  [shards(): near = [lax.ppermute(values, 'ctx', along_x(d)) for d in (1, 3)]]
    ppermute x2, starting transfers between devices: 2.1 us -> 3 us  [shards(): near = [lax.ppermute(values, 'ctx', along_x(d)) for d in (1, 3)]]
    ppermute x1, starting transfers between devices: 2.91 us -> 2.08 us  [shards(): far = lax.ppermute(values, 'ctx', along_x(2))]
  transfers between devices with their start and end apart: 15 -> 22, of which waited for: 6 -> 7; matrix products, arithmetic and copies ran while one was open for 0% -> 0% of each run, Pallas kernels for 9% -> 13%
where the time goes in v6:
time: 68.9 us; the launch traced here: 68.7 us
  starting transfers between devices  36.9 us (54%)
  waiting for transfers between devices  18.4 us (27%)
  Pallas kernels  11.8 us (17%)
  between operations  1.51 us (2%)
    all_to_all x1, starting transfers between devices, shards(): sums = lax.all_to_all(sums, 'tp', 0, 0, tiled=True)  8.46 us
    all_to_all x1, waiting for transfers between devices, shards(): sums = lax.all_to_all(sums, 'tp', 0, 0, tiled=True)  6.77 us
    all_to_all x1, starting transfers between devices, shards(): got = lax.all_to_all(msg, 'ctx', 0, 0, tiled=True)  6.23 us
    ppermute x3, starting transfers between devices, shards(): lax.ppermute(packs[d], 'ctx', along_y(d))  5.68 us
    ppermute x3, starting transfers between devices, shards(): spread += [lax.ppermute(attn_keys, 'ctx', along_x(d)) for d in (1, 2, 3)]  4.83 us
    ppermute x1, waiting for transfers between devices, shards(): far = lax.ppermute(values, 'ctx', along_x(2))  4.36 us
    ppermute x2, starting transfers between devices, shards(): near = [lax.ppermute(values, 'ctx', along_x(d)) for d in (1, 3)]  3 us
    ppermute x2, starting transfers between devices, shards(): back_near = [lax.ppermute(blocks[d], 'ctx', along_y(d)) for d in (1, 3)]  2.84 us
  transfers between devices with their start and end apart: 22, of which 7 were waited for; matrix products, arithmetic and copies ran while one was open for 0% of the time, Pallas kernels for 13%

profile of v6, /device:TPU:2, one launch (start us, length us, event | category | flops | bytes accessed | tf_op | source)
XLA Modules:
  0.0 68.7 jit_solution(10449629068540354948)
XLA Ops:
  0.6 0.0 copy-start.3
  0.6 0.0 copy-start.4
  0.7 0.0 copy-start.7
  0.7 1.6 %collective-permute-start = (bf16[128,512]{1,0:T(8,128)(2,1)}, bf16[128,512]{1,0:T(8,128)(2,1)S(1)}, u32[]{:S(2)}, u32[]{:S(2)}) collective-permute-start(bf16[128,512]{1,0:T(8,128)(2,1)} %k0.1), channel_id=1, source_target_pairs={{0,16},{8,24},{16,32},{24,40},{32,48},{40,56},{48,0},{56,8},{64,80... | collective-permute-start | bytes 393224 | tf_op jit(solution)/shard_map/ppermute | solution.py:352
  2.2 2.8 %collective-permute-start.1 = (bf16[128,512]{1,0:T(8,128)(2,1)}, bf16[128,512]{1,0:T(8,128)(2,1)S(1)}, u32[]{:S(2)}, u32[]{:S(2)}) collective-permute-start(bf16[128,512]{1,0:T(8,128)(2,1)} %k0.1), channel_id=1, source_target_pairs={{0,32},{8,40},{16,48},{24,56},{32,0},{40,8},{48,16},{56,24},{64,96... | collective-permute-start | bytes 393224 | tf_op jit(solution)/shard_map/ppermute | solution.py:352
  5.1 0.4 collective-permute-start.2
  5.5 2.0 %shard_map.142 = bf16[32,32,128]{2,1,0:T(8,128)(2,1)} custom-call(bf16[128,512]{1,0:T(8,128)(2,1)} %key_hbm.1, bf16[128,512]{1,0:T(8,128)(2,1)} %value_hbm.1, bf16[128,512]{1,0:T(8,128)(2,1)} %gate_hbm.1), custom_call_target="tpu_custom_call" | custom-call | flops 1000000000 | bytes 2000000 | tf_op jit(solution)/shard_map/pallas_call | solution.py:353
  7.5 0.0 copy-start
  7.5 0.0 copy-start.1
  7.6 6.2 %all-to-all-start = ((bf16[32,32,128]{2,1,0:T(8,128)(2,1)}), bf16[32,32,128]{2,1,0:T(8,128)(2,1)S(1)}, u32[]{:S(2)}, u32[]{:S(2)}) async-start(bf16[32,32,128]{2,1,0:T(8,128)(2,1)} %shard_map.142), calls=%async_computation | async-start | bytes 524288 | tf_op jit(solution)/shard_map/all_to_all | solution.py:361
  14.5 0.0 copy-start.2
  14.5 0.0 copy-start.5
  14.5 0.0 copy-start.6
  14.5 2.4 %shard_map.143.spec_ref = f32[512,256]{1,0:T(8,128)S(1)} custom-call(bf16[4096,512]{1,0:T(8,128)(2,1)} %taps_hbm.1, f32[2,32,128]{2,1,0:T(8,128)S(1)} %copy-done.7, bf16[256,256]{1,0:T(8,128)(2,1)S(1)} %copy-done.3, bf16[256,256]{1,0:T(8,128)(2,1)S(1)} %copy-done.4), custom_call_target="tpu_custom_call" | custom-call | flops 2000000000 | bytes 4000000 | tf_op jit(solution)/shard_map/pallas_call | solution.py:364
  16.9 0.0 collective-permute-done.k1
  16.9 0.0 collective-permute-done.1.k2
  16.9 0.0 collective-permute-done.2.k3
  17.0 0.1 shard_map.140
  17.1 1.5 %collective-permute-start.3 = (bf16[5,128,128]{2,1,0:T(8,128)(2,1)S(1)}, bf16[5,128,128]{2,1,0:T(8,128)(2,1)S(1)}, u32[]{:S(2)}, u32[]{:S(2)}) collective-permute-start(bf16[5,128,128]{2,1,0:T(8,128)(2,1)S(1)} %get-tuple-element.15), channel_id=1, source_target_pairs={{0,64},{8,72},{16,80},{24,88},{32,96},{40,104},{48,112},{56,120},{... | collective-permute-start | bytes 491528 | tf_op jit(solution)/shard_map/ppermute | solution.py:363
  18.6 2.7 %collective-permute-start.4 = (bf16[5,128,128]{2,1,0:T(8,128)(2,1)S(1)}, bf16[5,128,128]{2,1,0:T(8,128)(2,1)S(1)}, u32[]{:S(2)}, u32[]{:S(2)}) collective-permute-start(bf16[5,128,128]{2,1,0:T(8,128)(2,1)S(1)} %get-tuple-element.16), channel_id=1, source_target_pairs={{0,128},{8,136},{16,144},{24,152},{32,160},{40,168},{48,176},{56,1... | collective-permute-start | bytes 491528 | tf_op jit(solution)/shard_map/ppermute | solution.py:363
  21.4 1.4 %collective-permute-start.5 = (bf16[5,128,128]{2,1,0:T(8,128)(2,1)S(1)}, bf16[5,128,128]{2,1,0:T(8,128)(2,1)S(1)}, u32[]{:S(2)}, u32[]{:S(2)}) collective-permute-start(bf16[5,128,128]{2,1,0:T(8,128)(2,1)S(1)} %get-tuple-element.17), channel_id=1, source_target_pairs={{0,192},{8,200},{16,208},{24,216},{32,224},{40,232},{48,240},{56,2... | collective-permute-start | bytes 491528 | tf_op jit(solution)/shard_map/ppermute | solution.py:363
  22.8 0.0 collective-permute-start.6
  22.8 0.0 all-to-all-done.in_ref
  22.8 0.0 copy-done.2
  22.8 0.0 copy-done.5
  22.8 0.0 copy-done.6
  22.8 1.9 %shard_map.144.refs_0_ = bf16[32,16,128]{2,1,0:T(8,128)(2,1)S(1)} custom-call(s32[1]{0:T(128)S(6)} %copy.16.valid_ref, bf16[32,32,128]{2,1,0:T(8,128)(2,1)S(1)} %all-to-all-done.in_ref, f32[512,256]{1,0:T(8,128)S(1)} %shard_map.143.spec_ref, f32[512]{0:T(512)S(1)} %copy-done.2, f32[2,32,128]{2,1,0:T(8,128)S(1)} %copy-done.7, bf16[256,256]{1,0:T(8,128)(2,1)S(1)} %copy-done.3, ...), custom_call_target="tpu_custom_call" | custom-call | flops 3000000000 | bytes 6000000 | tf_op jit(solution)/shard_map/pallas_call | solution.py:380
  24.7 1.5 %collective-permute-start.10 = (bf16[32,16,128]{2,1,0:T(8,128)(2,1)S(1)}, bf16[32,16,128]{2,1,0:T(8,128)(2,1)S(1)}, u32[]{:S(2)}, u32[]{:S(2)}) collective-permute-start(bf16[32,16,128]{2,1,0:T(8,128)(2,1)S(1)} %shard_map.144.refs_0_), channel_id=1, source_target_pairs={{0,16},{8,24},{16,32},{24,40},{32,48},{40,56},{48,0},{56,8},{64,80... | collective-permute-start | bytes 393224 | tf_op jit(solution)/shard_map/ppermute | solution.py:388
  26.3 0.0 collective-permute-done.3.refs_1_
  26.3 0.2 collective-permute-start.7
  26.5 2.6 %collective-permute-done.4.refs_2_ = bf16[5,128,128]{2,1,0:T(8,128)(2,1)S(1)} collective-permute-done((bf16[5,128,128]{2,1,0:T(8,128)(2,1)S(1)}, bf16[5,128,128]{2,1,0:T(8,128)(2,1)S(1)}, u32[]{:S(2)}, u32[]{:S(2)}) %collective-permute-start.4) | collective-permute-done | bytes 163872 | tf_op jit(solution)/shard_map/ppermute | solution.py:363
  29.1 0.0 collective-permute-start.8
  29.1 0.0 collective-permute-done.5.refs_3_
  29.1 0.5 collective-permute-start.9
  29.6 0.0 collective-permute-done.6.refs_4_
  29.6 2.1 %collective-permute-start.11 = (bf16[32,16,128]{2,1,0:T(8,128)(2,1)S(1)}, bf16[32,16,128]{2,1,0:T(8,128)(2,1)S(1)}, u32[]{:S(2)}, u32[]{:S(2)}) collective-permute-start(bf16[32,16,128]{2,1,0:T(8,128)(2,1)S(1)} %shard_map.144.refs_0_), channel_id=1, source_target_pairs={{0,32},{8,40},{16,48},{24,56},{32,0},{40,8},{48,16},{56,24},{64,96... | collective-permute-start | bytes 393224 | tf_op jit(solution)/shard_map/ppermute | solution.py:387
  31.7 0.0 collective-permute-done.10.refs_1_
  31.7 1.5 %collective-permute-start.12 = (bf16[32,16,128]{2,1,0:T(8,128)(2,1)S(1)}, bf16[32,16,128]{2,1,0:T(8,128)(2,1)S(1)}, u32[]{:S(2)}, u32[]{:S(2)}) collective-permute-start(bf16[32,16,128]{2,1,0:T(8,128)(2,1)S(1)} %shard_map.144.refs_0_), channel_id=1, source_target_pairs={{0,48},{8,56},{16,0},{24,8},{32,16},{40,24},{48,32},{56,40},{64,11... | collective-permute-start | bytes 393224 | tf_op jit(solution)/shard_map/ppermute | solution.py:388
  33.2 4.4 %collective-permute-done.11.refs_2_ = bf16[32,16,128]{2,1,0:T(8,128)(2,1)S(1)} collective-permute-done((bf16[32,16,128]{2,1,0:T(8,128)(2,1)S(1)}, bf16[32,16,128]{2,1,0:T(8,128)(2,1)S(1)}, u32[]{:S(2)}, u32[]{:S(2)}) %collective-permute-start.11) | collective-permute-done | bytes 131104 | tf_op jit(solution)/shard_map/ppermute | solution.py:387
  37.5 0.0 collective-permute-start.13
  37.5 1.9 %collective-permute-done.12.refs_3_ = bf16[32,16,128]{2,1,0:T(8,128)(2,1)S(1)} collective-permute-done((bf16[32,16,128]{2,1,0:T(8,128)(2,1)S(1)}, bf16[32,16,128]{2,1,0:T(8,128)(2,1)S(1)}, u32[]{:S(2)}, u32[]{:S(2)}) %collective-permute-start.12) | collective-permute-done | bytes 131104 | tf_op jit(solution)/shard_map/ppermute | solution.py:388
  39.4 0.0 collective-permute-start.14
  39.4 0.0 collective-permute-done.7.refs_5_
  39.4 0.5 collective-permute-start.15
  39.9 0.0 collective-permute-done.8.refs_6_
  39.9 0.1 collective-permute-start.16
  40.0 0.0 collective-permute-done.9.refs_7_
  40.0 1.9 %shard_map.141 = (bf16[512,4096]{1,0:T(8,128)(2,1)S(1)}, f32[512,128]{1,0:T(8,128)S(1)}) custom-call(s32[1]{0:T(128)S(6)} %copy.16.valid_ref, bf16[5,128,128]{2,1,0:T(8,128)(2,1)S(1)} %get-tuple-element.14.refs_0_, bf16[5,128,128]{2,1,0:T(8,128)(2,1)S(1)} %collective-permute-done.3.refs_1_, bf16[5,128,128]{2,1,0:T(8,128)(2,1)S(1)} %collective-permute-done.4.refs_2_, ...), custom_call_target="tpu_custom_call" | custom-call | flops 2000000000 | bytes 4000000 | tf_op jit(solution)/shard_map/pallas_call | solution.py:391
  42.0 0.0 collective-permute-done.13.refs_4_
  42.0 0.0 collective-permute-done.14.refs_5_
  42.0 0.0 collective-permute-done.15.refs_6_
  42.0 0.0 collective-permute-done.16.refs_7_
  42.0 1.1 %shard_map.145 = (bf16[256,128]{1,0:T(8,128)(2,1)S(1)}, bf16[256,128]{1,0:T(8,128)(2,1)S(1)}, bf16[256,128]{1,0:T(8,128)(2,1)S(1)}, bf16[256,128]{1,0:T(8,128)(2,1)S(1)}) custom-call(bf16[512,4096]{1,0:T(8,128)(2,1)S(1)} %get-tuple-element.18.w_ref, f32[512,128]{1,0:T(8,128)S(1)} %get-tuple-element.19.inverse_ref, ...), custom_call_target="tpu_custom_call" | custom-call | flops 1000000000 | bytes 2000000 | tf_op jit(solution)/shard_map/pallas_call | solution.py:398
  43.1 1.3 %collective-permute-start.17 = (bf16[256,128]{1,0:T(8,128)(2,1)S(1)}, bf16[256,128]{1,0:T(8,128)(2,1)S(1)}, u32[]{:S(2)}, u32[]{:S(2)}) collective-permute-start(bf16[256,128]{1,0:T(8,128)(2,1)S(1)} %get-tuple-element.21), channel_id=1, source_target_pairs={{0,64},{8,72},{16,80},{24,88},{32,96},{40,104},{48,112},{56,120},{... | collective-permute-start | bytes 196616 | tf_op jit(solution)/shard_map/ppermute | solution.py:406
  44.4 2.4 %collective-permute-start.18 = (bf16[256,128]{1,0:T(8,128)(2,1)S(1)}, bf16[256,128]{1,0:T(8,128)(2,1)S(1)}, u32[]{:S(2)}, u32[]{:S(2)}) collective-permute-start(bf16[256,128]{1,0:T(8,128)(2,1)S(1)} %get-tuple-element.22), channel_id=1, source_target_pairs={{0,128},{8,136},{16,144},{24,152},{32,160},{40,168},{48,176},{56,1... | collective-permute-start | bytes 196616 | tf_op jit(solution)/shard_map/ppermute | solution.py:405
  46.8 1.5 %collective-permute-start.19 = (bf16[256,128]{1,0:T(8,128)(2,1)S(1)}, bf16[256,128]{1,0:T(8,128)(2,1)S(1)}, u32[]{:S(2)}, u32[]{:S(2)}) collective-permute-start(bf16[256,128]{1,0:T(8,128)(2,1)S(1)} %get-tuple-element.23), channel_id=1, source_target_pairs={{0,192},{8,200},{16,208},{24,216},{32,224},{40,232},{48,240},{56,2... | collective-permute-start | bytes 196616 | tf_op jit(solution)/shard_map/ppermute | solution.py:406
  48.3 0.6 collective-permute-done.17.h1.a1
  48.9 1.7 %collective-permute-done.18.h2.a2 = bf16[256,128]{1,0:T(8,128)(2,1)S(1)} collective-permute-done((bf16[256,128]{1,0:T(8,128)(2,1)S(1)}, bf16[256,128]{1,0:T(8,128)(2,1)S(1)}, u32[]{:S(2)}, u32[]{:S(2)}) %collective-permute-start.18) | collective-permute-done | bytes 65568 | tf_op jit(solution)/shard_map/ppermute | solution.py:405
  50.6 0.5 collective-permute-done.19.h3.a3
  51.1 0.7 %shard_map.147 = (bf16[128,512]{1,0:T(8,128)(2,1)S(1)}, f32[8,128]{1,0:T(8,128)}) custom-call(bf16[256,128]{1,0:T(8,128)(2,1)S(1)} %get-tuple-element.20.h0.a0, bf16[256,128]{1,0:T(8,128)(2,1)S(1)} %collective-permute-done.17.h1.a1, bf16[256,128]{1,0:T(8,128)(2,1)S(1)} %collective-permute-done.18.h2.a2, bf16[256,128]{1,0:T(8,128)(2,1)S(1)} %collective-permute-done.19.h3.a3), custom_call_target="tpu_custom_call" | custom-call | flops 1000000000 | bytes 2000000 | tf_op jit(solution)/shard_map/pallas_call | solution.py:408
  51.8 8.5 %all-to-all-start.1 = ((f32[8,1,128]{2,1,0:T(1,128)}), f32[8,1,128]{2,1,0:T(1,128)S(1)}, u32[]{:S(2)}, u32[]{:S(2)}) async-start(f32[8,1,128]{2,1,0:T(1,128)} %bitcast.1), calls=%async_computation.1 | async-start | bytes 8192 | tf_op jit(solution)/shard_map/all_to_all | solution.py:409
  60.2 0.9 %shard_map.146 = bf16[128,512]{1,0:T(8,128)(2,1)} custom-call(bf16[256,128]{1,0:T(8,128)(2,1)S(1)} %get-tuple-element.20.h0.a0, bf16[256,128]{1,0:T(8,128)(2,1)S(1)} %collective-permute-done.17.h1.a1, bf16[256,128]{1,0:T(8,128)(2,1)S(1)} %collective-permute-done.18.h2.a2, bf16[256,128]{1,0:T(8,128)(2,1)S(1)} %collective-permute-done.19.h3.a3), custom_call_target="tpu_custom_call" | custom-call | flops 1000000000 | bytes 2000000 | tf_op jit(solution)/shard_map/pallas_call | solution.py:410
  61.1 6.8 %all-to-all-done.1 = f32[8,1,128]{2,1,0:T(1,128)S(1)} async-done(((f32[8,1,128]{2,1,0:T(1,128)}), f32[8,1,128]{2,1,0:T(1,128)S(1)}, u32[]{:S(2)}, u32[]{:S(2)}) %all-to-all-start.1) | async-done | bytes 4128 | tf_op jit(solution)/shard_map/all_to_all | solution.py:409
  67.9 0.8 %shard_map.148 = bf16[128,512]{1,0:T(8,128)(2,1)} custom-call(s32[1]{0:T(128)S(6)} %copy.16.valid_ref, bf16[128,512]{1,0:T(8,128)(2,1)S(1)} %get-tuple-element.24.attended_ref, f32[8,128]{1,0:T(8,128)S(1)} %bitcast.4), custom_call_target="tpu_custom_call" | custom-call | flops 1000000000 | bytes 2000000 | tf_op jit(solution)/shard_map/pallas_call | solution.py:411
  (5 shorter events, 0.0 us)
Async XLA Ops:
  0.6 13.8 %copy-start.3 = (bf16[256,256]{1,0:T(8,128)(2,1)S(1)}, bf16[256,256]{1,0:T(8,128)(2,1)}, u32[]{:S(2)}) copy-start(bf16[256,256]{1,0:T(8,128)(2,1)} %constant.10.clone.mh_hbm.mh_ref) | copy-start | bytes 393220
  0.6 13.8 %copy-start.4 = (bf16[256,256]{1,0:T(8,128)(2,1)S(1)}, bf16[256,256]{1,0:T(8,128)(2,1)}, u32[]{:S(2)}) copy-start(bf16[256,256]{1,0:T(8,128)(2,1)} %constant.11.clone.ml_hbm.ml_ref) | copy-start | bytes 393220
  0.7 13.8 %copy-start.7 = (f32[2,32,128]{2,1,0:T(8,128)S(1)}, f32[2,32,128]{2,1,0:T(8,128)}, u32[]{:S(2)}) copy-start(f32[2,32,128]{2,1,0:T(8,128)} %constant.14.clone.tw_hbm.tw_ref) | copy-start | bytes 98308
  0.7 16.2 %collective-permute-start = (bf16[128,512]{1,0:T(8,128)(2,1)}, bf16[128,512]{1,0:T(8,128)(2,1)S(1)}, u32[]{:S(2)}, u32[]{:S(2)}) collective-permute-start(bf16[128,512]{1,0:T(8,128)(2,1)} %k0.1), channel_id=1, source_target_pairs={{0,16},{8,24},{16,32},{24,40},{32,48},{40,56},{48,0},{56,8},{64,80... | collective-permute-start | bytes 393224 | tf_op jit(solution)/shard_map/ppermute | solution.py:352
  2.2 14.7 %collective-permute-start.1 = (bf16[128,512]{1,0:T(8,128)(2,1)}, bf16[128,512]{1,0:T(8,128)(2,1)S(1)}, u32[]{:S(2)}, u32[]{:S(2)}) collective-permute-start(bf16[128,512]{1,0:T(8,128)(2,1)} %k0.1), channel_id=1, source_target_pairs={{0,32},{8,40},{16,48},{24,56},{32,0},{40,8},{48,16},{56,24},{64,96... | collective-permute-start | bytes 393224 | tf_op jit(solution)/shard_map/ppermute | solution.py:352
  5.1 11.9 %collective-permute-start.2 = (bf16[128,512]{1,0:T(8,128)(2,1)}, bf16[128,512]{1,0:T(8,128)(2,1)S(1)}, u32[]{:S(2)}, u32[]{:S(2)}) collective-permute-start(bf16[128,512]{1,0:T(8,128)(2,1)} %k0.1), channel_id=1, source_target_pairs={{0,48},{8,56},{16,0},{24,8},{32,16},{40,24},{48,32},{56,40},{64,11... | collective-permute-start | bytes 393224 | tf_op jit(solution)/shard_map/ppermute | solution.py:352
  7.5 9.4 %copy-start = (bf16[128,512]{1,0:T(8,128)(2,1)S(1)}, bf16[128,512]{1,0:T(8,128)(2,1)}, u32[]{:S(2)}) copy-start(bf16[128,512]{1,0:T(8,128)(2,1)} %q_ref.1) | copy-start | bytes 393220
  7.5 9.4 %copy-start.1 = (bf16[128,512]{1,0:T(8,128)(2,1)S(1)}, bf16[128,512]{1,0:T(8,128)(2,1)}, u32[]{:S(2)}) copy-start(bf16[128,512]{1,0:T(8,128)(2,1)} %k0.1) | copy-start | bytes 393220
  7.6 15.2 %all-to-all-start = ((bf16[32,32,128]{2,1,0:T(8,128)(2,1)}), bf16[32,32,128]{2,1,0:T(8,128)(2,1)S(1)}, u32[]{:S(2)}, u32[]{:S(2)}) async-start(bf16[32,32,128]{2,1,0:T(8,128)(2,1)} %shard_map.142), calls=%async_computation | async-start | bytes 524288 | tf_op jit(solution)/shard_map/all_to_all | solution.py:361
  14.5 8.3 %copy-start.2 = (f32[512]{0:T(512)S(1)}, f32[512]{0:T(512)}, u32[]{:S(2)}) copy-start(f32[512]{0:T(512)} %skip_ref.1) | copy-start | bytes 6148
  14.5 8.3 %copy-start.5 = (bf16[256,256]{1,0:T(8,128)(2,1)S(1)}, bf16[256,256]{1,0:T(8,128)(2,1)}, u32[]{:S(2)}) copy-start(bf16[256,256]{1,0:T(8,128)(2,1)} %constant.12.clone.nh_ref) | copy-start | bytes 393220
  14.5 8.3 %copy-start.6 = (bf16[256,256]{1,0:T(8,128)(2,1)S(1)}, bf16[256,256]{1,0:T(8,128)(2,1)}, u32[]{:S(2)}) copy-start(bf16[256,256]{1,0:T(8,128)(2,1)} %constant.13.clone.nl_ref) | copy-start | bytes 393220
  17.1 9.2 %collective-permute-start.3 = (bf16[5,128,128]{2,1,0:T(8,128)(2,1)S(1)}, bf16[5,128,128]{2,1,0:T(8,128)(2,1)S(1)}, u32[]{:S(2)}, u32[]{:S(2)}) collective-permute-start(bf16[5,128,128]{2,1,0:T(8,128)(2,1)S(1)} %get-tuple-element.15), channel_id=1, source_target_pairs={{0,64},{8,72},{16,80},{24,88},{32,96},{40,104},{48,112},{56,120},{... | collective-permute-start | bytes 491528 | tf_op jit(solution)/shard_map/ppermute | solution.py:363
  18.6 10.5 %collective-permute-start.4 = (bf16[5,128,128]{2,1,0:T(8,128)(2,1)S(1)}, bf16[5,128,128]{2,1,0:T(8,128)(2,1)S(1)}, u32[]{:S(2)}, u32[]{:S(2)}) collective-permute-start(bf16[5,128,128]{2,1,0:T(8,128)(2,1)S(1)} %get-tuple-element.16), channel_id=1, source_target_pairs={{0,128},{8,136},{16,144},{24,152},{32,160},{40,168},{48,176},{56,1... | collective-permute-start | bytes 491528 | tf_op jit(solution)/shard_map/ppermute | solution.py:363
  21.4 7.7 %collective-permute-start.5 = (bf16[5,128,128]{2,1,0:T(8,128)(2,1)S(1)}, bf16[5,128,128]{2,1,0:T(8,128)(2,1)S(1)}, u32[]{:S(2)}, u32[]{:S(2)}) collective-permute-start(bf16[5,128,128]{2,1,0:T(8,128)(2,1)S(1)} %get-tuple-element.17), channel_id=1, source_target_pairs={{0,192},{8,200},{16,208},{24,216},{32,224},{40,232},{48,240},{56,2... | collective-permute-start | bytes 491528 | tf_op jit(solution)/shard_map/ppermute | solution.py:363
  22.8 6.8 %collective-permute-start.6 = (bf16[5,128,128]{2,1,0:T(8,128)(2,1)S(1)}, bf16[5,128,128]{2,1,0:T(8,128)(2,1)S(1)}, u32[]{:S(2)}, u32[]{:S(2)}) collective-permute-start(bf16[5,128,128]{2,1,0:T(8,128)(2,1)S(1)} %get-tuple-element.14.refs_0_), channel_id=1, source_target_pairs={{0,8},{8,0},{16,24},{24,16},{32,40},{40,32},{48,56},{56,48},{64,72... | collective-permute-start | bytes 491528 | tf_op jit(solution)/shard_map/ppermute | solution.py:379
  24.7 7.0 %collective-permute-start.10 = (bf16[32,16,128]{2,1,0:T(8,128)(2,1)S(1)}, bf16[32,16,128]{2,1,0:T(8,128)(2,1)S(1)}, u32[]{:S(2)}, u32[]{:S(2)}) collective-permute-start(bf16[32,16,128]{2,1,0:T(8,128)(2,1)S(1)} %shard_map.144.refs_0_), channel_id=1, source_target_pairs={{0,16},{8,24},{16,32},{24,40},{32,48},{40,56},{48,0},{56,8},{64,80... | collective-permute-start | bytes 393224 | tf_op jit(solution)/shard_map/ppermute | solution.py:388
  26.3 13.2 %collective-permute-start.7 = (bf16[5,128,128]{2,1,0:T(8,128)(2,1)S(1)}, bf16[5,128,128]{2,1,0:T(8,128)(2,1)S(1)}, u32[]{:S(2)}, u32[]{:S(2)}) collective-permute-start(bf16[5,128,128]{2,1,0:T(8,128)(2,1)S(1)} %collective-permute-done.3.refs_1_), channel_id=1, source_target_pairs={{0,8},{8,0},{16,24},{24,16},{32,40},{40,32},{48,56},{56,48},{64,72... | collective-permute-start | bytes 491528 | tf_op jit(solution)/shard_map/ppermute | solution.py:379
  29.1 10.8 %collective-permute-start.8 = (bf16[5,128,128]{2,1,0:T(8,128)(2,1)S(1)}, bf16[5,128,128]{2,1,0:T(8,128)(2,1)S(1)}, u32[]{:S(2)}, u32[]{:S(2)}) collective-permute-start(bf16[5,128,128]{2,1,0:T(8,128)(2,1)S(1)} %collective-permute-done.4.refs_2_), channel_id=1, source_target_pairs={{0,8},{8,0},{16,24},{24,16},{32,40},{40,32},{48,56},{56,48},{64,72... | collective-permute-start | bytes 491528 | tf_op jit(solution)/shard_map/ppermute | solution.py:379
  29.1 10.9 %collective-permute-start.9 = (bf16[5,128,128]{2,1,0:T(8,128)(2,1)S(1)}, bf16[5,128,128]{2,1,0:T(8,128)(2,1)S(1)}, u32[]{:S(2)}, u32[]{:S(2)}) collective-permute-start(bf16[5,128,128]{2,1,0:T(8,128)(2,1)S(1)} %collective-permute-done.5.refs_3_), channel_id=1, source_target_pairs={{0,8},{8,0},{16,24},{24,16},{32,40},{40,32},{48,56},{56,48},{64,72... | collective-permute-start | bytes 491528 | tf_op jit(solution)/shard_map/ppermute | solution.py:379
  29.6 7.9 %collective-permute-start.11 = (bf16[32,16,128]{2,1,0:T(8,128)(2,1)S(1)}, bf16[32,16,128]{2,1,0:T(8,128)(2,1)S(1)}, u32[]{:S(2)}, u32[]{:S(2)}) collective-permute-start(bf16[32,16,128]{2,1,0:T(8,128)(2,1)S(1)} %shard_map.144.refs_0_), channel_id=1, source_target_pairs={{0,32},{8,40},{16,48},{24,56},{32,0},{40,8},{48,16},{56,24},{64,96... | collective-permute-start | bytes 393224 | tf_op jit(solution)/shard_map/ppermute | solution.py:387
  31.7 7.7 %collective-permute-start.12 = (bf16[32,16,128]{2,1,0:T(8,128)(2,1)S(1)}, bf16[32,16,128]{2,1,0:T(8,128)(2,1)S(1)}, u32[]{:S(2)}, u32[]{:S(2)}) collective-permute-start(bf16[32,16,128]{2,1,0:T(8,128)(2,1)S(1)} %shard_map.144.refs_0_), channel_id=1, source_target_pairs={{0,48},{8,56},{16,0},{24,8},{32,16},{40,24},{48,32},{56,40},{64,11... | collective-permute-start | bytes 393224 | tf_op jit(solution)/shard_map/ppermute | solution.py:388
  37.5 4.4 %collective-permute-start.13 = (bf16[32,16,128]{2,1,0:T(8,128)(2,1)S(1)}, bf16[32,16,128]{2,1,0:T(8,128)(2,1)S(1)}, u32[]{:S(2)}, u32[]{:S(2)}) collective-permute-start(bf16[32,16,128]{2,1,0:T(8,128)(2,1)S(1)} %shard_map.144.refs_0_), channel_id=1, source_target_pairs={{0,8},{8,0},{16,24},{24,16},{32,40},{40,32},{48,56},{56,48},{64,72... | collective-permute-start | bytes 393224 | tf_op jit(solution)/shard_map/ppermute | solution.py:390
  39.4 2.5 %collective-permute-start.14 = (bf16[32,16,128]{2,1,0:T(8,128)(2,1)S(1)}, bf16[32,16,128]{2,1,0:T(8,128)(2,1)S(1)}, u32[]{:S(2)}, u32[]{:S(2)}) collective-permute-start(bf16[32,16,128]{2,1,0:T(8,128)(2,1)S(1)} %collective-permute-done.10.refs_1_), channel_id=1, source_target_pairs={{0,8},{8,0},{16,24},{24,16},{32,40},{40,32},{48,56},{56,48},{64,72... | collective-permute-start | bytes 393224 | tf_op jit(solution)/shard_map/ppermute | solution.py:390
  39.4 2.5 %collective-permute-start.15 = (bf16[32,16,128]{2,1,0:T(8,128)(2,1)S(1)}, bf16[32,16,128]{2,1,0:T(8,128)(2,1)S(1)}, u32[]{:S(2)}, u32[]{:S(2)}) collective-permute-start(bf16[32,16,128]{2,1,0:T(8,128)(2,1)S(1)} %collective-permute-done.11.refs_2_), channel_id=1, source_target_pairs={{0,8},{8,0},{16,24},{24,16},{32,40},{40,32},{48,56},{56,48},{64,72... | collective-permute-start | bytes 393224 | tf_op jit(solution)/shard_map/ppermute | solution.py:390
  39.9 2.0 %collective-permute-start.16 = (bf16[32,16,128]{2,1,0:T(8,128)(2,1)S(1)}, bf16[32,16,128]{2,1,0:T(8,128)(2,1)S(1)}, u32[]{:S(2)}, u32[]{:S(2)}) collective-permute-start(bf16[32,16,128]{2,1,0:T(8,128)(2,1)S(1)} %collective-permute-done.12.refs_3_), channel_id=1, source_target_pairs={{0,8},{8,0},{16,24},{24,16},{32,40},{40,32},{48,56},{56,48},{64,72... | collective-permute-start | bytes 393224 | tf_op jit(solution)/shard_map/ppermute | solution.py:390
  43.1 5.8 %collective-permute-start.17 = (bf16[256,128]{1,0:T(8,128)(2,1)S(1)}, bf16[256,128]{1,0:T(8,128)(2,1)S(1)}, u32[]{:S(2)}, u32[]{:S(2)}) collective-permute-start(bf16[256,128]{1,0:T(8,128)(2,1)S(1)} %get-tuple-element.21), channel_id=1, source_target_pairs={{0,64},{8,72},{16,80},{24,88},{32,96},{40,104},{48,112},{56,120},{... | collective-permute-start | bytes 196616 | tf_op jit(solution)/shard_map/ppermute | solution.py:406
  44.4 6.2 %collective-permute-start.18 = (bf16[256,128]{1,0:T(8,128)(2,1)S(1)}, bf16[256,128]{1,0:T(8,128)(2,1)S(1)}, u32[]{:S(2)}, u32[]{:S(2)}) collective-permute-start(bf16[256,128]{1,0:T(8,128)(2,1)S(1)} %get-tuple-element.22), channel_id=1, source_target_pairs={{0,128},{8,136},{16,144},{24,152},{32,160},{40,168},{48,176},{56,1... | collective-permute-start | bytes 196616 | tf_op jit(solution)/shard_map/ppermute | solution.py:405
  46.8 4.3 %collective-permute-start.19 = (bf16[256,128]{1,0:T(8,128)(2,1)S(1)}, bf16[256,128]{1,0:T(8,128)(2,1)S(1)}, u32[]{:S(2)}, u32[]{:S(2)}) collective-permute-start(bf16[256,128]{1,0:T(8,128)(2,1)S(1)} %get-tuple-element.23), channel_id=1, source_target_pairs={{0,192},{8,200},{16,208},{24,216},{32,224},{40,232},{48,240},{56,2... | collective-permute-start | bytes 196616 | tf_op jit(solution)/shard_map/ppermute | solution.py:406
  51.8 16.1 %all-to-all-start.1 = ((f32[8,1,128]{2,1,0:T(1,128)}), f32[8,1,128]{2,1,0:T(1,128)S(1)}, u32[]{:S(2)}, u32[]{:S(2)}) async-start(f32[8,1,128]{2,1,0:T(1,128)} %bitcast.1), calls=%async_computation.1 | async-start | bytes 8192 | tf_op jit(solution)/shard_map/all_to_all | solution.py:409
